TPU v7x, 256 devices: a whole 4x4x8 slice. The times are simulated.
256 devices in a mesh: dp: 64 (over z, y, x_hi), mp: 4 (over x_lo, core).
Axes of the slice: x: 4 (x_hi: 2, x_lo: 2; x = x_hi * 2 + x_lo), y: 4, z: 8, core: 2. Of those that a mesh axis runs over, the one named last changes fastest.
Arguments:
- hidden_states: bfloat16 [32768, 3584], P('dp'), may hold values from -6 to 6
- token_ids: int32 [2048, 16], P('dp'), may hold values from 0 to 152063, as said below
- norm_gain: float32 [3584], replicated, may hold values from 0.5 to 1.5
- q_weight: bfloat16 [3584, 3584], P('dp', 'mp'), may hold values from -0.09375 to 0.09375
- key_matrix: bfloat16 [3584, 512], P('dp', 'mp'), may hold values from -0.09375 to 0.09375
- value_matrix: bfloat16 [3584, 512], P('dp', 'mp'), may hold values from -0.09375 to 0.09375
- out_weight: bfloat16 [3584, 3584], P('dp', 'mp'), may hold values from -0.09375 to 0.09375
- label_table: bfloat16 [65536, 3584], P(('dp', 'mp')), may hold values from -6 to 6
- refresh_rows: int32 [2048], P(('dp', 'mp')), may hold values from 0 to 255, as said below
- label_counts: int32 [65536], P(('dp', 'mp')), may hold values from 1 to 8191
- queries: bfloat16 [128, 3584], replicated, may hold values from -6 to 6
- positives: int32 [128, 8], replicated, may hold values from 0 to 65535
Outputs:
- label_grad: float32 [65536, 3584], P(('dp', 'mp'))
- query_grad: float32 [128, 3584], replicated
- loss: float32 [], replicated
Inputs may be any that keep to these rules, and one draw needn't show every extreme that they name: `token_ids`: in every text the first id is not 0, and after an id 0 all later ids of that text are 0. `refresh_rows`: the 8 entries of each aligned block of 8 entries are distinct.
All inputs are finite; a program needn't handle non-finite values.
Results may differ from a plain program's by a relative error of at most 0.003.
Values may be sent and summed in bfloat16 or wider, within the bound.
No kernel may reach another device: no remote copies, remote signals or barrier semaphores. Data moves between devices by JAX's collectives and lax.ppermute only.
A program may use at most 128 MiB of HBM per device.

v0:
```python
import math

import jax
import jax.numpy as jnp
from jax import lax
from jax.sharding import Mesh, PartitionSpec as P

HEAD_WIDTH = 128

rope_theta = 1000000.0
norm_eps = 1e-06
focal_beta = 0.9999

AXES = ("z", "y", "xh", "xl", "c")
SIZES = (8, 4, 2, 2, 2)
DP = ("z", "y", "xh")
MP = ("xl", "c")
RING_X = ("xh", "xl")


def rotary(values, head_size):
    length = values.shape[1]
    half = head_size // 2
    frequency = rope_theta ** (-2.0 * jnp.arange(half, dtype=jnp.float32) / head_size)
    angles = jnp.arange(length, dtype=jnp.float32)[:, None] * frequency[None, :]
    cosine = jnp.concatenate([jnp.cos(angles), jnp.cos(angles)], axis=1)[None, :, None, :]
    sine = jnp.concatenate([jnp.sin(angles), jnp.sin(angles)], axis=1)[None, :, None, :]
    turned = jnp.concatenate([-values[..., half:], values[..., :half]], axis=-1)
    return values * cosine + turned * sine


def attend_pooled(query_rows, key_rows, value_rows, text_ids, head_size):
    texts, length = text_ids.shape
    kv_heads = key_rows.shape[1] // head_size
    repeat = query_rows.shape[1] // head_size // kv_heads
    query_r = query_rows.reshape(texts, length, kv_heads, repeat, head_size)
    key_r = key_rows.reshape(texts, length, kv_heads, head_size)
    value_r = value_rows.reshape(texts, length, kv_heads, head_size)
    scores = jnp.einsum(
        "ntgrd,nsgd->ngrts", query_r, key_r, preferred_element_type=jnp.float32
    ) / math.sqrt(head_size)
    causal = jnp.arange(length)[:, None] >= jnp.arange(length)[None, :]
    live = text_ids != 0
    allowed = causal[None, None, None, :, :] & live[:, None, None, None, :]
    weights = jnp.where(allowed, jnp.exp(scores), 0.0)
    probs = weights / jnp.sum(weights, axis=-1, keepdims=True)
    column = jnp.sum(probs * live.astype(jnp.float32)[:, None, None, :, None], axis=3)
    pooled = jnp.sum(column[..., None] * value_r.transpose(0, 2, 1, 3)[:, :, None], axis=3)
    return pooled.reshape(texts, -1)


def shift(x, axis, size, by):
    return lax.ppermute(x, axis, [(i, (i + by) % size) for i in range(size)])


def swap(x, axis, size, bit):
    return lax.ppermute(x, axis, [(i, i ^ bit) for i in range(size)])


def spread(x, axes, size):
    return lax.all_to_all(jnp.broadcast_to(x[None], (size,) + x.shape), axes, 0, 0, tiled=True)


def focal(margin):
    missed = jax.nn.sigmoid(-margin)
    softened = jax.nn.softplus(-margin)
    return missed * missed * softened, -(missed * missed) * (
        2.0 * jax.nn.sigmoid(margin) * softened + missed
    )


def shards(
    hidden_states,
    token_ids,
    norm_gain,
    q_weight,
    key_matrix,
    value_matrix,
    out_weight,
    label_table,
    refresh_rows,
    label_counts,
    queries,
    positives,
):
    f32, bf16 = jnp.float32, jnp.bfloat16
    width = hidden_states.shape[1]
    group_tokens = hidden_states.shape[0]
    texts, length = token_ids.shape
    xh, core = lax.axis_index("xh"), lax.axis_index("c")
    member = lax.axis_index(MP)
    ndp, nmp = 64, 4
    rows = q_weight.shape[0]

    packed = jnp.concatenate([key_matrix, value_matrix, q_weight, out_weight], axis=1)
    moved = lax.ppermute(
        packed,
        ("xh", "xl", "c"),
        [(4 * h + 2 * l + k, 4 * l + 2 * k + h) for h in (0, 1) for l in (0, 1) for k in (0, 1)],
    )
    cut = packed.shape[1] - out_weight.shape[1]
    in_all = lax.all_gather(moved[:, :cut], ("z", "y"), axis=0, tiled=True)
    out_all = lax.all_gather(moved[:, cut:], ("z", "y"), axis=0, tiled=True)

    balance = (1.0 - focal_beta) / -jnp.expm1(
        label_counts.astype(f32) * math.log(focal_beta)
    )
    owned = label_table.shape[0]
    total = jnp.full((8, 128), jnp.sum(balance))
    for axis, size in zip(AXES[::-1], SIZES[::-1]):
        bit = 1
        while bit < size:
            total = total + swap(total, axis, size, bit)
            bit *= 2
    total_labels = owned * ndp * nmp
    factor = total_labels / total[0, 0]

    root = math.sqrt(width)
    first_label = (lax.axis_index(DP) * nmp + member) * owned
    own_rows = jnp.arange(owned, dtype=jnp.int32)
    chosen = refresh_rows[:, None] == own_rows[None, :]
    kept = ~jnp.any(chosen, axis=0)
    kept_balance = jnp.where(kept, balance, 0.0)
    matched = jnp.any(positives[:, :, None] == (first_label + own_rows)[None, None, :], axis=1)
    signs = jnp.where(matched, 1.0, -1.0)
    logits = (
        lax.dot_general(
            queries, label_table, (((1,), (1,)), ((), ())), preferred_element_type=f32
        )
        / root
    )
    terms, slope = focal(signs * logits)
    kept_loss = jnp.sum(kept_balance[None, :] * terms)
    kept_slopes = (kept_balance[None, :] * signs * slope).astype(bf16)
    kept_query = jnp.dot(kept_slopes, label_table, preferred_element_type=f32)
    new_balance = jnp.sum(jnp.where(chosen, balance[None, :], 0.0), axis=1)
    new_signs = jnp.where(
        jnp.any(positives[:, :, None] == (first_label + refresh_rows)[None, None, :], axis=1),
        1.0,
        -1.0,
    )

    states = hidden_states.astype(f32)
    scaled = lax.rsqrt(jnp.mean(states * states, axis=1, keepdims=True) + norm_eps)
    normed = (states * scaled * norm_gain).astype(bf16)
    live = (token_ids != 0).astype(f32)
    share = texts // nmp
    live_own = lax.dynamic_slice_in_dim(live, member * share, share, 0)
    states_own = lax.dynamic_slice_in_dim(
        hidden_states, member * share * length, share * length, 0
    ).reshape(share, length, width)
    counted = jnp.sum(live_own, axis=1, keepdims=True)
    states_sum = jnp.sum(states_own.astype(f32) * live_own[:, :, None], axis=1)

    half = normed.T.reshape(ndp // 2, 2, rows, group_tokens)
    half = lax.dynamic_index_in_dim(half, core, 1, keepdims=False).reshape(-1, group_tokens)
    facing = [(i, 3 - i) for i in range(4)]
    half_other = lax.ppermute(half, RING_X, facing)
    ids_other = lax.ppermute(token_ids, RING_X, facing)
    keeps = xh == core
    give = jnp.where(keeps, half_other, half)
    keep = jnp.where(keeps, half, half_other)
    ids = jnp.where(keeps, token_ids, ids_other)
    contract = (((0,), (0,)), ((), ()))
    given = lax.dot_general(give, in_all, contract, preferred_element_type=f32)
    taken = shift(given, "c", 2, 1)
    raw = lax.dot_general(keep, in_all, contract, preferred_element_type=f32) + taken
    key_raw, value_raw, query_raw = raw[:, :128], raw[:, 128:256], raw[:, 256:]
    queries_rot = (
        rotary(query_raw.reshape(texts, length, -1, HEAD_WIDTH), HEAD_WIDTH)
        .reshape(group_tokens, -1)
        .astype(bf16)
    )
    rotary_keys = (
        rotary(key_raw.reshape(texts, length, -1, HEAD_WIDTH), HEAD_WIDTH)
        .reshape(group_tokens, -1)
        .astype(bf16)
    )
    pooled = attend_pooled(queries_rot, rotary_keys, value_raw, ids, HEAD_WIDTH).astype(bf16)

    pooled_other = shift(pooled, "c", 2, 1)
    both = jnp.concatenate(
        [jnp.where(core == 0, pooled, pooled_other), jnp.where(core == 0, pooled_other, pooled)],
        axis=0,
    )
    head_terms = lax.dot_general(
        both, out_all, (((1,), (1,)), ((), ())), preferred_element_type=f32
    )
    exchanged = lax.all_to_all(
        head_terms.reshape(8, share, -1), ("xh", "xl", "c"), 0, 0, tiled=True
    )
    summed = jnp.sum(exchanged.reshape(nmp, 2, share, -1), axis=0)
    output_own = (
        summed.reshape(2, share, ndp // 2, rows).transpose(1, 2, 0, 3).reshape(share, width)
    )
    refreshed = ((states_sum + output_own) / counted).astype(bf16)

    new_logits = (
        lax.dot_general(
            queries, refreshed, (((1,), (1,)), ((), ())), preferred_element_type=f32
        )
        / root
    )
    new_terms, new_slope = focal(new_signs * new_logits)
    new_loss = jnp.sum(new_balance[None, :] * new_terms)
    new_slopes = (new_balance[None, :] * new_signs * new_slope).astype(bf16)
    query_part = kept_query + jnp.dot(new_slopes, refreshed, preferred_element_type=f32)
    slopes = kept_slopes + jnp.dot(
        new_slopes, chosen.astype(bf16), preferred_element_type=f32
    ).astype(bf16)
    label_part = lax.dot_general(
        slopes, queries, (((0,), (0,)), ((), ())), preferred_element_type=f32
    )

    batch = queries.shape[0]
    loss_lanes = jnp.full((batch, 128), (kept_loss + new_loss) / batch)
    payload = jnp.concatenate([query_part, loss_lanes], axis=1)
    halves = payload.reshape(2, batch // 2, -1)
    mine = lax.dynamic_index_in_dim(halves, core, 0, keepdims=False)
    theirs = lax.dynamic_index_in_dim(halves, 1 - core, 0, keepdims=False)
    part = mine + shift(theirs, "c", 2, 1)
    part = jnp.sum(
        lax.all_to_all(part.reshape(4, batch // 8, -1), "y", 0, 0, tiled=True), axis=0
    )
    part = jnp.sum(
        lax.all_to_all(part.reshape(4, batch // 32, -1), RING_X, 0, 0, tiled=True), axis=0
    )
    part = jnp.sum(spread(part, "z", 8), axis=0)
    part = spread(part, RING_X, 4).reshape(batch // 8, -1)
    part = spread(part, "y", 4).reshape(batch // 2, -1)
    back = shift(part, "c", 2, 1)
    whole = jnp.concatenate(
        [jnp.where(core == 0, part, back), jnp.where(core == 0, back, part)], axis=0
    )
    scale = factor / root
    loss = factor * jnp.sum(whole[:, width]) / (batch * total_labels)
    return (scale * label_part, scale * whole[:, :width], loss)


def solution(mesh):
    grid = Mesh(mesh.devices.reshape(SIZES), AXES)
    in_specs = (
        P(DP, None),
        P(DP, None),
        P(),
        P(DP, MP),
        P(DP, MP),
        P(DP, MP),
        P(DP, MP),
        P(AXES, None),
        P(AXES),
        P(AXES),
        P(),
        P(),
    )
    out_specs = (P(AXES, None), P(), P())
    return jax.shard_map(shards, mesh=grid, in_specs=in_specs, out_specs=out_specs, check_vma=False)
```

profile of v0, /device:TPU:2, one launch (start us, length us, event | category | flops | bytes accessed | tf_op | source)
XLA Modules:
  0.0 333.4 jit_solution(10685834836395014331)
XLA Ops:
  8.3 3.4 %collective-permute-start.10 = (bf16[56,2048]{1,0:T(8,128)(2,1)S(1)}, bf16[56,2048]{1,0:T(8,128)(2,1)S(1)}, u32[]{:S(2)}, u32[]{:S(2)}) collective-permute-start(bf16[56,2048]{1,0:T(8,128)(2,1)S(1)} %pad_maximum_fusion), channel_id=1, source_target_pairs={{0,0},{1,2},{2,4},{3,6},{4,1},{5,3},{6,5},{7,7},{8,8},{9,10},{10,1... | collective-permute-start | bytes 688136 | tf_op jit(solution)/shard_map/ppermute | solution.py:96
  11.7 3.9 %collective-permute-done.10 = bf16[56,2048]{1,0:T(8,128)(2,1)S(1)} collective-permute-done((bf16[56,2048]{1,0:T(8,128)(2,1)S(1)}, bf16[56,2048]{1,0:T(8,128)(2,1)S(1)}, u32[]{:S(2)}, u32[]{:S(2)}) %collective-permute-start.10) | collective-permute-done | bytes 229408 | tf_op jit(solution)/shard_map/ppermute | solution.py:96
  16.4 5.9 %copy.46 = bf16[512,3584]{0,1:T(8,128)(2,1)} copy(bf16[512,3584]{1,0:T(8,128)(2,1)} %param.12) | data formatting | bytes 7340032 | tf_op args[0]
  31.2 39.4 %collective-permute-done.9 = bf16[1792,512]{1,0:T(8,128)(2,1)} collective-permute-done((bf16[1792,512]{1,0:T(8,128)(2,1)}, bf16[1792,512]{1,0:T(8,128)(2,1)}, u32[]{:S(2)}, u32[]{:S(2)}) %collective-permute-start.9) | collective-permute-done | bytes 1835040 | tf_op jit(solution)/shard_map/ppermute | solution.py:158
  70.6 31.8 %all-gather.3.cloned.1.call-done = bf16[1792,1152]{1,0:T(8,128)(2,1)} async-done(((bf16[56,1152]{1,0:T(8,128)(2,1)}), bf16[1792,1152]{1,0:T(8,128)(2,1)}) %all-gather.3.cloned.1.call-update) | async-done | bytes 4128784 | tf_op jit(solution)/shard_map/all_gather | solution.py:102
  102.4 6.8 %fusion.7 = f32[512,1152]{1,0:T(8,128)} fusion(bf16[1792,1152]{1,0:T(8,128)(2,1)} %all-gather.3.cloned.1.call-done, bf16[1792,512]{1,0:T(8,128)(2,1)} %collective-permute-done.9, bf16[1792,512]{1,0:T(8,128)(2,1)} %bitcast.4, pred[]{:T(512)S(6)} %eq.58), kind=kOutput, calls=%fused_computation.23 | convolution fusion | flops 2114846720 | bytes 10158081 | tf_op jit(solution)/shard_map/dot_general | solution.py:165
  114.8 6.1 %convolution_add_fusion.1 = f32[512,1152]{1,0:T(8,128)S(1)} fusion(f32[512,1152]{1,0:T(8,128)} %collective-permute-done.11, bf16[1792,1152]{1,0:T(8,128)(2,1)} %all-gather.3.cloned.1.call-done, bf16[1792,512]{1,0:T(8,128)(2,1)} %bitcast.4, bf16[1792,512]{1,0:T(8,128)(2,1)} %collective-permute-done.9, pred[]{:T(512)S(6)} %eq.58), kind=kOutput, calls=%fused_computation.7 | convolution fusion | flops 2115436544 | bytes 12517377 | tf_op jit(solution)/shard_map/dot_general | solution.py:167
  125.7 3.1 slice_negate_fusion
  141.1 41.1 %all-gather.5.cloned.1.call-done = bf16[1792,896]{1,0:T(8,128)(2,1)} async-done(((bf16[56,896]{1,0:T(8,128)(2,1)}), bf16[1792,896]{1,0:T(8,128)(2,1)}) %all-gather.5.cloned.1.call-update) | async-done | bytes 3211280 | tf_op jit(solution)/shard_map/all_gather | solution.py:103
  182.3 3.8 %convolution_bitcast_fusion = f32[8,8,1792]{2,1,0:T(8,128)} fusion(bf16[1792,896]{1,0:T(8,128)(2,1)} %all-gather.5.cloned.1.call-done, bf16[32,896]{1,0:T(8,128)(2,1)S(1)} %get-tuple-element.18, bf16[32,896]{1,0:T(8,128)(2,1)S(1)} %get-tuple-element.17), kind=kOutput, calls=%fused_computation.8 | convolution fusion | flops 205750272 | bytes 3784704 | tf_op jit(solution)/shard_map/dot_general | solution.py:186
  186.0 4.8 %all-to-all-start = ((f32[8,8,1792]{2,1,0:T(8,128)}), f32[8,8,1792]{2,1,0:T(8,128)S(1)}, u32[]{:S(2)}, u32[]{:S(2)}) async-start(f32[8,8,1792]{2,1,0:T(8,128)} %convolution_bitcast_fusion), calls=%async_computation | async-start | bytes 917504 | tf_op jit(solution)/shard_map/all_to_all | solution.py:189
  192.8 6.2 %all-to-all-done = f32[8,8,1792]{2,1,0:T(8,128)S(1)} async-done(((f32[8,8,1792]{2,1,0:T(8,128)}), f32[8,8,1792]{2,1,0:T(8,128)S(1)}, u32[]{:S(2)}, u32[]{:S(2)}) %all-to-all-start) | async-done | bytes 458784 | tf_op jit(solution)/shard_map/all_to_all | solution.py:189
  203.3 3.2 convolution_add_fusion
  212.3 17.0 %all_to_all.30 = f32[4,16,3712]{2,1,0:T(8,128)S(1)} all-to-all(f32[4,16,3712]{2,1,0:T(8,128)S(1)} %bitcast.79), channel_id=1, replica_groups=mesh['z'=8,'y'=4,'xh'=2,'xl'=2,'c'=2] {'y'}, dimensions={0} | all-to-all | bytes 1900544 | tf_op jit(solution)/shard_map/all_to_all | solution.py:223
  229.4 8.9 %all_to_all.31 = f32[4,4,3712]{2,1,0:T(4,128)S(1)} all-to-all(f32[4,4,3712]{2,1,0:T(4,128)S(1)} %reshape.179), channel_id=1, replica_groups=mesh['z'=8,'y'=4,'xh'=2,'xl'=2,'c'=2] {'xh','xl'}, dimensions={0} | all-to-all | bytes 475136 | tf_op jit(solution)/shard_map/all_to_all | solution.py:226
  238.5 18.4 %all_to_all.32 = f32[8,4,3712]{2,1,0:T(4,128)S(1)} all-to-all(f32[8,4,3712]{2,1,0:T(4,128)S(1)} %broadcast_in_dim.64), channel_id=1, replica_groups=mesh['z'=8,'y'=4,'xh'=2,'xl'=2,'c'=2] {'z'}, dimensions={0} | all-to-all | bytes 950272 | tf_op jit(solution)/shard_map/all_to_all | solution.py:61
  257.0 8.9 %all_to_all.33 = f32[4,4,3712]{2,1,0:T(4,128)S(1)} all-to-all(f32[4,4,3712]{2,1,0:T(4,128)S(1)} %broadcast_in_dim.65), channel_id=1, replica_groups=mesh['z'=8,'y'=4,'xh'=2,'xl'=2,'c'=2] {'xh','xl'}, dimensions={0} | all-to-all | bytes 475136 | tf_op jit(solution)/shard_map/all_to_all | solution.py:61
  266.1 12.8 %all_to_all.34 = f32[4,16,3712]{2,1,0:T(8,128)S(1)} all-to-all(f32[4,16,3712]{2,1,0:T(8,128)S(1)} %broadcast_in_dim.67), channel_id=1, replica_groups=mesh['z'=8,'y'=4,'xh'=2,'xl'=2,'c'=2] {'y'}, dimensions={0} | all-to-all | bytes 1900544 | tf_op jit(solution)/shard_map/all_to_all | solution.py:61
  288.1 3.7 %collective-permute-done.2 = f32[8,128]{1,0:T(8,128)S(1)} collective-permute-done((f32[8,128]{1,0:T(8,128)S(1)}, f32[8,128]{1,0:T(8,128)S(1)}, u32[]{:S(2)}, u32[]{:S(2)}) %collective-permute-start.2) | collective-permute-done | bytes 4128 | tf_op jit(solution)/shard_map/ppermute | solution.py:57
  296.4 4.0 %collective-permute-done.4 = f32[8,128]{1,0:T(8,128)S(1)} collective-permute-done((f32[8,128]{1,0:T(8,128)S(1)}, f32[8,128]{1,0:T(8,128)S(1)}, u32[]{:S(2)}, u32[]{:S(2)}) %collective-permute-start.4) | collective-permute-done | bytes 4128 | tf_op jit(solution)/shard_map/ppermute | solution.py:57
  301.0 3.0 collective-permute-done.5
  304.4 4.2 %collective-permute-done.6 = f32[8,128]{1,0:T(8,128)S(1)} collective-permute-done((f32[8,128]{1,0:T(8,128)S(1)}, f32[8,128]{1,0:T(8,128)S(1)}, u32[]{:S(2)}, u32[]{:S(2)}) %collective-permute-start.6) | collective-permute-done | bytes 4128 | tf_op jit(solution)/shard_map/ppermute | solution.py:57
  309.8 6.4 %collective-permute-done.7 = f32[8,128]{1,0:T(8,128)S(1)} collective-permute-done((f32[8,128]{1,0:T(8,128)S(1)}, f32[8,128]{1,0:T(8,128)S(1)}, u32[]{:S(2)}, u32[]{:S(2)}) %collective-permute-start.7) | collective-permute-done | bytes 4128 | tf_op jit(solution)/shard_map/ppermute | solution.py:57
  317.3 4.0 %convolution_multiply_fusion = f32[256,3584]{1,0:T(8,128)} fusion(bf16[128,3584]{1,0:T(8,128)(2,1)} %param.22, f32[]{:T(128)S(6)} %div.91, s32[8]{0:T(128)S(1)} %copy-done.11, pred[128,8]{0,1:T(8,128)(4,1)S(1)} %compare_reduce_fusion.1, f32[128,8]{0,1:T(8,128)S(1)} %get-tuple-element.26, f32[8]{0:T(128)S(1)} %select_reduce_fusion, ...), kind=kOutput, calls=%fused_computation.5 | convolution fusion | flops 237198336 | bytes 4757572 | tf_op jit(solution)/shard_map/dot_general | solution.py:211
  (126 shorter events, 64.3 us)
Async XLA Ops:
  7.2 105.2 %copy-start = (bf16[256,3584]{1,0:T(8,128)(2,1)S(1)}, bf16[256,3584]{1,0:T(8,128)(2,1)}, u32[]{:S(2)}) copy-start(bf16[256,3584]{1,0:T(8,128)(2,1)} %param.19) | copy-start | bytes 5505028
  7.2 95.2 %all-gather.3.cloned.1.call-start = ((), (), s32[]{:S(2)}) async-start(), calls=%async_computation.6 | async-start | bytes 4257792 | tf_op jit(solution)/shard_map/all_gather | solution.py:102
  8.3 7.3 %collective-permute-start.10 = (bf16[56,2048]{1,0:T(8,128)(2,1)S(1)}, bf16[56,2048]{1,0:T(8,128)(2,1)S(1)}, u32[]{:S(2)}, u32[]{:S(2)}) collective-permute-start(bf16[56,2048]{1,0:T(8,128)(2,1)S(1)} %pad_maximum_fusion), channel_id=1, source_target_pairs={{0,0},{1,2},{2,4},{3,6},{4,1},{5,3},{6,5},{7,7},{8,8},{9,10},{10,1... | collective-permute-start | bytes 688136 | tf_op jit(solution)/shard_map/ppermute | solution.py:96
  16.3 165.9 %all-gather.5.cloned.1.call-start = ((), (), s32[]{:S(2)}) async-start(), calls=%async_computation.7 | async-start | bytes 3311616 | tf_op jit(solution)/shard_map/all_gather | solution.py:103
  28.4 42.2 %collective-permute-start.9 = (bf16[1792,512]{1,0:T(8,128)(2,1)}, bf16[1792,512]{1,0:T(8,128)(2,1)}, u32[]{:S(2)}, u32[]{:S(2)}) collective-permute-start(bf16[1792,512]{1,0:T(8,128)(2,1)} %bitcast.4), channel_id=1, source_target_pairs={{0,6},{2,4},{4,2},{6,0},{1,7},{3,5},{5,3},{7,1},{8,14},{10,12},{12... | collective-permute-start | bytes 5505032 | tf_op jit(solution)/shard_map/ppermute | solution.py:158
  30.5 84.0 %collective-permute-start.8 = (s32[32,16]{0,1:T(8,128)S(1)}, s32[32,16]{0,1:T(8,128)S(1)}, u32[]{:S(2)}, u32[]{:S(2)}) collective-permute-start(s32[32,16]{0,1:T(8,128)S(1)} %copy-done.8), channel_id=1, source_target_pairs={{0,6},{2,4},{4,2},{6,0},{1,7},{3,5},{5,3},{7,1},{8,14},{10,12},{12... | collective-permute-start | bytes 6152 | tf_op jit(solution)/shard_map/ppermute | solution.py:159
  31.2 78.1 %copy-start.10 = (s32[128,8]{0,1:T(8,128)S(1)}, s32[128,8]{0,1:T(8,128)}, u32[]{:S(2)}) copy-start(s32[128,8]{0,1:T(8,128)} %param.23) | copy-start | bytes 12292
  31.2 78.4 %copy-start.11 = (s32[8]{0:T(128)S(1)}, s32[8]{0:T(128)}, u32[]{:S(2)}) copy-start(s32[8]{0:T(128)} %param.20) | copy-start | bytes 100
  31.2 81.1 %copy-start.12 = (s32[256]{0:T(256)S(1)}, s32[256]{0:T(256)}, u32[]{:S(2)}) copy-start(s32[256]{0:T(256)} %param.21) | copy-start | bytes 3076
  31.2 81.2 %copy-start.4 = (bf16[128,3584]{1,0:T(8,128)(2,1)S(1)}, bf16[128,3584]{1,0:T(8,128)(2,1)}, u32[]{:S(2)}) copy-start(bf16[128,3584]{1,0:T(8,128)(2,1)} %param.22) | copy-start | bytes 2752516
  109.2 5.6 %collective-permute-start.11 = (f32[512,1152]{1,0:T(8,128)}, f32[512,1152]{1,0:T(8,128)}, u32[]{:S(2)}, u32[]{:S(2)}) collective-permute-start(f32[512,1152]{1,0:T(8,128)} %fusion.7), channel_id=1, source_target_pairs={{0,1},{1,0},{2,3},{3,2},{4,5},{5,4},{6,7},{7,6},{8,9},{9,8},{10,11... | collective-permute-start | bytes 7077896 | tf_op jit(solution)/shard_map/ppermute | solution.py:53
  139.7 1.5 collective-permute-start.12
  186.0 13.0 %all-to-all-start = ((f32[8,8,1792]{2,1,0:T(8,128)}), f32[8,8,1792]{2,1,0:T(8,128)S(1)}, u32[]{:S(2)}, u32[]{:S(2)}) async-start(f32[8,8,1792]{2,1,0:T(8,128)} %convolution_bitcast_fusion), calls=%async_computation | async-start | bytes 917504 | tf_op jit(solution)/shard_map/all_to_all | solution.py:189
  209.6 2.6 collective-permute-start.13
  265.9 51.4 %copy-start.7 = (f32[128,256]{1,0:T(8,128)S(1)}, f32[128,256]{1,0:T(8,128)}, u32[]{:S(2)}) copy-start(f32[128,256]{1,0:T(8,128)} %get-tuple-element.24) | copy-start | bytes 393220
  278.9 42.5 %collective-permute-start.14 = (f32[64,3712]{1,0:T(8,128)S(1)}, f32[64,3712]{1,0:T(8,128)}, u32[]{:S(2)}, u32[]{:S(2)}) collective-permute-start(f32[64,3712]{1,0:T(8,128)S(1)} %bitcast.80), channel_id=1, source_target_pairs={{0,1},{1,0},{2,3},{3,2},{4,5},{5,4},{6,7},{7,6},{8,9},{9,8},{10,11... | collective-permute-start | bytes 2850824 | tf_op jit(solution)/shard_map/ppermute | solution.py:53
  280.1 1.4 collective-permute-start
  282.2 3.7 %collective-permute-start.1 = (f32[8,128]{1,0:T(8,128)S(1)}, f32[8,128]{1,0:T(8,128)S(1)}, u32[]{:S(2)}, u32[]{:S(2)}) collective-permute-start(f32[8,128]{1,0:T(8,128)S(1)} %broadcast_add_fusion), channel_id=1, source_target_pairs={{0,2},{2,0},{1,3},{3,1},{4,6},{6,4},{5,7},{7,5},{8,10},{10,8},{9,1... | collective-permute-start | bytes 12296 | tf_op jit(solution)/shard_map/ppermute | solution.py:57
  286.5 5.2 %collective-permute-start.2 = (f32[8,128]{1,0:T(8,128)S(1)}, f32[8,128]{1,0:T(8,128)S(1)}, u32[]{:S(2)}, u32[]{:S(2)}) collective-permute-start(f32[8,128]{1,0:T(8,128)S(1)} %fusion.55), channel_id=1, source_target_pairs={{0,4},{4,0},{1,5},{5,1},{2,6},{6,2},{3,7},{7,3},{8,12},{12,8},{9,1... | collective-permute-start | bytes 12296 | tf_op jit(solution)/shard_map/ppermute | solution.py:57
  291.7 3.6 %collective-permute-start.3 = (f32[8,128]{1,0:T(8,128)S(1)}, f32[8,128]{1,0:T(8,128)S(1)}, u32[]{:S(2)}, u32[]{:S(2)}) collective-permute-start(f32[8,128]{1,0:T(8,128)S(1)} %add.137), channel_id=1, source_target_pairs={{0,8},{8,0},{16,24},{24,16},{1,9},{9,1},{17,25},{25,17},{2,10},{10... | collective-permute-start | bytes 12296 | tf_op jit(solution)/shard_map/ppermute | solution.py:57
  295.4 5.1 %collective-permute-start.4 = (f32[8,128]{1,0:T(8,128)S(1)}, f32[8,128]{1,0:T(8,128)S(1)}, u32[]{:S(2)}, u32[]{:S(2)}) collective-permute-start(f32[8,128]{1,0:T(8,128)S(1)} %add.138), channel_id=1, source_target_pairs={{0,16},{8,24},{16,0},{24,8},{1,17},{9,25},{17,1},{25,9},{2,18},{10... | collective-permute-start | bytes 12296 | tf_op jit(solution)/shard_map/ppermute | solution.py:57
  300.5 3.6 %collective-permute-start.5 = (f32[8,128]{1,0:T(8,128)S(1)}, f32[8,128]{1,0:T(8,128)S(1)}, u32[]{:S(2)}, u32[]{:S(2)}) collective-permute-start(f32[8,128]{1,0:T(8,128)S(1)} %add.139), channel_id=1, source_target_pairs={{0,32},{32,0},{64,96},{96,64},{128,160},{160,128},{192,224},{224,1... | collective-permute-start | bytes 12296 | tf_op jit(solution)/shard_map/ppermute | solution.py:57
  304.1 4.5 %collective-permute-start.6 = (f32[8,128]{1,0:T(8,128)S(1)}, f32[8,128]{1,0:T(8,128)S(1)}, u32[]{:S(2)}, u32[]{:S(2)}) collective-permute-start(f32[8,128]{1,0:T(8,128)S(1)} %add.140), channel_id=1, source_target_pairs={{0,64},{32,96},{64,0},{96,32},{128,192},{160,224},{192,128},{224,1... | collective-permute-start | bytes 12296 | tf_op jit(solution)/shard_map/ppermute | solution.py:57
  308.6 7.5 %collective-permute-start.7 = (f32[8,128]{1,0:T(8,128)S(1)}, f32[8,128]{1,0:T(8,128)S(1)}, u32[]{:S(2)}, u32[]{:S(2)}) collective-permute-start(f32[8,128]{1,0:T(8,128)S(1)} %add.141), channel_id=1, source_target_pairs={{0,128},{32,160},{64,192},{96,224},{128,0},{160,32},{192,64},{224,... | collective-permute-start | bytes 12296 | tf_op jit(solution)/shard_map/ppermute | solution.py:57
  (8 other events, 32.4 us)
Sparse Core Ops, SparseCore 0:
  16.5 85.8 all-gather.2
  105.0 77.2 all-gather.4
where the time goes:
time: 334 us; the launch traced here: 333 us
  waiting for transfers between devices  153 us (46%)
  blocking collectives  66 us (20%)
  matrix products  30.7 us (9%)
  other arithmetic  24.3 us (7%)
  local copies, waits for them, and re-layouts  22.6 us (7%)
  starting transfers between devices  18.4 us (6%)
  between operations  18.2 us (5%)
    all_gather x1, waiting for transfers between devices, shards(): out_all = lax.all_gather(moved[:, cut:], ('z', 'y'), axis=0, tiled=True)  41.1 us
    all_to_all x3, blocking collectives, spread(): lax.all_to_all(jnp.broadcast_to(x[None], (size,) + x.shape), axes, 0, 0,...  40.1 us
    ppermute x1, waiting for transfers between devices, shards(): half_other = lax.ppermute(half, RING_X, facing)  39.4 us
    all_gather x1, waiting for transfers between devices, shards(): in_all = lax.all_gather(moved[:, :cut], ('z', 'y'), axis=0, tiled=True)  31.8 us
    ppermute x8, waiting for transfers between devices, swap(): return lax.ppermute(x, axis, [(i, i ^ bit) for i in range(size)])  27.3 us
    all_to_all x1, blocking collectives, shards(): lax.all_to_all(part.reshape(4, batch // 8, -1), 'y', 0, 0, tiled=True)  17 us
    all_to_all x1, blocking collectives, shards(): lax.all_to_all(part.reshape(4, batch // 32, -1), RING_X, 0, 0, tiled=True)  8.94 us
    unnamed x29, local copies, waits for them, and re-layouts  7.58 us
  transfers between devices with their start and end apart: 18, of which 15 were waited for; matrix products, arithmetic and copies ran while one was open for 17% of the time, Pallas kernels for 0%

commit v1 on v0

v1 whole, which is shorter than its diff:
```python
import math

import jax
import jax.numpy as jnp
import numpy as np
from jax import lax
from jax.experimental import pallas as pl
from jax.experimental.pallas import tpu as pltpu
from jax.sharding import Mesh, PartitionSpec as P

HEAD_WIDTH = 128

rope_theta = 1000000.0
norm_eps = 1e-06
focal_beta = 0.9999

AXES = ("z", "y", "xh", "xl", "c")
SIZES = (8, 4, 2, 2, 2)
DP = ("z", "y", "xh")
MP = ("xl", "c")
RING_X = ("xh", "xl")


BLOCK = 128
CUT = 384


def rotary_tables(length):
    half = HEAD_WIDTH // 2
    frequency = rope_theta ** (-2.0 * np.arange(half) / HEAD_WIDTH)
    angles = np.arange(length)[:, None] * frequency[None, :]
    cosine = np.concatenate([np.cos(angles), np.cos(angles)], axis=1)
    sine = np.concatenate([-np.sin(angles), np.sin(angles)], axis=1)
    repeat = BLOCK // length
    return (
        jnp.asarray(np.tile(cosine, (repeat, 1)), jnp.float32),
        jnp.asarray(np.tile(sine, (repeat, 1)), jnp.float32),
    )


def project_kernel(place_ref, whole_ref, part_ref, a_ref, b0_ref, b1_ref, b2a_ref, b2b_ref, b3_ref, out_ref):
    contract = (((0,), (0,)), ((), ()))

    def dot(x, w):
        return lax.dot_general(x, w, contract, preferred_element_type=jnp.float32)

    y = place_ref[0]
    cut = a_ref.shape[1]
    half = b2a_ref.shape[0]
    out_ref[:, :cut] = dot(whole_ref[...], a_ref[...])
    far = part_ref[(y + 2) % 4]
    out_ref[:, cut:] = (
        dot(part_ref[y], b0_ref[...])
        + dot(part_ref[(y + 1) % 4], b1_ref[...])
        + dot(part_ref[(y + 3) % 4], b3_ref[...])
        + dot(far[:half], b2a_ref[...])
        + dot(far[half:], b2b_ref[...])
    )


def project(y, whole, part, a_all, pieces):
    depth, tokens = whole.shape
    columns = a_all.shape[1] + pieces[0].shape[1]
    block = tokens // 2
    fixed = [pl.BlockSpec(w.shape, lambda i, _: (0, 0)) for w in (a_all, *pieces)]
    return pl.pallas_call(
        project_kernel,
        out_shape=jax.ShapeDtypeStruct((tokens, columns), jnp.float32),
        grid_spec=pltpu.PrefetchScalarGridSpec(
            num_scalar_prefetch=1,
            grid=(tokens // block,),
            in_specs=[
                pl.BlockSpec((depth, block), lambda i, _: (0, i)),
                pl.BlockSpec((4, depth // 4, block), lambda i, _: (0, 0, i)),
                *fixed,
            ],
            out_specs=pl.BlockSpec((block, columns), lambda i, _: (i, 0)),
        ),
        compiler_params=pltpu.CompilerParams(vmem_limit_bytes=40 << 20),
        cost_estimate=pl.CostEstimate(
            flops=2 * depth * tokens * columns,
            bytes_accessed=4 * tokens * columns + 2 * depth * (2 * tokens + columns),
            transcendentals=0,
        ),
        name="project",
    )(y.reshape(1).astype(jnp.int32), whole, part, a_all, *pieces)


def attend_kernel(raw_ref, add_ref, allowed_ref, live_ref, member_ref, cos_ref, sin_ref, out_ref):
    width = HEAD_WIDTH
    cosine, sine = cos_ref[...], sin_ref[...]
    members = member_ref[...]
    heads = raw_ref.shape[1] // width - 2
    texts = members.shape[0] // heads

    def rotate(x):
        return (x * cosine + pltpu.roll(x, width // 2, 1) * sine).astype(jnp.bfloat16)

    for block in range(raw_ref.shape[0] // BLOCK):
        rows = slice(block * BLOCK, (block + 1) * BLOCK)

        def column(index):
            lanes = slice(index * width, (index + 1) * width)
            return raw_ref[rows, lanes] + add_ref[rows, lanes]

        allowed = jnp.concatenate([allowed_ref[rows, :]] * heads, axis=0)
        live = jnp.concatenate([live_ref[rows, :]] * heads, axis=0)
        keys = rotate(column(0))
        values = column(1).astype(jnp.bfloat16)
        rotated = jnp.concatenate([rotate(column(h + 2)) for h in range(heads)], axis=0)
        scores = lax.dot_general(
            rotated, keys, (((1,), (1,)), ((), ())), preferred_element_type=jnp.float32
        ) * (1.0 / math.sqrt(width))
        weights = jnp.where(allowed > 0.0, jnp.exp(scores), 0.0)
        total = jnp.sum(weights, axis=1, keepdims=True)
        probs = (weights * (live / total)).astype(jnp.bfloat16)
        shares = jnp.dot(members, probs, preferred_element_type=jnp.float32)
        high = shares.astype(jnp.bfloat16)
        low = (shares - high.astype(jnp.float32)).astype(jnp.bfloat16)
        pooled = jnp.dot(high, values, preferred_element_type=jnp.float32) + jnp.dot(
            low, values, preferred_element_type=jnp.float32
        )
        for head in range(heads):
            out_ref[block * texts : (block + 1) * texts, head * width : (head + 1) * width] = pooled[
                head * texts : (head + 1) * texts
            ]


def attend_pooled(raw, add, text_ids):
    texts, length = text_ids.shape
    tokens, columns = raw.shape
    per = BLOCK // length
    heads = columns // HEAD_WIDTH - 2
    live = (text_ids != 0).reshape(texts // per, BLOCK)
    place = np.arange(BLOCK)
    shape = (place[:, None] // length == place[None, :] // length) & (
        place[:, None] >= place[None, :]
    )
    allowed = (jnp.asarray(shape)[None] & live[:, None, :]).astype(jnp.float32)
    owner = (np.arange(per)[:, None] == place[None, :] // length).astype(np.float32)
    members = jnp.asarray(np.kron(np.eye(heads), owner), jnp.bfloat16)
    cosine, sine = rotary_tables(length)
    step = 2 * BLOCK
    return pl.pallas_call(
        attend_kernel,
        out_shape=jax.ShapeDtypeStruct((texts, heads * HEAD_WIDTH), jnp.float32),
        grid=(tokens // step,),
        in_specs=[
            pl.BlockSpec((step, columns), lambda i: (i, 0)),
            pl.BlockSpec((step, columns), lambda i: (i, 0)),
            pl.BlockSpec((step, BLOCK), lambda i: (i, 0)),
            pl.BlockSpec((step, 1), lambda i: (i, 0)),
            pl.BlockSpec(members.shape, lambda i: (0, 0)),
            pl.BlockSpec((BLOCK, HEAD_WIDTH), lambda i: (0, 0)),
            pl.BlockSpec((BLOCK, HEAD_WIDTH), lambda i: (0, 0)),
        ],
        out_specs=pl.BlockSpec((2 * per, heads * HEAD_WIDTH), lambda i: (i, 0)),
        compiler_params=pltpu.CompilerParams(vmem_limit_bytes=32 << 20),
        cost_estimate=pl.CostEstimate(
            flops=4 * tokens * BLOCK * heads * HEAD_WIDTH,
            bytes_accessed=raw.size * 8,
            transcendentals=tokens * BLOCK * heads,
        ),
        name="attend",
    )(
        raw,
        add,
        allowed.reshape(tokens, BLOCK),
        live.astype(jnp.float32).reshape(tokens, 1),
        members,
        cosine,
        sine,
    )


def shift(x, axis, size, by):
    return lax.ppermute(x, axis, [(i, (i + by) % size) for i in range(size)])


def ring_pieces(own):
    up, down = shift(own, "y", 4, -1), shift(own, "y", 4, 1)
    half = own.shape[0] // 2
    return own, up, shift(up[:half], "y", 4, -1), shift(down[half:], "y", 4, 1), down


def in_order(parts, index):
    n = len(parts)
    out = jnp.zeros((n,) + parts[0].shape, parts[0].dtype)
    for d, part in enumerate(parts):
        out = lax.dynamic_update_slice_in_dim(out, part[None], (index + d) % n, 0)
    return out


def spread(x, axes, size):
    return lax.all_to_all(jnp.broadcast_to(x[None], (size,) + x.shape), axes, 0, 0, tiled=True)


def focal(margin):
    missed = jax.nn.sigmoid(-margin)
    softened = jax.nn.softplus(-margin)
    return missed * missed * softened, -(missed * missed) * (
        2.0 * jax.nn.sigmoid(margin) * softened + missed
    )


def shards(
    hidden_states,
    token_ids,
    norm_gain,
    q_weight,
    key_matrix,
    value_matrix,
    out_weight,
    label_table,
    refresh_rows,
    label_counts,
    queries,
    positives,
):
    f32, bf16 = jnp.float32, jnp.bfloat16
    width = hidden_states.shape[1]
    group_tokens = hidden_states.shape[0]
    texts, length = token_ids.shape
    xh, core = lax.axis_index("xh"), lax.axis_index("c")
    member = lax.axis_index(MP)
    ndp, nmp = 64, 4
    rows = q_weight.shape[0]

    packed = jnp.concatenate([key_matrix, value_matrix, q_weight, out_weight], axis=1)
    moved = lax.ppermute(
        packed,
        ("xh", "xl", "c"),
        [(4 * h + 2 * l + k, 4 * l + 2 * k + h) for h in (0, 1) for l in (0, 1) for k in (0, 1)],
    )
    cut = packed.shape[1] - out_weight.shape[1]
    y = lax.axis_index("y")
    far_z = lax.all_gather(moved[:, CUT:], "z", axis=0, tiled=True)
    part_a = moved[:, :CUT]
    a_y = in_order([part_a] + [shift(part_a, "y", 4, -d) for d in (1, 2, 3)], y)
    a_all = lax.all_gather(a_y.reshape(-1, CUT), "z", axis=0, tiled=True)
    pieces = ring_pieces(far_z[:, : cut - CUT])
    out_pieces = ring_pieces(far_z[:, cut - CUT :])

    balance = (1.0 - focal_beta) / -jnp.expm1(
        label_counts.astype(f32) * math.log(focal_beta)
    )
    owned = label_table.shape[0]
    root = math.sqrt(width)
    first_label = (lax.axis_index(DP) * nmp + member) * owned
    own_rows = jnp.arange(owned, dtype=jnp.int32)
    chosen = refresh_rows[:, None] == own_rows[None, :]
    kept = ~jnp.any(chosen, axis=0)
    kept_balance = jnp.where(kept, balance, 0.0)
    matched = jnp.any(positives[:, :, None] == (first_label + own_rows)[None, None, :], axis=1)
    signs = jnp.where(matched, 1.0, -1.0)
    logits = (
        lax.dot_general(
            queries, label_table, (((1,), (1,)), ((), ())), preferred_element_type=f32
        )
        / root
    )
    terms, slope = focal(signs * logits)
    kept_loss = jnp.sum(kept_balance[None, :] * terms)
    kept_slopes = (kept_balance[None, :] * signs * slope).astype(bf16)
    kept_query = jnp.dot(kept_slopes, label_table, preferred_element_type=f32)
    new_balance = jnp.sum(jnp.where(chosen, balance[None, :], 0.0), axis=1)
    new_signs = jnp.where(
        jnp.any(positives[:, :, None] == (first_label + refresh_rows)[None, None, :], axis=1),
        1.0,
        -1.0,
    )

    states = hidden_states.astype(f32)
    scaled = lax.rsqrt(jnp.mean(states * states, axis=1, keepdims=True) + norm_eps)
    normed = (states * scaled * norm_gain).astype(bf16)
    live = (token_ids != 0).astype(f32)
    share = texts // nmp
    live_own = lax.dynamic_slice_in_dim(live, member * share, share, 0)
    states_own = lax.dynamic_slice_in_dim(
        hidden_states, member * share * length, share * length, 0
    ).reshape(share, length, width)
    counted = jnp.sum(live_own, axis=1, keepdims=True)
    states_sum = jnp.sum(states_own.astype(f32) * live_own[:, :, None], axis=1)

    half = normed.T.reshape(ndp // 2, 2, rows, group_tokens)
    half = lax.dynamic_index_in_dim(half, core, 1, keepdims=False).reshape(-1, group_tokens)
    facing = [(i, 3 - i) for i in range(4)]
    half_other = lax.ppermute(half, RING_X, facing)
    ids_other = lax.ppermute(token_ids, RING_X, facing)
    keeps = xh == core
    give = jnp.where(keeps, half_other, half)
    keep = jnp.where(keeps, half, half_other)
    ids = jnp.where(keeps, token_ids, ids_other)

    def by_y(block):
        return block.reshape(8, 4, rows, -1).transpose(1, 0, 2, 3).reshape(4, 8 * rows, -1)

    taken = shift(project(y, give, by_y(give), a_all, pieces), "c", 2, 1)
    raw = project(y, keep, by_y(keep), a_all, pieces)
    pooled = attend_pooled(raw, taken, ids).astype(bf16)

    pooled_other = shift(pooled, "c", 2, 1)
    both = jnp.concatenate(
        [jnp.where(core == 0, pooled, pooled_other), jnp.where(core == 0, pooled_other, pooled)],
        axis=0,
    )
    out_all = jnp.concatenate(out_pieces, axis=0)
    head_terms = lax.dot_general(
        both, out_all, (((1,), (1,)), ((), ())), preferred_element_type=f32
    )
    blocks = head_terms.reshape(8, share, 4, 8 * rows)
    turned = jnp.concatenate([blocks, blocks], axis=2)
    head_terms = lax.dynamic_slice_in_dim(turned, 4 - y, 4, 2)
    exchanged = lax.all_to_all(
        head_terms.reshape(8, share, -1), ("xh", "xl", "c"), 0, 0, tiled=True
    )
    summed = jnp.sum(exchanged.reshape(nmp, 2, share, -1), axis=0)
    output_own = (
        summed.reshape(2, share, 4, 8, rows).transpose(1, 3, 2, 0, 4).reshape(share, width)
    )
    refreshed = ((states_sum + output_own) / counted).astype(bf16)

    new_logits = (
        lax.dot_general(
            queries, refreshed, (((1,), (1,)), ((), ())), preferred_element_type=f32
        )
        / root
    )
    new_terms, new_slope = focal(new_signs * new_logits)
    new_loss = jnp.sum(new_balance[None, :] * new_terms)
    new_slopes = (new_balance[None, :] * new_signs * new_slope).astype(bf16)
    query_part = kept_query + jnp.dot(new_slopes, refreshed, preferred_element_type=f32)
    slopes = kept_slopes + jnp.dot(
        new_slopes, chosen.astype(bf16), preferred_element_type=f32
    ).astype(bf16)
    label_part = lax.dot_general(
        slopes, queries, (((0,), (0,)), ((), ())), preferred_element_type=f32
    )

    batch = queries.shape[0]
    extra = jnp.stack([kept_loss + new_loss, jnp.sum(balance)]) / batch
    lanes = jnp.broadcast_to(jnp.repeat(extra, 64)[None, :], (batch, 128))
    payload = jnp.concatenate([query_part, lanes], axis=1)
    near = ("y", "xh", "xl", "c")
    part = jnp.sum(
        lax.all_to_all(payload.reshape(32, batch // 32, -1), near, 0, 0, tiled=True), axis=0
    )
    part = jnp.sum(spread(part, "z", 8), axis=0)
    whole = spread(part, near, 32).reshape(batch, -1)
    sums = jnp.sum(whole[:, width:], axis=0)
    total_labels = owned * ndp * nmp
    factor = total_labels / sums[64]
    scale = factor / root
    loss = factor * sums[0] / (batch * total_labels)
    return (scale * label_part, scale * whole[:, :width], loss)


def solution(mesh):
    grid = Mesh(mesh.devices.reshape(SIZES), AXES)
    in_specs = (
        P(DP, None),
        P(DP, None),
        P(),
        P(DP, MP),
        P(DP, MP),
        P(DP, MP),
        P(DP, MP),
        P(AXES, None),
        P(AXES),
        P(AXES),
        P(),
        P(),
    )
    out_specs = (P(AXES, None), P(), P())
    return jax.shard_map(shards, mesh=grid, in_specs=in_specs, out_specs=out_specs, check_vma=False)
```

time: 334 us -> 306 us (0.916)
  waiting for transfers between devices: 153 us -> 68 us
  local copies, waits for them, and re-layouts: 22.6 us -> 49 us
  matrix products: 30.7 us -> 12.5 us
  blocking collectives: 66 us -> 82.2 us
  Pallas kernels: 0 us -> 14.1 us
  starting transfers between devices: 18.4 us -> 26.9 us
  other arithmetic: 24.3 us -> 31.7 us
    ppermute x1, waiting for transfers between devices: 39.4 us -> 0.01 us  [shards(): half_other = lax.ppermute(half, RING_X, facing)]
    all_gather x2, waiting for transfers between devices: 72.9 us -> 38.5 us  [the longest x1 25.9 us: shards(): far_z = lax.all_gather(moved[:, CUT:], 'z', axis=0, tiled=True)]
    ppermute x8 -> x0, waiting for transfers between devices: 27.3 us -> none  [swap(): return lax.ppermute(x, axis, [(i, i ^ bit) for i in range(size)])]
    ppermute x4 -> x13, waiting for transfers between devices: 3.33 us -> 23.8 us  [shift(): return lax.ppermute(x, axis, [(i, (i + by) % size) for i in range(size)])]
    ppermute x4 -> x13, starting transfers between devices: 0.68 us -> 17 us  [shift(): return lax.ppermute(x, axis, [(i, (i + by) % size) for i in range(size)])]
    dot_general x3 -> x0, matrix products: 14.9 us -> none  [the longest x1 6.76 us: shards(): given = lax.dot_general(give, in_all, contract, preferred_element_type=f32)]
    pallas_call x0 -> x3, Pallas kernels: none -> 14.1 us  [the longest x2 9.88 us: project(): pl.pallas_call(project_kernel, out_shape=jax.ShapeDtypeStruct((tokens, co...]
    all_to_all x3 -> x2, blocking collectives: 40.1 us -> 51 us  [spread(): lax.all_to_all(jnp.broadcast_to(x[None], (size,) + x.shape), axes, 0, 0,...]
  transfers between devices with their start and end apart: 18 -> 19, of which waited for: 15 -> 9; matrix products, arithmetic and copies ran while one was open for 17% -> 19% of each run, Pallas kernels for 0% -> 3%
where the time goes in v1:
time: 306 us; the launch traced here: 303 us
  blocking collectives  82.2 us (27%)
  waiting for transfers between devices  68 us (22%)
  local copies, waits for them, and re-layouts  49 us (16%)
  other arithmetic  31.7 us (10%)
  starting transfers between devices  26.9 us (9%)
  between operations  18.2 us (6%)
  Pallas kernels  14.1 us (5%)
  matrix products  12.5 us (4%)
    all_to_all x2, blocking collectives, spread(): lax.all_to_all(jnp.broadcast_to(x[None], (size,) + x.shape), axes, 0, 0,...  51 us
    all_to_all x1, blocking collectives, shards(): lax.all_to_all(payload.reshape(32, batch // 32, -1), near, 0, 0, tiled=True)  31.2 us
    all_gather x1, waiting for transfers between devices, shards(): far_z = lax.all_gather(moved[:, CUT:], 'z', axis=0, tiled=True)  25.9 us
    ppermute x13, waiting for transfers between devices, shift(): return lax.ppermute(x, axis, [(i, (i + by) % size) for i in range(size)])  23.8 us
    unnamed x69, local copies, waits for them, and re-layouts  17.5 us
    ppermute x13, starting transfers between devices, shift(): return lax.ppermute(x, axis, [(i, (i + by) % size) for i in range(size)])  17 us
    all_gather x1, waiting for transfers between devices, shards(): a_all = lax.all_gather(a_y.reshape(-1, CUT), 'z', axis=0, tiled=True)  12.6 us
    pallas_call x2, Pallas kernels, project(): pl.pallas_call(project_kernel, out_shape=jax.ShapeDtypeStruct((tokens, co...  9.88 us
  transfers between devices with their start and end apart: 19, of which 9 were waited for; matrix products, arithmetic and copies ran while one was open for 19% of the time, Pallas kernels for 3%

profile of v1, /device:TPU:2, one launch (start us, length us, event | category | flops | bytes accessed | tf_op | source)
XLA Modules:
  0.0 302.7 jit_solution(1750977218204640767)
XLA Ops:
  8.3 3.4 %collective-permute-start.1 = (bf16[56,2048]{1,0:T(8,128)(2,1)S(1)}, bf16[56,2048]{1,0:T(8,128)(2,1)S(1)}, u32[]{:S(2)}, u32[]{:S(2)}) collective-permute-start(bf16[56,2048]{1,0:T(8,128)(2,1)S(1)} %pad_maximum_fusion.1), channel_id=1, source_target_pairs={{0,0},{1,2},{2,4},{3,6},{4,1},{5,3},{6,5},{7,7},{8,8},{9,10},{10,1... | collective-permute-start | bytes 688136 | tf_op jit(solution)/shard_map/ppermute | solution.py:230
  11.7 5.9 %copy.56 = bf16[512,3584]{0,1:T(8,128)(2,1)} copy(bf16[512,3584]{1,0:T(8,128)(2,1)} %param.16) | data formatting | bytes 7340032 | tf_op args[0]
  18.4 3.0 %fusion = f32[512]{0:T(512)S(1)} fusion(bf16[512,3584]{0,1:T(8,128)(2,1)} %copy.56), kind=kLoop, calls=%fused_computation.2 | loop fusion | flops 5504512 | bytes 3672064 | tf_op jit(solution)/shard_map/reduce_sum | solution.py:274
  24.6 3.0 %collective-permute-start.2 = (bf16[56,384]{1,0:T(8,128)(2,1)S(1)}, bf16[56,384]{1,0:T(8,128)(2,1)S(1)}, u32[]{:S(2)}, u32[]{:S(2)}) collective-permute-start(bf16[56,384]{1,0:T(8,128)(2,1)S(1)} %slice.48), channel_id=1, source_target_pairs={{0,24},{8,0},{16,8},{24,16},{1,25},{9,1},{17,9},{25,17},{2,26},{10... | collective-permute-start | bytes 129032 | tf_op jit(solution)/shard_map/ppermute | solution.py:177
  29.4 4.1 %collective-permute-done.3 = bf16[56,384]{1,0:T(8,128)(2,1)S(1)} collective-permute-done((bf16[56,384]{1,0:T(8,128)(2,1)S(1)}, bf16[56,384]{1,0:T(8,128)(2,1)S(1)}, u32[]{:S(2)}, u32[]{:S(2)}) %collective-permute-start.3) | collective-permute-done | bytes 43040 | tf_op jit(solution)/shard_map/ppermute | solution.py:177
  34.7 25.9 %all-gather.5.cloned.1.call-done = bf16[448,1664]{1,0:T(8,128)(2,1)} async-done(((bf16[56,1664]{1,0:T(8,128)(2,1)}), bf16[448,1664]{1,0:T(8,128)(2,1)}) %all-gather.5.cloned.1.call-update) | async-done | bytes 1490960 | tf_op jit(solution)/shard_map/all_gather | solution.py:237
  67.9 8.3 %collective-permute-done.5.b1_ref = bf16[448,768]{1,0:T(8,128)(2,1)S(1)} collective-permute-done((bf16[448,768]{1,0:T(8,128)(2,1)S(1)}, bf16[448,768]{1,0:T(8,128)(2,1)S(1)}, u32[]{:S(2)}, u32[]{:S(2)}) %collective-permute-start.5) | collective-permute-done | bytes 688160 | tf_op jit(solution)/shard_map/ppermute | solution.py:177
  76.9 3.0 collective-permute-start.6
  81.7 3.6 %broadcast_select_fusion = (bf16[1792,512]{1,0:T(8,128)(2,1)S(1)}, bf16[1792,512]{1,0:T(8,128)(2,1)}) fusion(bf16[1792,512]{1,0:T(8,128)(2,1)} %collective-permute-done, pred[]{:T(512)S(6)} %eq.61, bf16[32,1,56,512]{3,2,1,0:T(8,128)(2,1)} %constant_dynamic-slice_fusion), kind=kLoop, calls=%fused_computation.11 | loop fusion | flops 1835008 | bytes 7340033 | tf_op jit(solution)/shard_map/jit(_where)/select_n | solution.py:291
  87.9 12.6 %all-gather.3.cloned.1.call-done.a_ref = bf16[1792,384]{1,0:T(8,128)(2,1)} async-done(((bf16[224,384]{1,0:T(8,128)(2,1)}), bf16[1792,384]{1,0:T(8,128)(2,1)}) %all-gather.3.cloned.1.call-update) | async-done | bytes 1376272 | tf_op jit(solution)/shard_map/all_gather | solution.py:240
  104.9 5.4 %project.3 = f32[512,1152]{1,0:T(8,128)} custom-call(s32[1]{0:T(128)} %bitcast.1.place_ref, bf16[1792,512]{1,0:T(8,128)(2,1)S(1)} %copy-done.3, bf16[4,448,512]{2,1,0:T(8,128)(2,1)S(1)} %bitcast.50, bf16[1792,384]{1,0:T(8,128)(2,1)S(1)} %copy-done.5, bf16[448,768]{1,0:T(8,128)(2,1)S(1)} %slice.50.b0_ref, bf16[448,768]{1,0:T(8,128)(2,1)S(1)} %collective-permute-done.5.b1_ref, ...), custom_call_target="tpu_custom_call" | custom-call | flops 2113929216 | bytes 10158080 | tf_op jit(solution)/shard_map/project/pallas_call | solution.py:66
  113.6 3.2 %multiply_reduce_fusion = (f32[]{:T(128)}, f32[128,256]{1,0:T(8,128)}) fusion(f32[256]{0:T(256)} %broadcast_select_fusion.4, bf16[128,3584]{1,0:T(8,128)(2,1)} %param.26, bf16[256,3584]{1,0:T(8,128)(2,1)S(1)} %copy-done, pred[128,256]{1,0:T(8,128)(4,1)S(1)} %compare_reduce_fusion), kind=kOutput, calls=%fused_computation.30 | convolution fusion | flops 235405312 | bytes 2917380 | tf_op jit(solution)/shard_map/dot_general | solution.py:257
  132.3 6.7 %collective-permute-done.12 = bf16[448,896]{1,0:T(8,128)(2,1)} collective-permute-done((bf16[448,896]{1,0:T(8,128)(2,1)}, bf16[448,896]{1,0:T(8,128)(2,1)}, u32[]{:S(2)}, u32[]{:S(2)}) %collective-permute-start.12) | collective-permute-done | bytes 802848 | tf_op jit(solution)/shard_map/ppermute | solution.py:177
  140.8 3.7 %collective-permute-start.13 = (bf16[224,896]{1,0:T(8,128)(2,1)}, bf16[224,896]{1,0:T(8,128)(2,1)}, u32[]{:S(2)}, u32[]{:S(2)}) collective-permute-start(bf16[224,896]{1,0:T(8,128)(2,1)} %slice.54), channel_id=1, source_target_pairs={{0,24},{8,0},{16,8},{24,16},{1,25},{9,1},{17,9},{25,17},{2,26},{10... | collective-permute-start | bytes 1204232 | tf_op jit(solution)/shard_map/ppermute | solution.py:177
  154.1 4.5 %project.2.raw_ref = f32[512,1152]{1,0:T(8,128)S(1)} custom-call(s32[1]{0:T(128)} %bitcast.1.place_ref, bf16[1792,512]{1,0:T(8,128)(2,1)S(1)} %copy-done.1, bf16[4,448,512]{2,1,0:T(8,128)(2,1)S(1)} %bitcast.49, bf16[1792,384]{1,0:T(8,128)(2,1)S(1)} %copy-done.6, bf16[448,768]{1,0:T(8,128)(2,1)S(1)} %slice.50.b0_ref, ...), custom_call_target="tpu_custom_call" | custom-call | flops 2113929216 | bytes 10158080 | tf_op jit(solution)/shard_map/project/pallas_call | solution.py:66
  159.7 4.1 %collective-permute-done.15 = bf16[224,896]{1,0:T(8,128)(2,1)S(1)} collective-permute-done((bf16[224,896]{1,0:T(8,128)(2,1)S(1)}, bf16[224,896]{1,0:T(8,128)(2,1)S(1)}, u32[]{:S(2)}, u32[]{:S(2)}) %collective-permute-start.15) | collective-permute-done | bytes 401440 | tf_op jit(solution)/shard_map/ppermute | solution.py:177
  163.9 4.3 %attend.1 = f32[32,896]{1,0:T(8,128)S(1)} custom-call(f32[512,1152]{1,0:T(8,128)S(1)} %project.2.raw_ref, f32[512,1152]{1,0:T(8,128)} %collective-permute-done.9.add_ref, f32[512,128]{1,0:T(8,128)S(1)} %bitcast.51, f32[512,1]{1,0:T(8,128)S(1)} %copy-done.8, bf16[56,896]{1,0:T(8,128)(2,1)S(1)} %copy-done.9, f32[128,128]{1,0:T(8,128)S(1)} %copy-done.10, ...), custom_call_target="tpu_custom_call" | custom-call | flops 234881024 | bytes 4718592 | tf_op jit(solution)/shard_map/attend/pallas_call | solution.py:144
  172.8 4.9 %all-to-all-start = ((f32[8,8,1792]{2,1,0:T(8,128)}), f32[8,8,1792]{2,1,0:T(8,128)S(1)}, u32[]{:S(2)}, u32[]{:S(2)}) async-start(f32[8,8,1792]{2,1,0:T(8,128)} %reshape.118), calls=%async_computation | async-start | bytes 917504 | tf_op jit(solution)/shard_map/all_to_all | solution.py:314
  180.2 5.7 %all-to-all-done = f32[8,8,1792]{2,1,0:T(8,128)S(1)} async-done(((f32[8,8,1792]{2,1,0:T(8,128)}), f32[8,8,1792]{2,1,0:T(8,128)S(1)}, u32[]{:S(2)}, u32[]{:S(2)}) %all-to-all-start) | async-done | bytes 458784 | tf_op jit(solution)/shard_map/all_to_all | solution.py:314
  199.0 31.2 %all_to_all.20 = f32[32,4,3712]{2,1,0:T(4,128)} all-to-all(f32[32,4,3712]{2,1,0:T(4,128)} %reshape.122), channel_id=1, replica_groups=mesh['z'=8,'y'=4,'xh'=2,'xl'=2,'c'=2] {'y','xh','xl','c'}, dimensions={0} | all-to-all | bytes 3801088 | tf_op jit(solution)/shard_map/all_to_all | solution.py:346
  232.1 21.0 %all_to_all.21 = f32[8,4,3712]{2,1,0:T(4,128)S(1)} all-to-all(f32[8,4,3712]{2,1,0:T(4,128)S(1)} %broadcast_in_dim.100), channel_id=1, replica_groups=mesh['z'=8,'y'=4,'xh'=2,'xl'=2,'c'=2] {'z'}, dimensions={0} | all-to-all | bytes 950272 | tf_op jit(solution)/shard_map/all_to_all | solution.py:195
  253.4 30.0 %all_to_all.22 = f32[32,4,3712]{2,1,0:T(4,128)} all-to-all(f32[32,4,3712]{2,1,0:T(4,128)S(1)} %broadcast_in_dim.101), channel_id=1, replica_groups=mesh['z'=8,'y'=4,'xh'=2,'xl'=2,'c'=2] {'y','xh','xl','c'}, dimensions={0} | all-to-all | bytes 3801088 | tf_op jit(solution)/shard_map/all_to_all | solution.py:195
  283.4 2.9 reshape.123
  288.4 2.9 slice_multiply_fusion
  (160 shorter events, 81.3 us)
Async XLA Ops:
  7.2 106.4 %copy-start = (bf16[256,3584]{1,0:T(8,128)(2,1)S(1)}, bf16[256,3584]{1,0:T(8,128)(2,1)}, u32[]{:S(2)}) copy-start(bf16[256,3584]{1,0:T(8,128)(2,1)} %param.23) | copy-start | bytes 5505028
  7.2 53.4 %all-gather.5.cloned.1.call-start = ((), (), s32[]{:S(2)}) async-start(), calls=%async_computation.5 | async-start | bytes 1677312 | tf_op jit(solution)/shard_map/all_gather | solution.py:237
  8.3 9.3 %collective-permute-start.1 = (bf16[56,2048]{1,0:T(8,128)(2,1)S(1)}, bf16[56,2048]{1,0:T(8,128)(2,1)S(1)}, u32[]{:S(2)}, u32[]{:S(2)}) collective-permute-start(bf16[56,2048]{1,0:T(8,128)(2,1)S(1)} %pad_maximum_fusion.1), channel_id=1, source_target_pairs={{0,0},{1,2},{2,4},{3,6},{4,1},{5,3},{6,5},{7,7},{8,8},{9,10},{10,1... | collective-permute-start | bytes 688136 | tf_op jit(solution)/shard_map/ppermute | solution.py:230
  18.4 82.2 %all-gather.3.cloned.1.call-start = ((), (), s32[]{:S(2)}) async-start(), calls=%async_computation.4 | async-start | bytes 1548288 | tf_op jit(solution)/shard_map/all_gather | solution.py:240
  24.5 41.5 %copy-start.28 = (s32[8]{0:T(128)S(1)}, s32[8]{0:T(128)}, u32[]{:S(2)}) copy-start(s32[8]{0:T(128)} %param.24) | copy-start | bytes 100
  24.5 41.6 %copy-start.31 = (s32[256]{0:T(256)S(1)}, s32[256]{0:T(256)}, u32[]{:S(2)}) copy-start(s32[256]{0:T(256)} %param.25) | copy-start | bytes 3076
  24.5 57.2 %collective-permute-start = (bf16[1792,512]{1,0:T(8,128)(2,1)}, bf16[1792,512]{1,0:T(8,128)(2,1)}, u32[]{:S(2)}, u32[]{:S(2)}) collective-permute-start(bf16[1792,512]{1,0:T(8,128)(2,1)} %bitcast.4), channel_id=1, source_target_pairs={{0,6},{2,4},{4,2},{6,0},{1,7},{3,5},{5,3},{7,1},{8,14},{10,12},{12... | collective-permute-start | bytes 5505032 | tf_op jit(solution)/shard_map/ppermute | solution.py:288
  24.6 4.9 %collective-permute-start.2 = (bf16[56,384]{1,0:T(8,128)(2,1)S(1)}, bf16[56,384]{1,0:T(8,128)(2,1)S(1)}, u32[]{:S(2)}, u32[]{:S(2)}) collective-permute-start(bf16[56,384]{1,0:T(8,128)(2,1)S(1)} %slice.48), channel_id=1, source_target_pairs={{0,24},{8,0},{16,8},{24,16},{1,25},{9,1},{17,9},{25,17},{2,26},{10... | collective-permute-start | bytes 129032 | tf_op jit(solution)/shard_map/ppermute | solution.py:177
  27.6 5.9 %collective-permute-start.3 = (bf16[56,384]{1,0:T(8,128)(2,1)S(1)}, bf16[56,384]{1,0:T(8,128)(2,1)S(1)}, u32[]{:S(2)}, u32[]{:S(2)}) collective-permute-start(bf16[56,384]{1,0:T(8,128)(2,1)S(1)} %slice.48), channel_id=1, source_target_pairs={{0,16},{8,24},{16,0},{24,8},{1,17},{9,25},{17,1},{25,9},{2,18},{10... | collective-permute-start | bytes 129032 | tf_op jit(solution)/shard_map/ppermute | solution.py:177
  28.2 5.8 %collective-permute-start.4 = (bf16[56,384]{1,0:T(8,128)(2,1)S(1)}, bf16[56,384]{1,0:T(8,128)(2,1)S(1)}, u32[]{:S(2)}, u32[]{:S(2)}) collective-permute-start(bf16[56,384]{1,0:T(8,128)(2,1)S(1)} %slice.48), channel_id=1, source_target_pairs={{0,8},{8,16},{16,24},{24,0},{1,9},{9,17},{17,25},{25,1},{2,10},{10... | collective-permute-start | bytes 129032 | tf_op jit(solution)/shard_map/ppermute | solution.py:177
  61.7 14.5 %collective-permute-start.5 = (bf16[448,768]{1,0:T(8,128)(2,1)S(1)}, bf16[448,768]{1,0:T(8,128)(2,1)S(1)}, u32[]{:S(2)}, u32[]{:S(2)}) collective-permute-start(bf16[448,768]{1,0:T(8,128)(2,1)S(1)} %slice.50.b0_ref), channel_id=1, source_target_pairs={{0,24},{8,0},{16,8},{24,16},{1,25},{9,1},{17,9},{25,17},{2,26},{10... | collective-permute-start | bytes 2064392 | tf_op jit(solution)/shard_map/ppermute | solution.py:177
  64.5 15.4 %collective-permute-start.7 = (bf16[448,768]{1,0:T(8,128)(2,1)S(1)}, bf16[448,768]{1,0:T(8,128)(2,1)}, u32[]{:S(2)}, u32[]{:S(2)}) collective-permute-start(bf16[448,768]{1,0:T(8,128)(2,1)S(1)} %slice.50.b0_ref), channel_id=1, source_target_pairs={{0,8},{8,16},{16,24},{24,0},{1,9},{9,17},{17,25},{25,1},{2,10},{10... | collective-permute-start | bytes 2064392 | tf_op jit(solution)/shard_map/ppermute | solution.py:177
  64.6 63.8 %collective-permute-start.10 = (s32[32,16]{0,1:T(8,128)}, s32[32,16]{0,1:T(8,128)}, u32[]{:S(2)}, u32[]{:S(2)}) collective-permute-start(s32[32,16]{0,1:T(8,128)} %param.17), channel_id=1, source_target_pairs={{0,6},{2,4},{4,2},{6,0},{1,7},{3,5},{5,3},{7,1},{8,14},{10,12},{12... | collective-permute-start | bytes 6152 | tf_op jit(solution)/shard_map/ppermute | solution.py:289
  76.9 23.6 %collective-permute-start.6 = (bf16[224,768]{1,0:T(8,128)(2,1)}, bf16[224,768]{1,0:T(8,128)(2,1)S(1)}, u32[]{:S(2)}, u32[]{:S(2)}) collective-permute-start(bf16[224,768]{1,0:T(8,128)(2,1)} %slice.51), channel_id=1, source_target_pairs={{0,24},{8,0},{16,8},{24,16},{1,25},{9,1},{17,9},{25,17},{2,26},{10... | collective-permute-start | bytes 1032200 | tf_op jit(solution)/shard_map/ppermute | solution.py:177
  81.7 18.9 %collective-permute-start.8 = (bf16[224,768]{1,0:T(8,128)(2,1)}, bf16[224,768]{1,0:T(8,128)(2,1)}, u32[]{:S(2)}, u32[]{:S(2)}) collective-permute-start(bf16[224,768]{1,0:T(8,128)(2,1)} %slice.52), channel_id=1, source_target_pairs={{0,8},{8,16},{16,24},{24,0},{1,9},{9,17},{17,25},{25,1},{2,10},{10... | collective-permute-start | bytes 1032200 | tf_op jit(solution)/shard_map/ppermute | solution.py:177
  110.3 53.6 %collective-permute-start.9 = (f32[512,1152]{1,0:T(8,128)}, f32[512,1152]{1,0:T(8,128)}, u32[]{:S(2)}, u32[]{:S(2)}) collective-permute-start(f32[512,1152]{1,0:T(8,128)} %project.3), channel_id=1, source_target_pairs={{0,1},{1,0},{2,3},{3,2},{4,5},{5,4},{6,7},{7,6},{8,9},{9,8},{10,11... | collective-permute-start | bytes 7077896 | tf_op jit(solution)/shard_map/ppermute | solution.py:177
  118.1 20.8 %collective-permute-start.12 = (bf16[448,896]{1,0:T(8,128)(2,1)}, bf16[448,896]{1,0:T(8,128)(2,1)}, u32[]{:S(2)}, u32[]{:S(2)}) collective-permute-start(bf16[448,896]{1,0:T(8,128)(2,1)} %get-tuple-element.11), channel_id=1, source_target_pairs={{0,24},{8,0},{16,8},{24,16},{1,25},{9,1},{17,9},{25,17},{2,26},{10... | collective-permute-start | bytes 2408456 | tf_op jit(solution)/shard_map/ppermute | solution.py:177
  124.0 26.6 %collective-permute-start.14 = (bf16[448,896]{1,0:T(8,128)(2,1)}, bf16[448,896]{1,0:T(8,128)(2,1)}, u32[]{:S(2)}, u32[]{:S(2)}) collective-permute-start(bf16[448,896]{1,0:T(8,128)(2,1)} %get-tuple-element.11), channel_id=1, source_target_pairs={{0,8},{8,16},{16,24},{24,0},{1,9},{9,17},{17,25},{25,1},{2,10},{10... | collective-permute-start | bytes 2408456 | tf_op jit(solution)/shard_map/ppermute | solution.py:177
  140.8 17.8 %collective-permute-start.13 = (bf16[224,896]{1,0:T(8,128)(2,1)}, bf16[224,896]{1,0:T(8,128)(2,1)}, u32[]{:S(2)}, u32[]{:S(2)}) collective-permute-start(bf16[224,896]{1,0:T(8,128)(2,1)} %slice.54), channel_id=1, source_target_pairs={{0,24},{8,0},{16,8},{24,16},{1,25},{9,1},{17,9},{25,17},{2,26},{10... | collective-permute-start | bytes 1204232 | tf_op jit(solution)/shard_map/ppermute | solution.py:177
  151.8 11.9 %collective-permute-start.15 = (bf16[224,896]{1,0:T(8,128)(2,1)S(1)}, bf16[224,896]{1,0:T(8,128)(2,1)S(1)}, u32[]{:S(2)}, u32[]{:S(2)}) collective-permute-start(bf16[224,896]{1,0:T(8,128)(2,1)S(1)} %slice.55), channel_id=1, source_target_pairs={{0,8},{8,16},{16,24},{24,0},{1,9},{9,17},{17,25},{25,1},{2,10},{10... | collective-permute-start | bytes 1204232 | tf_op jit(solution)/shard_map/ppermute | solution.py:177
  154.0 9.8 %copy-start.8 = (f32[512,1]{1,0:T(8,128)S(1)}, f32[512,1]{1,0:T(8,128)}, u32[]{:S(2)}) copy-start(f32[512,1]{1,0:T(8,128)} %reshape.127.live_ref) | copy-start | bytes 6148
  168.2 1.4 collective-permute-start.11
  172.8 13.1 %all-to-all-start = ((f32[8,8,1792]{2,1,0:T(8,128)}), f32[8,8,1792]{2,1,0:T(8,128)S(1)}, u32[]{:S(2)}, u32[]{:S(2)}) async-start(f32[8,8,1792]{2,1,0:T(8,128)} %reshape.118), calls=%async_computation | async-start | bytes 917504 | tf_op jit(solution)/shard_map/all_to_all | solution.py:314
  178.4 9.8 %copy-start.18 = (f32[8,3584]{1,0:T(8,128)S(1)}, f32[8,3584]{1,0:T(8,128)}, u32[]{:S(2)}) copy-start(f32[8,3584]{1,0:T(8,128)} %fusion.3) | copy-start | bytes 344068
  (27 other events, 141.0 us)
Sparse Core Ops, SparseCore 0:
  18.5 42.0 all-gather.4
  62.4 38.1 all-gather.2

commit v2 on v1

--- a/solution.py
+++ b/solution.py
@@ -22,7 +22,8 @@
 
 
 BLOCK = 128
-CUT = 384
+CUT = 256
+HALF = 1920
 
 
 def rotary_tables(length):
@@ -126,18 +127,24 @@
             ]
 
 
-def attend_pooled(raw, add, text_ids):
+def attend_tables(text_ids):
     texts, length = text_ids.shape
-    tokens, columns = raw.shape
     per = BLOCK // length
-    heads = columns // HEAD_WIDTH - 2
     live = (text_ids != 0).reshape(texts // per, BLOCK)
     place = np.arange(BLOCK)
     shape = (place[:, None] // length == place[None, :] // length) & (
         place[:, None] >= place[None, :]
     )
     allowed = (jnp.asarray(shape)[None] & live[:, None, :]).astype(jnp.float32)
-    owner = (np.arange(per)[:, None] == place[None, :] // length).astype(np.float32)
+    return allowed.reshape(-1, BLOCK), (text_ids != 0).astype(jnp.float32).reshape(-1, 1)
+
+
+def attend_pooled(raw, add, allowed, live, length):
+    tokens, columns = raw.shape
+    texts = tokens // length
+    per = BLOCK // length
+    heads = columns // HEAD_WIDTH - 2
+    owner = (np.arange(per)[:, None] == np.arange(BLOCK)[None, :] // length).astype(np.float32)
     members = jnp.asarray(np.kron(np.eye(heads), owner), jnp.bfloat16)
     cosine, sine = rotary_tables(length)
     step = 2 * BLOCK
@@ -165,8 +172,8 @@
     )(
         raw,
         add,
-        allowed.reshape(tokens, BLOCK),
-        live.astype(jnp.float32).reshape(tokens, 1),
+        allowed,
+        live,
         members,
         cosine,
         sine,
@@ -197,10 +204,64 @@
 
 def focal(margin):
     missed = jax.nn.sigmoid(-margin)
-    softened = jax.nn.softplus(-margin)
+    softened = jnp.maximum(-margin, 0.0) + jnp.log1p(jnp.exp(-jnp.abs(margin)))
     return missed * missed * softened, -(missed * missed) * (
         2.0 * jax.nn.sigmoid(margin) * softened + missed
     )
+
+
+def tail_kernel(core_ref, sums_ref, new_ref, queries_ref, kept_ref, signs_ref, balance_ref, mine_ref, theirs_ref, slopes_ref):
+    batch, width = queries_ref.shape
+    rows = new_ref[...]
+    logits = lax.dot_general(
+        queries_ref[...], rows, (((1,), (1,)), ((), ())), preferred_element_type=jnp.float32
+    ) / math.sqrt(width)
+    signs = signs_ref[...]
+    balance = balance_ref[...]
+    terms, slope = focal(signs * logits)
+    losses = jnp.sum(balance * terms, axis=1, keepdims=True) + sums_ref[0] / batch
+    slopes = (balance * signs * slope).astype(jnp.bfloat16)
+    slopes_ref[...] = slopes.astype(jnp.float32)
+    left = kept_ref[:, :HALF] + jnp.dot(slopes, rows[:, :HALF], preferred_element_type=jnp.float32)
+    right = kept_ref[:, HALF:] + jnp.dot(slopes, rows[:, HALF:], preferred_element_type=jnp.float32)
+    rest = width - HALF
+    lanes = (2 * HALF - width) // 2
+    loss_lanes = jnp.broadcast_to(losses, (batch, lanes))
+    class_lanes = jnp.full((batch, lanes), sums_ref[1] / batch, jnp.float32)
+
+    def write(first, second):
+        first[...] = left
+        second[:, :rest] = right
+        second[:, rest : rest + lanes] = loss_lanes
+        second[:, rest + lanes :] = class_lanes
+
+    @pl.when(core_ref[0] == 0)
+    def _():
+        write(mine_ref, theirs_ref)
+
+    @pl.when(core_ref[0] != 0)
+    def _():
+        write(theirs_ref, mine_ref)
+
+
+def tail(core, sums, rows, queries, kept, signs, balance):
+    batch, width = queries.shape
+    smem = pl.BlockSpec(memory_space=pltpu.SMEM)
+    vmem = pl.BlockSpec(memory_space=pltpu.VMEM)
+    half = jax.ShapeDtypeStruct((batch, HALF), jnp.float32)
+    return pl.pallas_call(
+        tail_kernel,
+        out_shape=(half, half, jax.ShapeDtypeStruct((batch, rows.shape[0]), jnp.float32)),
+        in_specs=[smem, smem, vmem, vmem, vmem, vmem, vmem],
+        out_specs=(vmem, vmem, vmem),
+        compiler_params=pltpu.CompilerParams(vmem_limit_bytes=24 << 20),
+        cost_estimate=pl.CostEstimate(
+            flops=4 * batch * width * rows.shape[0],
+            bytes_accessed=10 * batch * width,
+            transcendentals=8 * batch,
+        ),
+        name="tail",
+    )(core.reshape(1).astype(jnp.int32), sums, rows, queries, kept, signs, balance)
 
 
 def shards(
@@ -295,9 +356,16 @@
     def by_y(block):
         return block.reshape(8, 4, rows, -1).transpose(1, 0, 2, 3).reshape(4, 8 * rows, -1)
 
-    taken = shift(project(y, give, by_y(give), a_all, pieces), "c", 2, 1)
-    raw = project(y, keep, by_y(keep), a_all, pieces)
-    pooled = attend_pooled(raw, taken, ids).astype(bf16)
+    allowed, live_rows = attend_tables(ids)
+    sums = jnp.stack([kept_loss, jnp.sum(balance)])
+    early = (kept_query, kept_slopes, sums, new_balance, new_signs, chosen, states_sum, counted)
+    early = early + (allowed, live_rows, give, keep, by_y(give), by_y(keep))
+    (a_all, pieces, early) = lax.optimization_barrier((a_all, pieces, early))
+    kept_query, kept_slopes, sums, new_balance, new_signs, chosen, states_sum, counted = early[:8]
+    allowed, live_rows, give, keep, give_y, keep_y = early[8:]
+    taken = shift(project(y, give, give_y, a_all, pieces), "c", 2, 1)
+    raw = project(y, keep, keep_y, a_all, pieces)
+    pooled = attend_pooled(raw, taken, allowed, live_rows, length).astype(bf16)
 
     pooled_other = shift(pooled, "c", 2, 1)
     both = jnp.concatenate(
@@ -308,51 +376,46 @@
     head_terms = lax.dot_general(
         both, out_all, (((1,), (1,)), ((), ())), preferred_element_type=f32
     )
-    blocks = head_terms.reshape(8, share, 4, 8 * rows)
-    turned = jnp.concatenate([blocks, blocks], axis=2)
-    head_terms = lax.dynamic_slice_in_dim(turned, 4 - y, 4, 2)
     exchanged = lax.all_to_all(
         head_terms.reshape(8, share, -1), ("xh", "xl", "c"), 0, 0, tiled=True
     )
     summed = jnp.sum(exchanged.reshape(nmp, 2, share, -1), axis=0)
+    blocks = summed.reshape(2, share, 4, 8 * rows)
+    turned = lax.dynamic_slice_in_dim(jnp.concatenate([blocks, blocks], axis=2), 4 - y, 4, 2)
     output_own = (
-        summed.reshape(2, share, 4, 8, rows).transpose(1, 3, 2, 0, 4).reshape(share, width)
+        turned.reshape(2, share, 4, 8, rows).transpose(1, 3, 2, 0, 4).reshape(share, width)
     )
     refreshed = ((states_sum + output_own) / counted).astype(bf16)
 
-    new_logits = (
-        lax.dot_general(
-            queries, refreshed, (((1,), (1,)), ((), ())), preferred_element_type=f32
-        )
-        / root
-    )
-    new_terms, new_slope = focal(new_signs * new_logits)
-    new_loss = jnp.sum(new_balance[None, :] * new_terms)
-    new_slopes = (new_balance[None, :] * new_signs * new_slope).astype(bf16)
-    query_part = kept_query + jnp.dot(new_slopes, refreshed, preferred_element_type=f32)
+    mine, theirs, new_slopes = tail(
+        core, sums, refreshed, queries, kept_query, new_signs, new_balance[None, :]
+    )
     slopes = kept_slopes + jnp.dot(
-        new_slopes, chosen.astype(bf16), preferred_element_type=f32
+        new_slopes.astype(bf16), chosen.astype(bf16), preferred_element_type=f32
     ).astype(bf16)
     label_part = lax.dot_general(
         slopes, queries, (((0,), (0,)), ((), ())), preferred_element_type=f32
     )
 
     batch = queries.shape[0]
-    extra = jnp.stack([kept_loss + new_loss, jnp.sum(balance)]) / batch
-    lanes = jnp.broadcast_to(jnp.repeat(extra, 64)[None, :], (batch, 128))
-    payload = jnp.concatenate([query_part, lanes], axis=1)
-    near = ("y", "xh", "xl", "c")
+    near = ("y", "xh", "xl")
+    part = mine + shift(theirs, "c", 2, 1)
     part = jnp.sum(
-        lax.all_to_all(payload.reshape(32, batch // 32, -1), near, 0, 0, tiled=True), axis=0
+        lax.all_to_all(part.reshape(16, batch // 16, HALF), near, 0, 0, tiled=True), axis=0
     )
     part = jnp.sum(spread(part, "z", 8), axis=0)
-    whole = spread(part, near, 32).reshape(batch, -1)
-    sums = jnp.sum(whole[:, width:], axis=0)
+    part = spread(part, near, 16).reshape(batch, HALF)
+    back = shift(part, "c", 2, 1)
+    left = jnp.where(core == 0, part, back)
+    right = jnp.where(core == 0, back, part)
+    rest = width - HALF
+    lanes = (2 * HALF - width) // 2
     total_labels = owned * ndp * nmp
-    factor = total_labels / sums[64]
+    factor = total_labels / jnp.sum(right[:, rest + lanes])
     scale = factor / root
-    loss = factor * sums[0] / (batch * total_labels)
-    return (scale * label_part, scale * whole[:, :width], loss)
+    loss = factor * jnp.sum(right[:, rest]) / (batch * total_labels)
+    query_grad = scale * jnp.concatenate([left, right[:, :rest]], axis=1)
+    return (scale * label_part, query_grad, loss)
 
 
 def solution(mesh):

time: 306 us -> 277 us (0.905)
  local copies, waits for them, and re-layouts: 49 us -> 32 us
  other arithmetic: 31.7 us -> 23.6 us
  matrix products: 12.5 us -> 7.68 us
  starting transfers between devices: 26.9 us -> 30.3 us
  waiting for transfers between devices: 68 us -> 64.9 us
    all_gather x0 -> x1, blocking collectives: none -> 25.9 us  [shards(): a_all = lax.all_gather(a_y.reshape(-1, CUT), 'z', axis=0, tiled=True)]
    all_gather x1 -> x0, waiting for transfers between devices: 12.6 us -> none  [shards(): a_all = lax.all_gather(a_y.reshape(-1, CUT), 'z', axis=0, tiled=True)]
    all_to_all x2, blocking collectives: 51 us -> 38.5 us  [spread(): lax.all_to_all(jnp.broadcast_to(x[None], (size,) + x.shape), axes, 0, 0,...]
    all_to_all x1, blocking collectives: 31.2 us -> 19.7 us  [shards(): lax.all_to_all(part.reshape(16, batch // 16, HALF), near, 0, 0, tiled=True)]
    ppermute x13 -> x15, waiting for transfers between devices: 23.8 us -> 34.2 us  [shift(): return lax.ppermute(x, axis, [(i, (i + by) % size) for i in range(size)])]
    reshape x6 -> x5, local copies, waits for them, and re-layouts: 8.86 us -> 2.27 us  [the longest x1 1.03 us: shards(): blocks = summed.reshape(2, share, 4, 8 * rows)]
    dot_general x2 -> x0, matrix products: 3.69 us -> none  [the longest x1 2.02 us: shards(): jnp.dot(new_slopes, refreshed, preferred_element_type=f32)]
    all_gather x1, waiting for transfers between devices: 25.9 us -> 22.5 us  [shards(): far_z = lax.all_gather(moved[:, CUT:], 'z', axis=0, tiled=True)]
  transfers between devices with their start and end apart: 19 -> 20, of which waited for: 9 -> 10; matrix products, arithmetic and copies ran while one was open for 19% -> 16% of each run, Pallas kernels for 3% -> 1%
where the time goes in v2:
time: 277 us; the launch traced here: 274 us
  blocking collectives  84.1 us (30%)
  waiting for transfers between devices  64.9 us (23%)
  local copies, waits for them, and re-layouts  32 us (12%)
  starting transfers between devices  30.3 us (11%)
  other arithmetic  23.6 us (9%)
  between operations  17.1 us (6%)
  Pallas kernels  14.4 us (5%)
  matrix products  7.68 us (3%)
    all_to_all x2, blocking collectives, spread(): lax.all_to_all(jnp.broadcast_to(x[None], (size,) + x.shape), axes, 0, 0,...  38.5 us
    ppermute x15, waiting for transfers between devices, shift(): return lax.ppermute(x, axis, [(i, (i + by) % size) for i in range(size)])  34.2 us
    all_gather x1, blocking collectives, shards(): a_all = lax.all_gather(a_y.reshape(-1, CUT), 'z', axis=0, tiled=True)  25.9 us
    all_gather x1, waiting for transfers between devices, shards(): far_z = lax.all_gather(moved[:, CUT:], 'z', axis=0, tiled=True)  22.5 us
    all_to_all x1, blocking collectives, shards(): lax.all_to_all(part.reshape(16, batch // 16, HALF), near, 0, 0, tiled=True)  19.7 us
    ppermute x15, starting transfers between devices, shift(): return lax.ppermute(x, axis, [(i, (i + by) % size) for i in range(size)])  19.5 us
    unnamed x79, local copies, waits for them, and re-layouts  18.6 us
    all_to_all x1, waiting for transfers between devices, shards(): lax.all_to_all(head_terms.reshape(8, share, -1), ('xh', 'xl', 'c'), 0, 0,...  8.19 us
  transfers between devices with their start and end apart: 20, of which 10 were waited for; matrix products, arithmetic and copies ran while one was open for 16% of the time, Pallas kernels for 1%

profile of v2, /device:TPU:2, one launch (start us, length us, event | category | flops | bytes accessed | tf_op | source)
XLA Modules:
  0.0 274.1 jit_solution(6558734536911630763)
XLA Ops:
  12.2 5.9 %copy.52 = bf16[512,3584]{0,1:T(8,128)(2,1)} copy(bf16[512,3584]{1,0:T(8,128)(2,1)} %param.16) | data formatting | bytes 7340032 | tf_op args[0]
  18.2 2.9 %fusion = f32[512]{0:T(512)S(1)} fusion(bf16[512,3584]{0,1:T(8,128)(2,1)} %copy.52), kind=kLoop, calls=%fused_computation.2 | loop fusion | flops 5504512 | bytes 3672064 | tf_op jit(solution)/shard_map/reduce_sum | solution.py:335
  21.1 3.1 %fusion.2 = bf16[512,3584]{0,1:T(8,128)(2,1)S(1)} fusion(bf16[512,3584]{0,1:T(8,128)(2,1)} %copy.52, f32[3584]{0:T(1024)S(1)} %copy-done.30, f32[512]{0:T(512)S(1)} %add_rsqrt_fusion), kind=kLoop, calls=%fused_computation.4 | loop fusion | flops 7340032 | bytes 7356416 | tf_op jit(solution)/shard_map/convert_element_type | solution.py:336
  41.3 3.2 %collective-permute-start.2 = (bf16[56,256]{1,0:T(8,128)(2,1)S(1)}, bf16[56,256]{1,0:T(8,128)(2,1)S(1)}, u32[]{:S(2)}, u32[]{:S(2)}) collective-permute-start(bf16[56,256]{1,0:T(8,128)(2,1)S(1)} %slice.44), channel_id=1, source_target_pairs={{0,16},{8,24},{16,0},{24,8},{1,17},{9,25},{17,1},{25,9},{2,18},{10... | collective-permute-start | bytes 86024 | tf_op jit(solution)/shard_map/ppermute | solution.py:184
  48.3 22.5 %all-gather.2.cloned.1.call-done = bf16[448,1792]{1,0:T(8,128)(2,1)} async-done(((bf16[56,1792]{1,0:T(8,128)(2,1)}), bf16[448,1792]{1,0:T(8,128)(2,1)}) %all-gather.2.cloned.1.call-update) | async-done | bytes 1605648 | tf_op jit(solution)/shard_map/all_gather | solution.py:298
  76.6 25.9 %all_gather.6.a_ref = bf16[1792,256]{1,0:T(8,128)(2,1)S(1)} all-gather(bf16[224,256]{1,0:T(8,128)(2,1)S(1)} %bitcast.65), channel_id=1, replica_groups=mesh['z'=8,'y'=4,'xh'=2,'xl'=2,'c'=2] {'z'}, dimensions={0}, use_global_device_ids=true | all-gather | bytes 1032192 | tf_op jit(solution)/shard_map/all_gather | solution.py:301
  103.3 2.8 %collective-permute-start.5 = (bf16[224,896]{1,0:T(8,128)(2,1)S(1)}, bf16[224,896]{1,0:T(8,128)(2,1)S(1)}, u32[]{:S(2)}, u32[]{:S(2)}) collective-permute-start(bf16[224,896]{1,0:T(8,128)(2,1)S(1)} %slice.47), channel_id=1, source_target_pairs={{0,24},{8,0},{16,8},{24,16},{1,25},{9,1},{17,9},{25,17},{2,26},{10... | collective-permute-start | bytes 1204232 | tf_op jit(solution)/shard_map/ppermute | solution.py:184
  111.7 4.5 %project.3 = f32[512,1152]{1,0:T(8,128)} custom-call(s32[1]{0:T(128)} %bitcast.20.place_ref, bf16[1792,512]{1,0:T(8,128)(2,1)S(1)} %get-tuple-element.36.whole_ref, bf16[4,448,512]{2,1,0:T(8,128)(2,1)S(1)} %bitcast.58, bf16[1792,256]{1,0:T(8,128)(2,1)S(1)} %all_gather.6.a_ref, bf16[448,896]{1,0:T(8,128)(2,1)S(1)} %get-tuple-element.31.b0_ref, ...), custom_call_target="tpu_custom_call" | custom-call | flops 2113929216 | bytes 10158080 | tf_op jit(solution)/shard_map/project/pallas_call | solution.py:67
  116.2 3.6 %collective-permute-start.12 = (bf16[448,896]{1,0:T(8,128)(2,1)S(1)}, bf16[448,896]{1,0:T(8,128)(2,1)S(1)}, u32[]{:S(2)}, u32[]{:S(2)}) collective-permute-start(bf16[448,896]{1,0:T(8,128)(2,1)S(1)} %get-tuple-element.61), channel_id=1, source_target_pairs={{0,24},{8,0},{16,8},{24,16},{1,25},{9,1},{17,9},{25,17},{2,26},{10... | collective-permute-start | bytes 2408456 | tf_op jit(solution)/shard_map/ppermute | solution.py:184
  119.8 17.8 %collective-permute-done.12 = bf16[448,896]{1,0:T(8,128)(2,1)S(1)} collective-permute-done((bf16[448,896]{1,0:T(8,128)(2,1)S(1)}, bf16[448,896]{1,0:T(8,128)(2,1)S(1)}, u32[]{:S(2)}, u32[]{:S(2)}) %collective-permute-start.12) | collective-permute-done | bytes 802848 | tf_op jit(solution)/shard_map/ppermute | solution.py:184
  138.4 3.7 %collective-permute-start.13 = (bf16[224,896]{1,0:T(8,128)(2,1)}, bf16[224,896]{1,0:T(8,128)(2,1)}, u32[]{:S(2)}, u32[]{:S(2)}) collective-permute-start(bf16[224,896]{1,0:T(8,128)(2,1)} %slice.50), channel_id=1, source_target_pairs={{0,24},{8,0},{16,8},{24,16},{1,25},{9,1},{17,9},{25,17},{2,26},{10... | collective-permute-start | bytes 1204232 | tf_op jit(solution)/shard_map/ppermute | solution.py:184
  147.5 3.3 %collective-permute-done.13 = bf16[224,896]{1,0:T(8,128)(2,1)} collective-permute-done((bf16[224,896]{1,0:T(8,128)(2,1)}, bf16[224,896]{1,0:T(8,128)(2,1)}, u32[]{:S(2)}, u32[]{:S(2)}) %collective-permute-start.13) | collective-permute-done | bytes 401440 | tf_op jit(solution)/shard_map/ppermute | solution.py:184
  152.5 3.4 %collective-permute-done.15 = bf16[224,896]{1,0:T(8,128)(2,1)} collective-permute-done((bf16[224,896]{1,0:T(8,128)(2,1)}, bf16[224,896]{1,0:T(8,128)(2,1)}, u32[]{:S(2)}, u32[]{:S(2)}) %collective-permute-start.15) | collective-permute-done | bytes 401440 | tf_op jit(solution)/shard_map/ppermute | solution.py:184
  163.5 3.4 %project.2.raw_ref = f32[512,1152]{1,0:T(8,128)S(1)} custom-call(s32[1]{0:T(128)} %bitcast.20.place_ref, bf16[1792,512]{1,0:T(8,128)(2,1)S(1)} %get-tuple-element.28.whole_ref, bf16[4,448,512]{2,1,0:T(8,128)(2,1)S(1)} %bitcast.57, bf16[1792,256]{1,0:T(8,128)(2,1)S(1)} %all_gather.6.a_ref, bf16[448,896]{1,0:T(8,128)(2,1)S(1)} %get-tuple-element.31.b0_ref, ...), custom_call_target="tpu_custom_call" | custom-call | flops 2113929216 | bytes 10158080 | tf_op jit(solution)/shard_map/project/pallas_call | solution.py:67
  167.0 4.4 %attend.1 = f32[32,896]{1,0:T(8,128)S(1)} custom-call(f32[512,1152]{1,0:T(8,128)S(1)} %project.2.raw_ref, f32[512,1152]{1,0:T(8,128)} %collective-permute-done.10.add_ref, f32[512,128]{1,0:T(8,128)S(1)} %bitcast.59, f32[512,1]{1,0:T(8,128)S(1)} %copy-done.15, bf16[56,896]{1,0:T(8,128)(2,1)S(1)} %copy-done.17, f32[128,128]{1,0:T(8,128)S(1)} %copy-done.19, ...), custom_call_target="tpu_custom_call" | custom-call | flops 234881024 | bytes 4718592 | tf_op jit(solution)/shard_map/attend/pallas_call | solution.py:151
  174.8 4.9 %all-to-all-start = ((f32[8,8,1792]{2,1,0:T(8,128)}), f32[8,8,1792]{2,1,0:T(8,128)S(1)}, u32[]{:S(2)}, u32[]{:S(2)}) async-start(f32[8,8,1792]{2,1,0:T(8,128)} %convolution_bitcast_fusion), calls=%async_computation | async-start | bytes 917504 | tf_op jit(solution)/shard_map/all_to_all | solution.py:379
  179.7 8.2 %all-to-all-done = f32[8,8,1792]{2,1,0:T(8,128)S(1)} async-done(((f32[8,8,1792]{2,1,0:T(8,128)}), f32[8,8,1792]{2,1,0:T(8,128)S(1)}, u32[]{:S(2)}, u32[]{:S(2)}) %all-to-all-start) | async-done | bytes 458784 | tf_op jit(solution)/shard_map/all_to_all | solution.py:379
  192.8 2.6 collective-permute-done.16
  195.5 19.7 %all_to_all.20 = f32[16,8,1920]{2,1,0:T(8,128)S(1)} all-to-all(f32[16,8,1920]{2,1,0:T(8,128)S(1)} %add_bitcast_fusion), channel_id=1, replica_groups=mesh['z'=8,'y'=4,'xh'=2,'xl'=2,'c'=2] {'y','xh','xl'}, dimensions={0} | all-to-all | bytes 1966080 | tf_op jit(solution)/shard_map/all_to_all | solution.py:404
  215.3 20.5 %all_to_all.21 = f32[8,8,1920]{2,1,0:T(8,128)S(1)} all-to-all(f32[8,8,1920]{2,1,0:T(8,128)S(1)} %broadcast_in_dim.92), channel_id=1, replica_groups=mesh['z'=8,'y'=4,'xh'=2,'xl'=2,'c'=2] {'z'}, dimensions={0} | all-to-all | bytes 983040 | tf_op jit(solution)/shard_map/all_to_all | solution.py:202
  235.9 18.0 %all_to_all.22 = f32[16,8,1920]{2,1,0:T(8,128)S(1)} all-to-all(f32[16,8,1920]{2,1,0:T(8,128)S(1)} %broadcast_in_dim.93), channel_id=1, replica_groups=mesh['z'=8,'y'=4,'xh'=2,'xl'=2,'c'=2] {'y','xh','xl'}, dimensions={0} | all-to-all | bytes 1966080 | tf_op jit(solution)/shard_map/all_to_all | solution.py:202
  253.9 2.6 collective-permute-done.17
  260.5 3.0 %maximum_multiply_fusion = f32[128,3584]{1,0:T(8,128)} fusion(f32[128,1664]{1,0:T(8,128)} %slice.53, f32[128,1920]{1,0:T(8,128)} %get-tuple-element.59, f32[]{:T(128)S(6)} %div.55), kind=kLoop, calls=%fused_computation.7 | loop fusion | flops 917504 | bytes 3670020 | tf_op jit(solution)/shard_map/mul | solution.py:417
  263.4 2.6 convolution_multiply_fusion
  (169 shorter events, 64.6 us)
Async XLA Ops:
  7.2 23.8 %copy-start = (bf16[256,3584]{1,0:T(8,128)(2,1)S(1)}, bf16[256,3584]{1,0:T(8,128)(2,1)}, u32[]{:S(2)}) copy-start(bf16[256,3584]{1,0:T(8,128)(2,1)} %param.23) | copy-start | bytes 5505028
  7.2 63.7 %all-gather.2.cloned.1.call-start = ((), (), s32[]{:S(2)}) async-start(), calls=%async_computation.4 | async-start | bytes 1806336 | tf_op jit(solution)/shard_map/all_gather | solution.py:298
  7.2 32.4 %collective-permute-start.8 = (s32[32,16]{0,1:T(8,128)}, s32[32,16]{0,1:T(8,128)S(1)}, u32[]{:S(2)}, u32[]{:S(2)}) collective-permute-start(s32[32,16]{0,1:T(8,128)} %param.17), channel_id=1, source_target_pairs={{0,6},{2,4},{4,2},{6,0},{1,7},{3,5},{5,3},{7,1},{8,14},{10,12},{12... | collective-permute-start | bytes 6152 | tf_op jit(solution)/shard_map/ppermute | solution.py:350
  9.8 18.3 %collective-permute-start = (bf16[56,2048]{1,0:T(8,128)(2,1)S(1)}, bf16[56,2048]{1,0:T(8,128)(2,1)S(1)}, u32[]{:S(2)}, u32[]{:S(2)}) collective-permute-start(bf16[56,2048]{1,0:T(8,128)(2,1)S(1)} %pad_maximum_fusion), channel_id=1, source_target_pairs={{0,0},{1,2},{2,4},{3,6},{4,1},{5,3},{6,5},{7,7},{8,8},{9,10},{10,1... | collective-permute-start | bytes 688136 | tf_op jit(solution)/shard_map/ppermute | solution.py:291
  25.6 80.5 %collective-permute-start.9 = (bf16[1792,512]{1,0:T(8,128)(2,1)}, bf16[1792,512]{1,0:T(8,128)(2,1)}, u32[]{:S(2)}, u32[]{:S(2)}) collective-permute-start(bf16[1792,512]{1,0:T(8,128)(2,1)} %bitcast.13), channel_id=1, source_target_pairs={{0,6},{2,4},{4,2},{6,0},{1,7},{3,5},{5,3},{7,1},{8,14},{10,12},{12... | collective-permute-start | bytes 5505032 | tf_op jit(solution)/shard_map/ppermute | solution.py:349
  41.3 35.3 %collective-permute-start.2 = (bf16[56,256]{1,0:T(8,128)(2,1)S(1)}, bf16[56,256]{1,0:T(8,128)(2,1)S(1)}, u32[]{:S(2)}, u32[]{:S(2)}) collective-permute-start(bf16[56,256]{1,0:T(8,128)(2,1)S(1)} %slice.44), channel_id=1, source_target_pairs={{0,16},{8,24},{16,0},{24,8},{1,17},{9,25},{17,1},{25,9},{2,18},{10... | collective-permute-start | bytes 86024 | tf_op jit(solution)/shard_map/ppermute | solution.py:184
  44.5 3.9 %collective-permute-start.1 = (bf16[56,256]{1,0:T(8,128)(2,1)S(1)}, bf16[56,256]{1,0:T(8,128)(2,1)S(1)}, u32[]{:S(2)}, u32[]{:S(2)}) collective-permute-start(bf16[56,256]{1,0:T(8,128)(2,1)S(1)} %slice.44), channel_id=1, source_target_pairs={{0,24},{8,0},{16,8},{24,16},{1,25},{9,1},{17,9},{25,17},{2,26},{10... | collective-permute-start | bytes 86024 | tf_op jit(solution)/shard_map/ppermute | solution.py:184
  45.5 31.0 %collective-permute-start.3 = (bf16[56,256]{1,0:T(8,128)(2,1)S(1)}, bf16[56,256]{1,0:T(8,128)(2,1)S(1)}, u32[]{:S(2)}, u32[]{:S(2)}) collective-permute-start(bf16[56,256]{1,0:T(8,128)(2,1)S(1)} %slice.44), channel_id=1, source_target_pairs={{0,8},{8,16},{16,24},{24,0},{1,9},{9,17},{17,25},{25,1},{2,10},{10... | collective-permute-start | bytes 86024 | tf_op jit(solution)/shard_map/ppermute | solution.py:184
  73.3 29.2 %collective-permute-start.6 = (bf16[448,896]{1,0:T(8,128)(2,1)S(1)}, bf16[448,896]{1,0:T(8,128)(2,1)S(1)}, u32[]{:S(2)}, u32[]{:S(2)}) collective-permute-start(bf16[448,896]{1,0:T(8,128)(2,1)S(1)} %get-tuple-element.31.b0_ref), channel_id=1, source_target_pairs={{0,8},{8,16},{16,24},{24,0},{1,9},{9,17},{17,25},{25,1},{2,10},{10... | collective-permute-start | bytes 2408456 | tf_op jit(solution)/shard_map/ppermute | solution.py:184
  74.8 28.5 %collective-permute-start.4 = (bf16[448,896]{1,0:T(8,128)(2,1)S(1)}, bf16[448,896]{1,0:T(8,128)(2,1)S(1)}, u32[]{:S(2)}, u32[]{:S(2)}) collective-permute-start(bf16[448,896]{1,0:T(8,128)(2,1)S(1)} %get-tuple-element.31.b0_ref), channel_id=1, source_target_pairs={{0,24},{8,0},{16,8},{24,16},{1,25},{9,1},{17,9},{25,17},{2,26},{10... | collective-permute-start | bytes 2408456 | tf_op jit(solution)/shard_map/ppermute | solution.py:184
  102.5 9.2 %collective-permute-start.7 = (bf16[224,896]{1,0:T(8,128)(2,1)S(1)}, bf16[224,896]{1,0:T(8,128)(2,1)S(1)}, u32[]{:S(2)}, u32[]{:S(2)}) collective-permute-start(bf16[224,896]{1,0:T(8,128)(2,1)S(1)} %slice.48), channel_id=1, source_target_pairs={{0,8},{8,16},{16,24},{24,0},{1,9},{9,17},{17,25},{25,1},{2,10},{10... | collective-permute-start | bytes 1204232 | tf_op jit(solution)/shard_map/ppermute | solution.py:184
  103.3 8.3 %collective-permute-start.5 = (bf16[224,896]{1,0:T(8,128)(2,1)S(1)}, bf16[224,896]{1,0:T(8,128)(2,1)S(1)}, u32[]{:S(2)}, u32[]{:S(2)}) collective-permute-start(bf16[224,896]{1,0:T(8,128)(2,1)S(1)} %slice.47), channel_id=1, source_target_pairs={{0,24},{8,0},{16,8},{24,16},{1,25},{9,1},{17,9},{25,17},{2,26},{10... | collective-permute-start | bytes 1204232 | tf_op jit(solution)/shard_map/ppermute | solution.py:184
  116.2 50.8 %collective-permute-start.10 = (f32[512,1152]{1,0:T(8,128)}, f32[512,1152]{1,0:T(8,128)}, u32[]{:S(2)}, u32[]{:S(2)}) collective-permute-start(f32[512,1152]{1,0:T(8,128)} %project.3), channel_id=1, source_target_pairs={{0,1},{1,0},{2,3},{3,2},{4,5},{5,4},{6,7},{7,6},{8,9},{9,8},{10,11... | collective-permute-start | bytes 7077896 | tf_op jit(solution)/shard_map/ppermute | solution.py:184
  116.2 21.4 %collective-permute-start.12 = (bf16[448,896]{1,0:T(8,128)(2,1)S(1)}, bf16[448,896]{1,0:T(8,128)(2,1)S(1)}, u32[]{:S(2)}, u32[]{:S(2)}) collective-permute-start(bf16[448,896]{1,0:T(8,128)(2,1)S(1)} %get-tuple-element.61), channel_id=1, source_target_pairs={{0,24},{8,0},{16,8},{24,16},{1,25},{9,1},{17,9},{25,17},{2,26},{10... | collective-permute-start | bytes 2408456 | tf_op jit(solution)/shard_map/ppermute | solution.py:184
  119.8 22.3 %collective-permute-start.14 = (bf16[448,896]{1,0:T(8,128)(2,1)S(1)}, bf16[448,896]{1,0:T(8,128)(2,1)S(1)}, u32[]{:S(2)}, u32[]{:S(2)}) collective-permute-start(bf16[448,896]{1,0:T(8,128)(2,1)S(1)} %get-tuple-element.61), channel_id=1, source_target_pairs={{0,8},{8,16},{16,24},{24,0},{1,9},{9,17},{17,25},{25,1},{2,10},{10... | collective-permute-start | bytes 2408456 | tf_op jit(solution)/shard_map/ppermute | solution.py:184
  138.4 12.4 %collective-permute-start.13 = (bf16[224,896]{1,0:T(8,128)(2,1)}, bf16[224,896]{1,0:T(8,128)(2,1)}, u32[]{:S(2)}, u32[]{:S(2)}) collective-permute-start(bf16[224,896]{1,0:T(8,128)(2,1)} %slice.50), channel_id=1, source_target_pairs={{0,24},{8,0},{16,8},{24,16},{1,25},{9,1},{17,9},{25,17},{2,26},{10... | collective-permute-start | bytes 1204232 | tf_op jit(solution)/shard_map/ppermute | solution.py:184
  143.9 12.1 %collective-permute-start.15 = (bf16[224,896]{1,0:T(8,128)(2,1)}, bf16[224,896]{1,0:T(8,128)(2,1)}, u32[]{:S(2)}, u32[]{:S(2)}) collective-permute-start(bf16[224,896]{1,0:T(8,128)(2,1)} %slice.51), channel_id=1, source_target_pairs={{0,8},{8,16},{16,24},{24,0},{1,9},{9,17},{17,25},{25,1},{2,10},{10... | collective-permute-start | bytes 1204232 | tf_op jit(solution)/shard_map/ppermute | solution.py:184
  171.5 1.3 collective-permute-start.11
  172.9 17.7 %copy-start.3 = (f32[128,3584]{1,0:T(8,128)S(1)}, f32[128,3584]{1,0:T(8,128)}, u32[]{:S(2)}) copy-start(f32[128,3584]{1,0:T(8,128)} %fusion.22.kept_ref) | copy-start | bytes 5505028
  172.9 17.7 %copy-start.9 = (bf16[128,3584]{1,0:T(8,128)(2,1)S(1)}, bf16[128,3584]{1,0:T(8,128)(2,1)}, u32[]{:S(2)}) copy-start(bf16[128,3584]{1,0:T(8,128)(2,1)} %queries_ref.1) | copy-start | bytes 2752516
  172.9 17.7 %copy-start.16 = (f32[128,8]{1,0:T(8,128)S(1)}, f32[128,8]{1,0:T(8,128)}, u32[]{:S(2)}) copy-start(f32[128,8]{1,0:T(8,128)} %broadcast_select_fusion.6.signs_ref) | copy-start | bytes 12292
  174.8 13.1 %all-to-all-start = ((f32[8,8,1792]{2,1,0:T(8,128)}), f32[8,8,1792]{2,1,0:T(8,128)S(1)}, u32[]{:S(2)}, u32[]{:S(2)}) async-start(f32[8,8,1792]{2,1,0:T(8,128)} %convolution_bitcast_fusion), calls=%async_computation | async-start | bytes 917504 | tf_op jit(solution)/shard_map/all_to_all | solution.py:379
  192.7 2.7 collective-permute-start.16
  253.9 2.6 collective-permute-start.17
  (33 other events, 194.5 us)
Sparse Core Ops, SparseCore 0:
  29.0 41.8 all-gather.1

commit v3 on v2

--- a/solution.py
+++ b/solution.py
@@ -1,3 +1,4 @@
+import functools
 import math
 
 import jax
@@ -22,7 +23,7 @@
 
 
 BLOCK = 128
-CUT = 256
+CUT = 384
 HALF = 1920
 
 
@@ -77,7 +78,7 @@
             ],
             out_specs=pl.BlockSpec((block, columns), lambda i, _: (i, 0)),
         ),
-        compiler_params=pltpu.CompilerParams(vmem_limit_bytes=40 << 20),
+        compiler_params=pltpu.CompilerParams(vmem_limit_bytes=56 << 20),
         cost_estimate=pl.CostEstimate(
             flops=2 * depth * tokens * columns,
             bytes_accessed=4 * tokens * columns + 2 * depth * (2 * tokens + columns),
@@ -162,7 +163,7 @@
             pl.BlockSpec((BLOCK, HEAD_WIDTH), lambda i: (0, 0)),
         ],
         out_specs=pl.BlockSpec((2 * per, heads * HEAD_WIDTH), lambda i: (i, 0)),
-        compiler_params=pltpu.CompilerParams(vmem_limit_bytes=32 << 20),
+        compiler_params=pltpu.CompilerParams(vmem_limit_bytes=56 << 20),
         cost_estimate=pl.CostEstimate(
             flops=4 * tokens * BLOCK * heads * HEAD_WIDTH,
             bytes_accessed=raw.size * 8,
@@ -184,10 +185,13 @@
     return lax.ppermute(x, axis, [(i, (i + by) % size) for i in range(size)])
 
 
-def ring_pieces(own):
-    up, down = shift(own, "y", 4, -1), shift(own, "y", 4, 1)
-    half = own.shape[0] // 2
-    return own, up, shift(up[:half], "y", 4, -1), shift(down[half:], "y", 4, 1), down
+def ring_near(own):
+    return shift(own, "y", 4, -1), shift(own, "y", 4, 1)
+
+
+def ring_far(up, down):
+    half = up.shape[0] // 2
+    return shift(up[:half], "y", 4, -1), shift(down[half:], "y", 4, 1)
 
 
 def in_order(parts, index):
@@ -262,6 +266,70 @@
         ),
         name="tail",
     )(core.reshape(1).astype(jnp.int32), sums, rows, queries, kept, signs, balance)
+
+
+def final_kernel(core_ref, part_ref, back_ref, slopes_ref, queries_ref, label_ref, query_ref, loss_ref, *, labels):
+    batch, width = queries_ref.shape
+    rest = width - HALF
+    lanes = (2 * HALF - width) // 2
+    first = core_ref[0] == 0
+    step = pl.program_id(0)
+    rows = pl.ds(pl.multiple_of(step * query_ref.shape[0], 8), query_ref.shape[0])
+
+    def side(left_ref, right_ref):
+        losses = jnp.sum(right_ref[:, rest : rest + lanes]) / lanes
+        weights = jnp.sum(right_ref[:, rest + lanes :]) / lanes
+        factor = labels / weights
+        scale = factor / math.sqrt(width)
+        loss_ref[...] = jnp.full(loss_ref.shape, factor * losses / (batch * labels), jnp.float32)
+        query_ref[:, :HALF] = scale * left_ref[rows, :]
+        query_ref[:, HALF:] = scale * right_ref[rows, :rest]
+        label_ref[...] = scale * lax.dot_general(
+            slopes_ref[...],
+            queries_ref[...],
+            (((1,), (0,)), ((), ())),
+            preferred_element_type=jnp.float32,
+        )
+
+    @pl.when(first)
+    def _():
+        side(part_ref, back_ref)
+
+    @pl.when(jnp.logical_not(first))
+    def _():
+        side(back_ref, part_ref)
+
+
+def final(core, part, back, slopes, queries, labels):
+    batch, width = queries.shape
+    owned = slopes.shape[0]
+    steps = 4
+    whole = lambda x: pl.BlockSpec(x.shape, lambda i, _: (0, 0))
+    return pl.pallas_call(
+        functools.partial(final_kernel, labels=labels),
+        out_shape=(
+            jax.ShapeDtypeStruct((owned, width), jnp.float32),
+            jax.ShapeDtypeStruct((batch, width), jnp.float32),
+            jax.ShapeDtypeStruct((8, 128), jnp.float32),
+        ),
+        grid_spec=pltpu.PrefetchScalarGridSpec(
+            num_scalar_prefetch=1,
+            grid=(steps,),
+            in_specs=[
+                whole(part),
+                whole(back),
+                pl.BlockSpec((owned // steps, batch), lambda i, _: (i, 0)),
+                whole(queries),
+            ],
+            out_specs=(
+                pl.BlockSpec((owned // steps, width), lambda i, _: (i, 0)),
+                pl.BlockSpec((batch // steps, width), lambda i, _: (i, 0)),
+                pl.BlockSpec((8, 128), lambda i, _: (0, 0)),
+            ),
+        ),
+        compiler_params=pltpu.CompilerParams(vmem_limit_bytes=32 << 20),
+        name="final",
+    )(core.reshape(1).astype(jnp.int32), part, back, slopes, queries)
 
 
 def shards(
@@ -294,13 +362,18 @@
         [(4 * h + 2 * l + k, 4 * l + 2 * k + h) for h in (0, 1) for l in (0, 1) for k in (0, 1)],
     )
     cut = packed.shape[1] - out_weight.shape[1]
+    moved, hidden_states = lax.optimization_barrier((moved, hidden_states))
     y = lax.axis_index("y")
     far_z = lax.all_gather(moved[:, CUT:], "z", axis=0, tiled=True)
     part_a = moved[:, :CUT]
     a_y = in_order([part_a] + [shift(part_a, "y", 4, -d) for d in (1, 2, 3)], y)
     a_all = lax.all_gather(a_y.reshape(-1, CUT), "z", axis=0, tiled=True)
-    pieces = ring_pieces(far_z[:, : cut - CUT])
-    out_pieces = ring_pieces(far_z[:, cut - CUT :])
+    own = far_z[:, : cut - CUT]
+    up, down = ring_near(own)
+    pieces = (own, up, *ring_far(up, down), down)
+    far_z, pieces = lax.optimization_barrier((far_z, pieces))
+    out_own = far_z[:, cut - CUT :]
+    out_up, out_down = ring_near(out_own)
 
     balance = (1.0 - focal_beta) / -jnp.expm1(
         label_counts.astype(f32) * math.log(focal_beta)
@@ -365,6 +438,8 @@
     allowed, live_rows, give, keep, give_y, keep_y = early[8:]
     taken = shift(project(y, give, give_y, a_all, pieces), "c", 2, 1)
     raw = project(y, keep, keep_y, a_all, pieces)
+    raw, out_up, out_down = lax.optimization_barrier((raw, out_up, out_down))
+    out_far = ring_far(out_up, out_down)
     pooled = attend_pooled(raw, taken, allowed, live_rows, length).astype(bf16)
 
     pooled_other = shift(pooled, "c", 2, 1)
@@ -372,7 +447,7 @@
         [jnp.where(core == 0, pooled, pooled_other), jnp.where(core == 0, pooled_other, pooled)],
         axis=0,
     )
-    out_all = jnp.concatenate(out_pieces, axis=0)
+    out_all = jnp.concatenate([out_own, out_up, *out_far, out_down], axis=0)
     head_terms = lax.dot_general(
         both, out_all, (((1,), (1,)), ((), ())), preferred_element_type=f32
     )
@@ -390,12 +465,12 @@
     mine, theirs, new_slopes = tail(
         core, sums, refreshed, queries, kept_query, new_signs, new_balance[None, :]
     )
-    slopes = kept_slopes + jnp.dot(
-        new_slopes.astype(bf16), chosen.astype(bf16), preferred_element_type=f32
+    slopes = kept_slopes.T + lax.dot_general(
+        chosen.astype(bf16),
+        new_slopes.astype(bf16),
+        (((0,), (1,)), ((), ())),
+        preferred_element_type=f32,
     ).astype(bf16)
-    label_part = lax.dot_general(
-        slopes, queries, (((0,), (0,)), ((), ())), preferred_element_type=f32
-    )
 
     batch = queries.shape[0]
     near = ("y", "xh", "xl")
@@ -406,16 +481,8 @@
     part = jnp.sum(spread(part, "z", 8), axis=0)
     part = spread(part, near, 16).reshape(batch, HALF)
     back = shift(part, "c", 2, 1)
-    left = jnp.where(core == 0, part, back)
-    right = jnp.where(core == 0, back, part)
-    rest = width - HALF
-    lanes = (2 * HALF - width) // 2
-    total_labels = owned * ndp * nmp
-    factor = total_labels / jnp.sum(right[:, rest + lanes])
-    scale = factor / root
-    loss = factor * jnp.sum(right[:, rest]) / (batch * total_labels)
-    query_grad = scale * jnp.concatenate([left, right[:, :rest]], axis=1)
-    return (scale * label_part, query_grad, loss)
+    label_grad, query_grad, loss = final(core, part, back, slopes, queries, owned * ndp * nmp)
+    return (label_grad, query_grad, loss[0, 0])
 
 
 def solution(mesh):

time: 277 us -> 268 us (0.968)
  blocking collectives: 84.1 us -> 58.3 us
  waiting for transfers between devices: 64.9 us -> 83.2 us
  Pallas kernels: 14.4 us -> 24.5 us
  starting transfers between devices: 30.3 us -> 26.2 us
    all_gather x1 -> x0, blocking collectives: 25.9 us -> none  [shards(): a_all = lax.all_gather(a_y.reshape(-1, CUT), 'z', axis=0, tiled=True)]
    all_gather x0 -> x1, waiting for transfers between devices: none -> 10.5 us  [shards(): a_all = lax.all_gather(a_y.reshape(-1, CUT), 'z', axis=0, tiled=True)]
    unnamed x79 -> x44, local copies, waits for them, and re-layouts: 18.6 us -> 9.12 us
    all_gather x1, waiting for transfers between devices: 22.5 us -> 29.8 us  [shards(): far_z = lax.all_gather(moved[:, CUT:], 'z', axis=0, tiled=True)]
    optimization_barrier x0 -> x1, local copies, waits for them, and re-layouts: none -> 5.92 us  [shards(): moved, hidden_states = lax.optimization_barrier((moved, hidden_states))]
    pallas_call x2, Pallas kernels: 7.89 us -> 13.6 us  [project(): pl.pallas_call(project_kernel, out_shape=jax.ShapeDtypeStruct((tokens, co...]
    ppermute x15, starting transfers between devices: 19.5 us -> 15.8 us  [shift(): return lax.ppermute(x, axis, [(i, (i + by) % size) for i in range(size)])]
    pallas_call x0 -> x1, Pallas kernels: none -> 3.22 us  [final(): pl.pallas_call(functools.partial(final_kernel, labels=labels), out_shape=...]
  transfers between devices with their start and end apart: 20 -> 21, of which waited for: 10 -> 12; matrix products, arithmetic and copies ran while one was open for 16% -> 17% of each run, Pallas kernels for 1% -> 3%
where the time goes in v3:
time: 268 us; the launch traced here: 265 us
  waiting for transfers between devices  83.2 us (31%)
  blocking collectives  58.3 us (22%)
  local copies, waits for them, and re-layouts  30 us (11%)
  starting transfers between devices  26.2 us (10%)
  Pallas kernels  24.5 us (9%)
  other arithmetic  23.2 us (9%)
  between operations  14.5 us (5%)
  matrix products  5.14 us (2%)
    all_to_all x2, blocking collectives, spread(): lax.all_to_all(jnp.broadcast_to(x[None], (size,) + x.shape), axes, 0, 0,...  38 us
    ppermute x15, waiting for transfers between devices, shift(): return lax.ppermute(x, axis, [(i, (i + by) % size) for i in range(size)])  34.6 us
    all_gather x1, waiting for transfers between devices, shards(): far_z = lax.all_gather(moved[:, CUT:], 'z', axis=0, tiled=True)  29.8 us
    all_to_all x1, blocking collectives, shards(): lax.all_to_all(part.reshape(16, batch // 16, HALF), near, 0, 0, tiled=True)  20.3 us
    ppermute x15, starting transfers between devices, shift(): return lax.ppermute(x, axis, [(i, (i + by) % size) for i in range(size)])  15.8 us
    pallas_call x2, Pallas kernels, project(): pl.pallas_call(project_kernel, out_shape=jax.ShapeDtypeStruct((tokens, co...  13.6 us
    all_gather x1, waiting for transfers between devices, shards(): a_all = lax.all_gather(a_y.reshape(-1, CUT), 'z', axis=0, tiled=True)  10.5 us
    unnamed x44, local copies, waits for them, and re-layouts  9.12 us
  transfers between devices with their start and end apart: 21, of which 12 were waited for; matrix products, arithmetic and copies ran while one was open for 17% of the time, Pallas kernels for 3%

profile of v3, /device:TPU:2, one launch (start us, length us, event | category | flops | bytes accessed | tf_op | source)
XLA Modules:
  0.0 265.0 jit_solution(10807783287810135024)
XLA Ops:
  8.3 3.4 %collective-permute-start = (bf16[56,2048]{1,0:T(8,128)(2,1)S(1)}, bf16[56,2048]{1,0:T(8,128)(2,1)S(1)}, u32[]{:S(2)}, u32[]{:S(2)}) collective-permute-start(bf16[56,2048]{1,0:T(8,128)(2,1)S(1)} %pad_maximum_fusion), channel_id=1, source_target_pairs={{0,0},{1,2},{2,4},{3,6},{4,1},{5,3},{6,5},{7,7},{8,8},{9,10},{10,1... | collective-permute-start | bytes 688136 | tf_op jit(solution)/shard_map/ppermute | solution.py:359
  19.0 3.1 %collective-permute-start.1 = (bf16[56,384]{1,0:T(8,128)(2,1)S(1)}, bf16[56,384]{1,0:T(8,128)(2,1)S(1)}, u32[]{:S(2)}, u32[]{:S(2)}) collective-permute-start(bf16[56,384]{1,0:T(8,128)(2,1)S(1)} %slice.27), channel_id=1, source_target_pairs={{0,24},{8,0},{16,8},{24,16},{1,25},{9,1},{17,9},{25,17},{2,26},{10... | collective-permute-start | bytes 129032 | tf_op jit(solution)/shard_map/ppermute | solution.py:185
  24.3 5.9 %copy.57 = bf16[512,3584]{0,1:T(8,128)(2,1)} copy(bf16[512,3584]{1,0:T(8,128)(2,1)} %param.16) | data formatting | bytes 7340032 | tf_op jit(solution)/shard_map/optimization_barrier | solution.py:365
  30.4 3.0 %fusion = f32[512]{0:T(512)S(1)} fusion(bf16[512,3584]{0,1:T(8,128)(2,1)} %copy.57), kind=kLoop, calls=%fused_computation.2 | loop fusion | flops 5504512 | bytes 3672064 | tf_op jit(solution)/shard_map/reduce_sum | solution.py:408
  43.0 29.8 %all-gather.5.cloned.1.call-done = bf16[448,1664]{1,0:T(8,128)(2,1)} async-done(((bf16[56,1664]{1,0:T(8,128)(2,1)}), bf16[448,1664]{1,0:T(8,128)(2,1)}) %all-gather.5.cloned.1.call-update) | async-done | bytes 1490960 | tf_op jit(solution)/shard_map/all_gather | solution.py:367
  74.0 2.8 %collective-permute-start.4 = (bf16[448,768]{1,0:T(8,128)(2,1)S(1)}, bf16[448,768]{1,0:T(8,128)(2,1)}, u32[]{:S(2)}, u32[]{:S(2)}) collective-permute-start(bf16[448,768]{1,0:T(8,128)(2,1)S(1)} %slice.36.b0_ref), channel_id=1, source_target_pairs={{0,24},{8,0},{16,8},{24,16},{1,25},{9,1},{17,9},{25,17},{2,26},{10... | collective-permute-start | bytes 2064392 | tf_op jit(solution)/shard_map/ppermute | solution.py:185
  82.3 6.2 %collective-permute-done.4.b1_ref = bf16[448,768]{1,0:T(8,128)(2,1)} collective-permute-done((bf16[448,768]{1,0:T(8,128)(2,1)S(1)}, bf16[448,768]{1,0:T(8,128)(2,1)}, u32[]{:S(2)}, u32[]{:S(2)}) %collective-permute-start.4) | collective-permute-done | bytes 688160 | tf_op jit(solution)/shard_map/ppermute | solution.py:185
  89.4 3.0 %collective-permute-start.5 = (bf16[224,768]{1,0:T(8,128)(2,1)S(1)}, bf16[224,768]{1,0:T(8,128)(2,1)S(1)}, u32[]{:S(2)}, u32[]{:S(2)}) collective-permute-start(bf16[224,768]{1,0:T(8,128)(2,1)S(1)} %slice.37), channel_id=1, source_target_pairs={{0,24},{8,0},{16,8},{24,16},{1,25},{9,1},{17,9},{25,17},{2,26},{10... | collective-permute-start | bytes 1032200 | tf_op jit(solution)/shard_map/ppermute | solution.py:185
  99.9 2.4 collective-permute-done.7.b2b_ref
  102.3 10.5 %all-gather.3.cloned.1.call-done.a_ref = bf16[1792,384]{1,0:T(8,128)(2,1)} async-done(((bf16[224,384]{1,0:T(8,128)(2,1)}), bf16[1792,384]{1,0:T(8,128)(2,1)}) %all-gather.3.cloned.1.call-update) | async-done | bytes 1376272 | tf_op jit(solution)/shard_map/all_gather | solution.py:370
  112.8 6.8 %project.3 = f32[512,1152]{1,0:T(8,128)} custom-call(s32[1]{0:T(128)} %bitcast.20.place_ref, bf16[1792,512]{1,0:T(8,128)(2,1)} %copy-done.5, bf16[4,448,512]{2,1,0:T(8,128)(2,1)} %bitcast.61, bf16[1792,384]{1,0:T(8,128)(2,1)} %all-gather.3.cloned.1.call-done.a_ref, bf16[448,768]{1,0:T(8,128)(2,1)} %copy-done.6, ...), custom_call_target="tpu_custom_call" | custom-call | flops 2113929216 | bytes 10158080 | tf_op jit(solution)/shard_map/project/pallas_call | solution.py:68
  120.6 2.7 %collective-permute-start.10 = (bf16[448,896]{1,0:T(8,128)(2,1)S(1)}, bf16[448,896]{1,0:T(8,128)(2,1)S(1)}, u32[]{:S(2)}, u32[]{:S(2)}) collective-permute-start(bf16[448,896]{1,0:T(8,128)(2,1)S(1)} %get-tuple-element.85), channel_id=1, source_target_pairs={{0,24},{8,0},{16,8},{24,16},{1,25},{9,1},{17,9},{25,17},{2,26},{10... | collective-permute-start | bytes 2408456 | tf_op jit(solution)/shard_map/ppermute | solution.py:185
  123.3 6.8 %project.2.raw_ref = f32[512,1152]{1,0:T(8,128)} custom-call(s32[1]{0:T(128)} %bitcast.20.place_ref, bf16[1792,512]{1,0:T(8,128)(2,1)} %copy-done.4, bf16[4,448,512]{2,1,0:T(8,128)(2,1)} %bitcast.60, bf16[1792,384]{1,0:T(8,128)(2,1)} %all-gather.3.cloned.1.call-done.a_ref, bf16[448,768]{1,0:T(8,128)(2,1)} %copy-done.6, ...), custom_call_target="tpu_custom_call" | custom-call | flops 2113929216 | bytes 10158080 | tf_op jit(solution)/shard_map/project/pallas_call | solution.py:68
  130.1 11.0 %collective-permute-done.10 = bf16[448,896]{1,0:T(8,128)(2,1)S(1)} collective-permute-done((bf16[448,896]{1,0:T(8,128)(2,1)S(1)}, bf16[448,896]{1,0:T(8,128)(2,1)S(1)}, u32[]{:S(2)}, u32[]{:S(2)}) %collective-permute-start.10) | collective-permute-done | bytes 802848 | tf_op jit(solution)/shard_map/ppermute | solution.py:185
  141.2 3.4 %collective-permute-done.11 = bf16[448,896]{1,0:T(8,128)(2,1)S(1)} collective-permute-done((bf16[448,896]{1,0:T(8,128)(2,1)S(1)}, bf16[448,896]{1,0:T(8,128)(2,1)S(1)}, u32[]{:S(2)}, u32[]{:S(2)}) %collective-permute-start.11) | collective-permute-done | bytes 802848 | tf_op jit(solution)/shard_map/ppermute | solution.py:185
  151.2 5.1 %collective-permute-done.14 = bf16[224,896]{1,0:T(8,128)(2,1)} collective-permute-done((bf16[224,896]{1,0:T(8,128)(2,1)}, bf16[224,896]{1,0:T(8,128)(2,1)}, u32[]{:S(2)}, u32[]{:S(2)}) %collective-permute-start.14) | collective-permute-done | bytes 401440 | tf_op jit(solution)/shard_map/ppermute | solution.py:185
  159.3 5.8 %attend.1 = f32[32,896]{1,0:T(8,128)} custom-call(f32[512,1152]{1,0:T(8,128)} %project.2.raw_ref, f32[512,1152]{1,0:T(8,128)} %collective-permute-done.12.add_ref, f32[512,128]{1,0:T(8,128)} %bitcast.63, f32[512,1]{1,0:T(8,128)} %copy.60.live_ref, bf16[56,896]{1,0:T(8,128)(2,1)} %constant.103.clone.member_ref, f32[128,128]{1,0:T(8,128)} %constant.104.clone.cos_ref, ...), custom_call_target="tpu_custom_call" | custom-call | flops 234881024 | bytes 4718592 | tf_op jit(solution)/shard_map/attend/pallas_call | solution.py:152
  170.1 4.8 %all-to-all-start = ((f32[8,8,1792]{2,1,0:T(8,128)}), f32[8,8,1792]{2,1,0:T(8,128)S(1)}, u32[]{:S(2)}, u32[]{:S(2)}) async-start(f32[8,8,1792]{2,1,0:T(8,128)} %convolution_bitcast_fusion), calls=%async_computation | async-start | bytes 917504 | tf_op jit(solution)/shard_map/all_to_all | solution.py:454
  174.9 8.2 %all-to-all-done = f32[8,8,1792]{2,1,0:T(8,128)S(1)} async-done(((f32[8,8,1792]{2,1,0:T(8,128)}), f32[8,8,1792]{2,1,0:T(8,128)S(1)}, u32[]{:S(2)}, u32[]{:S(2)}) %all-to-all-start) | async-done | bytes 458784 | tf_op jit(solution)/shard_map/all_to_all | solution.py:454
  189.5 2.6 collective-permute-done.16
  192.1 20.3 %all_to_all.20 = f32[16,8,1920]{2,1,0:T(8,128)} all-to-all(f32[16,8,1920]{2,1,0:T(8,128)S(1)} %add_bitcast_fusion), channel_id=1, replica_groups=mesh['z'=8,'y'=4,'xh'=2,'xl'=2,'c'=2] {'y','xh','xl'}, dimensions={0} | all-to-all | bytes 1966080 | tf_op jit(solution)/shard_map/all_to_all | solution.py:479
  213.8 20.0 %all_to_all.21 = f32[8,8,1920]{2,1,0:T(8,128)S(1)} all-to-all(f32[8,8,1920]{2,1,0:T(8,128)S(1)} %broadcast_in_dim.92), channel_id=1, replica_groups=mesh['z'=8,'y'=4,'xh'=2,'xl'=2,'c'=2] {'z'}, dimensions={0} | all-to-all | bytes 983040 | tf_op jit(solution)/shard_map/all_to_all | solution.py:206
  233.9 18.0 %all_to_all.22 = f32[16,8,1920]{2,1,0:T(8,128)S(1)} all-to-all(f32[16,8,1920]{2,1,0:T(8,128)S(1)} %broadcast_in_dim.93), channel_id=1, replica_groups=mesh['z'=8,'y'=4,'xh'=2,'xl'=2,'c'=2] {'y','xh','xl'}, dimensions={0} | all-to-all | bytes 1966080 | tf_op jit(solution)/shard_map/all_to_all | solution.py:206
  254.4 3.2 %final.1 = (f32[256,3584]{1,0:T(8,128)}, f32[128,3584]{1,0:T(8,128)}, f32[8,128]{1,0:T(8,128)S(1)}) custom-call(s32[1]{0:T(128)} %bitcast.core_ref, f32[128,1920]{1,0:T(8,128)S(1)} %bitcast.55, f32[128,1920]{1,0:T(8,128)S(1)} %collective-permute-done.17.back_ref, bf16[256,128]{1,0:T(8,128)(2,1)S(1)} %bitcast_add_fusion.slopes_ref, ...), custom_call_target="tpu_custom_call" | custom-call | tf_op jit(solution)/shard_map/final/pallas_call | solution.py:308
  (137 shorter events, 61.5 us)
Async XLA Ops:
  7.2 32.1 %copy-start = (bf16[256,3584]{1,0:T(8,128)(2,1)S(1)}, bf16[256,3584]{1,0:T(8,128)(2,1)}, u32[]{:S(2)}) copy-start(bf16[256,3584]{1,0:T(8,128)(2,1)} %param.23) | copy-start | bytes 5505028
  7.2 65.7 %all-gather.5.cloned.1.call-start = ((), (), s32[]{:S(2)}) async-start(), calls=%async_computation.5 | async-start | bytes 1677312 | tf_op jit(solution)/shard_map/all_gather | solution.py:367
  8.3 10.6 %collective-permute-start = (bf16[56,2048]{1,0:T(8,128)(2,1)S(1)}, bf16[56,2048]{1,0:T(8,128)(2,1)S(1)}, u32[]{:S(2)}, u32[]{:S(2)}) collective-permute-start(bf16[56,2048]{1,0:T(8,128)(2,1)S(1)} %pad_maximum_fusion), channel_id=1, source_target_pairs={{0,0},{1,2},{2,4},{3,6},{4,1},{5,3},{6,5},{7,7},{8,8},{9,10},{10,1... | collective-permute-start | bytes 688136 | tf_op jit(solution)/shard_map/ppermute | solution.py:359
  11.7 66.5 %collective-permute-start.8 = (s32[32,16]{0,1:T(8,128)}, s32[32,16]{0,1:T(8,128)S(1)}, u32[]{:S(2)}, u32[]{:S(2)}) collective-permute-start(s32[32,16]{0,1:T(8,128)} %param.17), channel_id=1, source_target_pairs={{0,6},{2,4},{4,2},{6,0},{1,7},{3,5},{5,3},{7,1},{8,14},{10,12},{12... | collective-permute-start | bytes 6152 | tf_op jit(solution)/shard_map/ppermute | solution.py:423
  19.0 19.5 %collective-permute-start.1 = (bf16[56,384]{1,0:T(8,128)(2,1)S(1)}, bf16[56,384]{1,0:T(8,128)(2,1)S(1)}, u32[]{:S(2)}, u32[]{:S(2)}) collective-permute-start(bf16[56,384]{1,0:T(8,128)(2,1)S(1)} %slice.27), channel_id=1, source_target_pairs={{0,24},{8,0},{16,8},{24,16},{1,25},{9,1},{17,9},{25,17},{2,26},{10... | collective-permute-start | bytes 129032 | tf_op jit(solution)/shard_map/ppermute | solution.py:185
  22.1 16.4 %collective-permute-start.2 = (bf16[56,384]{1,0:T(8,128)(2,1)S(1)}, bf16[56,384]{1,0:T(8,128)(2,1)S(1)}, u32[]{:S(2)}, u32[]{:S(2)}) collective-permute-start(bf16[56,384]{1,0:T(8,128)(2,1)S(1)} %slice.27), channel_id=1, source_target_pairs={{0,16},{8,24},{16,0},{24,8},{1,17},{9,25},{17,1},{25,9},{2,18},{10... | collective-permute-start | bytes 129032 | tf_op jit(solution)/shard_map/ppermute | solution.py:185
  22.7 15.8 %collective-permute-start.3 = (bf16[56,384]{1,0:T(8,128)(2,1)S(1)}, bf16[56,384]{1,0:T(8,128)(2,1)S(1)}, u32[]{:S(2)}, u32[]{:S(2)}) collective-permute-start(bf16[56,384]{1,0:T(8,128)(2,1)S(1)} %slice.27), channel_id=1, source_target_pairs={{0,8},{8,16},{16,24},{24,0},{1,9},{9,17},{17,25},{25,1},{2,10},{10... | collective-permute-start | bytes 129032 | tf_op jit(solution)/shard_map/ppermute | solution.py:185
  30.3 82.5 %all-gather.3.cloned.1.call-start = ((), (), s32[]{:S(2)}) async-start(), calls=%async_computation.4 | async-start | bytes 1548288 | tf_op jit(solution)/shard_map/all_gather | solution.py:370
  36.4 57.3 %collective-permute-start.9 = (bf16[1792,512]{1,0:T(8,128)(2,1)}, bf16[1792,512]{1,0:T(8,128)(2,1)}, u32[]{:S(2)}, u32[]{:S(2)}) collective-permute-start(bf16[1792,512]{1,0:T(8,128)(2,1)} %bitcast.13), channel_id=1, source_target_pairs={{0,6},{2,4},{4,2},{6,0},{1,7},{3,5},{5,3},{7,1},{8,14},{10,12},{12... | collective-permute-start | bytes 5505032 | tf_op jit(solution)/shard_map/ppermute | solution.py:422
  40.7 37.5 %copy-start.17 = (s32[32,16]{0,1:T(8,128)S(1)}, s32[32,16]{0,1:T(8,128)}, u32[]{:S(2)}) copy-start(s32[32,16]{0,1:T(8,128)} %param.17) | copy-start | bytes 6148
  74.0 14.4 %collective-permute-start.4 = (bf16[448,768]{1,0:T(8,128)(2,1)S(1)}, bf16[448,768]{1,0:T(8,128)(2,1)}, u32[]{:S(2)}, u32[]{:S(2)}) collective-permute-start(bf16[448,768]{1,0:T(8,128)(2,1)S(1)} %slice.36.b0_ref), channel_id=1, source_target_pairs={{0,24},{8,0},{16,8},{24,16},{1,25},{9,1},{17,9},{25,17},{2,26},{10... | collective-permute-start | bytes 2064392 | tf_op jit(solution)/shard_map/ppermute | solution.py:185
  76.8 15.6 %collective-permute-start.6 = (bf16[448,768]{1,0:T(8,128)(2,1)S(1)}, bf16[448,768]{1,0:T(8,128)(2,1)}, u32[]{:S(2)}, u32[]{:S(2)}) collective-permute-start(bf16[448,768]{1,0:T(8,128)(2,1)S(1)} %slice.36.b0_ref), channel_id=1, source_target_pairs={{0,8},{8,16},{16,24},{24,0},{1,9},{9,17},{17,25},{25,1},{2,10},{10... | collective-permute-start | bytes 2064392 | tf_op jit(solution)/shard_map/ppermute | solution.py:185
  89.4 9.7 %collective-permute-start.5 = (bf16[224,768]{1,0:T(8,128)(2,1)S(1)}, bf16[224,768]{1,0:T(8,128)(2,1)S(1)}, u32[]{:S(2)}, u32[]{:S(2)}) collective-permute-start(bf16[224,768]{1,0:T(8,128)(2,1)S(1)} %slice.37), channel_id=1, source_target_pairs={{0,24},{8,0},{16,8},{24,16},{1,25},{9,1},{17,9},{25,17},{2,26},{10... | collective-permute-start | bytes 1032200 | tf_op jit(solution)/shard_map/ppermute | solution.py:185
  93.4 8.8 %collective-permute-start.7 = (bf16[224,768]{1,0:T(8,128)(2,1)S(1)}, bf16[224,768]{1,0:T(8,128)(2,1)}, u32[]{:S(2)}, u32[]{:S(2)}) collective-permute-start(bf16[224,768]{1,0:T(8,128)(2,1)S(1)} %slice.38), channel_id=1, source_target_pairs={{0,8},{8,16},{16,24},{24,0},{1,9},{9,17},{17,25},{25,1},{2,10},{10... | collective-permute-start | bytes 1032200 | tf_op jit(solution)/shard_map/ppermute | solution.py:185
  119.6 39.7 %collective-permute-start.12 = (f32[512,1152]{1,0:T(8,128)}, f32[512,1152]{1,0:T(8,128)}, u32[]{:S(2)}, u32[]{:S(2)}) collective-permute-start(f32[512,1152]{1,0:T(8,128)} %project.3), channel_id=1, source_target_pairs={{0,1},{1,0},{2,3},{3,2},{4,5},{5,4},{6,7},{7,6},{8,9},{9,8},{10,11... | collective-permute-start | bytes 7077896 | tf_op jit(solution)/shard_map/ppermute | solution.py:185
  120.6 20.5 %collective-permute-start.10 = (bf16[448,896]{1,0:T(8,128)(2,1)S(1)}, bf16[448,896]{1,0:T(8,128)(2,1)S(1)}, u32[]{:S(2)}, u32[]{:S(2)}) collective-permute-start(bf16[448,896]{1,0:T(8,128)(2,1)S(1)} %get-tuple-element.85), channel_id=1, source_target_pairs={{0,24},{8,0},{16,8},{24,16},{1,25},{9,1},{17,9},{25,17},{2,26},{10... | collective-permute-start | bytes 2408456 | tf_op jit(solution)/shard_map/ppermute | solution.py:185
  123.3 21.2 %collective-permute-start.11 = (bf16[448,896]{1,0:T(8,128)(2,1)S(1)}, bf16[448,896]{1,0:T(8,128)(2,1)S(1)}, u32[]{:S(2)}, u32[]{:S(2)}) collective-permute-start(bf16[448,896]{1,0:T(8,128)(2,1)S(1)} %get-tuple-element.85), channel_id=1, source_target_pairs={{0,8},{8,16},{16,24},{24,0},{1,9},{9,17},{17,25},{25,1},{2,10},{10... | collective-permute-start | bytes 2408456 | tf_op jit(solution)/shard_map/ppermute | solution.py:185
  145.4 10.9 %collective-permute-start.14 = (bf16[224,896]{1,0:T(8,128)(2,1)}, bf16[224,896]{1,0:T(8,128)(2,1)}, u32[]{:S(2)}, u32[]{:S(2)}) collective-permute-start(bf16[224,896]{1,0:T(8,128)(2,1)} %slice.33), channel_id=1, source_target_pairs={{0,24},{8,0},{16,8},{24,16},{1,25},{9,1},{17,9},{25,17},{2,26},{10... | collective-permute-start | bytes 1204232 | tf_op jit(solution)/shard_map/ppermute | solution.py:185
  146.5 12.1 %collective-permute-start.15 = (bf16[224,896]{1,0:T(8,128)(2,1)}, bf16[224,896]{1,0:T(8,128)(2,1)S(1)}, u32[]{:S(2)}, u32[]{:S(2)}) collective-permute-start(bf16[224,896]{1,0:T(8,128)(2,1)} %slice.34), channel_id=1, source_target_pairs={{0,8},{8,16},{16,24},{24,0},{1,9},{9,17},{17,25},{25,1},{2,10},{10... | collective-permute-start | bytes 1204232 | tf_op jit(solution)/shard_map/ppermute | solution.py:185
  166.1 1.2 collective-permute-start.13
  170.1 13.0 %all-to-all-start = ((f32[8,8,1792]{2,1,0:T(8,128)}), f32[8,8,1792]{2,1,0:T(8,128)S(1)}, u32[]{:S(2)}, u32[]{:S(2)}) async-start(f32[8,8,1792]{2,1,0:T(8,128)} %convolution_bitcast_fusion), calls=%async_computation | async-start | bytes 917504 | tf_op jit(solution)/shard_map/all_to_all | solution.py:454
  189.1 2.9 %collective-permute-start.16 = (f32[128,1920]{1,0:T(8,128)S(1)}, f32[128,1920]{1,0:T(8,128)S(1)}, u32[]{:S(2)}, u32[]{:S(2)}) collective-permute-start(f32[128,1920]{1,0:T(8,128)S(1)} %get-tuple-element.70), channel_id=1, source_target_pairs={{0,1},{1,0},{2,3},{3,2},{4,5},{5,4},{6,7},{7,6},{8,9},{9,8},{10,11... | collective-permute-start | bytes 2949128 | tf_op jit(solution)/shard_map/ppermute | solution.py:185
  212.5 39.4 %copy-start.16 = (bf16[128,256]{0,1:T(8,128)(2,1)S(1)}, bf16[128,256]{0,1:T(8,128)(2,1)}, u32[]{:S(2)}) copy-start(bf16[128,256]{0,1:T(8,128)(2,1)} %copy-done.15) | copy-start | bytes 196612
  251.9 2.6 collective-permute-start.17
  (17 other events, 105.1 us)
Sparse Core Ops, SparseCore 0:
  30.4 42.3 all-gather.4
  74.6 38.1 all-gather.2

commit v4 on v3

--- a/solution.py
+++ b/solution.py
@@ -23,7 +23,7 @@
 
 
 BLOCK = 128
-CUT = 384
+SENT = 1280
 HALF = 1920
 
 
@@ -40,31 +40,28 @@
     )
 
 
-def project_kernel(place_ref, whole_ref, part_ref, a_ref, b0_ref, b1_ref, b2a_ref, b2b_ref, b3_ref, out_ref):
-    contract = (((0,), (0,)), ((), ()))
-
+def project_kernel(place_ref, x_ref, w0_ref, w1_ref, w2a_ref, w2b_ref, w3_ref, out_ref):
     def dot(x, w):
-        return lax.dot_general(x, w, contract, preferred_element_type=jnp.float32)
+        return lax.dot_general(
+            x, w, (((0,), (0,)), ((), ())), preferred_element_type=jnp.float32
+        )
 
     y = place_ref[0]
-    cut = a_ref.shape[1]
-    half = b2a_ref.shape[0]
-    out_ref[:, :cut] = dot(whole_ref[...], a_ref[...])
-    far = part_ref[(y + 2) % 4]
-    out_ref[:, cut:] = (
-        dot(part_ref[y], b0_ref[...])
-        + dot(part_ref[(y + 1) % 4], b1_ref[...])
-        + dot(part_ref[(y + 3) % 4], b3_ref[...])
-        + dot(far[:half], b2a_ref[...])
-        + dot(far[half:], b2b_ref[...])
-    )
-
-
-def project(y, whole, part, a_all, pieces):
-    depth, tokens = whole.shape
-    columns = a_all.shape[1] + pieces[0].shape[1]
+    half = w2a_ref.shape[0]
+    far = x_ref[(y + 2) % 4]
+    out_ref[...] = (
+        dot(x_ref[y], w0_ref[...])
+        + dot(x_ref[(y + 1) % 4], w1_ref[...])
+        + dot(x_ref[(y + 3) % 4], w3_ref[...])
+        + dot(far[:half], w2a_ref[...])
+        + dot(far[half:], w2b_ref[...])
+    )
+
+
+def project(y, x, pieces):
+    _, depth, tokens = x.shape
+    columns = pieces[0].shape[1]
     block = tokens // 2
-    fixed = [pl.BlockSpec(w.shape, lambda i, _: (0, 0)) for w in (a_all, *pieces)]
     return pl.pallas_call(
         project_kernel,
         out_shape=jax.ShapeDtypeStruct((tokens, columns), jnp.float32),
@@ -72,20 +69,19 @@
             num_scalar_prefetch=1,
             grid=(tokens // block,),
             in_specs=[
-                pl.BlockSpec((depth, block), lambda i, _: (0, i)),
-                pl.BlockSpec((4, depth // 4, block), lambda i, _: (0, 0, i)),
-                *fixed,
+                pl.BlockSpec((4, depth, block), lambda i, _: (0, 0, i)),
+                *[pl.BlockSpec(w.shape, lambda i, _: (0, 0)) for w in pieces],
             ],
             out_specs=pl.BlockSpec((block, columns), lambda i, _: (i, 0)),
         ),
         compiler_params=pltpu.CompilerParams(vmem_limit_bytes=56 << 20),
         cost_estimate=pl.CostEstimate(
-            flops=2 * depth * tokens * columns,
-            bytes_accessed=4 * tokens * columns + 2 * depth * (2 * tokens + columns),
+            flops=8 * depth * tokens * columns,
+            bytes_accessed=4 * tokens * columns + 8 * depth * (tokens + columns),
             transcendentals=0,
         ),
         name="project",
-    )(y.reshape(1).astype(jnp.int32), whole, part, a_all, *pieces)
+    )(y.reshape(1).astype(jnp.int32), x, *pieces)
 
 
 def attend_kernel(raw_ref, add_ref, allowed_ref, live_ref, member_ref, cos_ref, sin_ref, out_ref):
@@ -362,18 +358,15 @@
         [(4 * h + 2 * l + k, 4 * l + 2 * k + h) for h in (0, 1) for l in (0, 1) for k in (0, 1)],
     )
     cut = packed.shape[1] - out_weight.shape[1]
-    moved, hidden_states = lax.optimization_barrier((moved, hidden_states))
     y = lax.axis_index("y")
-    far_z = lax.all_gather(moved[:, CUT:], "z", axis=0, tiled=True)
-    part_a = moved[:, :CUT]
-    a_y = in_order([part_a] + [shift(part_a, "y", 4, -d) for d in (1, 2, 3)], y)
-    a_all = lax.all_gather(a_y.reshape(-1, CUT), "z", axis=0, tiled=True)
-    own = far_z[:, : cut - CUT]
+    in_z = lax.all_gather(moved[:, :SENT], "z", axis=0, tiled=True)
+    out_part = moved[:, cut:]
+    out_y = in_order([out_part] + [shift(out_part, "y", 4, -d) for d in (1, 2, 3)], y)
+    out_y, hidden_states = lax.optimization_barrier((out_y, hidden_states))
+    out_all = lax.all_gather(out_y.reshape(4 * rows, -1), "z", axis=0, tiled=True)
+    own = in_z[:, :cut]
     up, down = ring_near(own)
     pieces = (own, up, *ring_far(up, down), down)
-    far_z, pieces = lax.optimization_barrier((far_z, pieces))
-    out_own = far_z[:, cut - CUT :]
-    out_up, out_down = ring_near(out_own)
 
     balance = (1.0 - focal_beta) / -jnp.expm1(
         label_counts.astype(f32) * math.log(focal_beta)
@@ -432,14 +425,12 @@
     allowed, live_rows = attend_tables(ids)
     sums = jnp.stack([kept_loss, jnp.sum(balance)])
     early = (kept_query, kept_slopes, sums, new_balance, new_signs, chosen, states_sum, counted)
-    early = early + (allowed, live_rows, give, keep, by_y(give), by_y(keep))
-    (a_all, pieces, early) = lax.optimization_barrier((a_all, pieces, early))
+    early = early + (allowed, live_rows, by_y(give), by_y(keep))
+    pieces, early = lax.optimization_barrier((pieces, early))
     kept_query, kept_slopes, sums, new_balance, new_signs, chosen, states_sum, counted = early[:8]
-    allowed, live_rows, give, keep, give_y, keep_y = early[8:]
-    taken = shift(project(y, give, give_y, a_all, pieces), "c", 2, 1)
-    raw = project(y, keep, keep_y, a_all, pieces)
-    raw, out_up, out_down = lax.optimization_barrier((raw, out_up, out_down))
-    out_far = ring_far(out_up, out_down)
+    allowed, live_rows, give, keep = early[8:]
+    taken = shift(project(y, give, pieces), "c", 2, 1)
+    raw = project(y, keep, pieces)
     pooled = attend_pooled(raw, taken, allowed, live_rows, length).astype(bf16)
 
     pooled_other = shift(pooled, "c", 2, 1)
@@ -447,7 +438,6 @@
         [jnp.where(core == 0, pooled, pooled_other), jnp.where(core == 0, pooled_other, pooled)],
         axis=0,
     )
-    out_all = jnp.concatenate([out_own, out_up, *out_far, out_down], axis=0)
     head_terms = lax.dot_general(
         both, out_all, (((1,), (1,)), ((), ())), preferred_element_type=f32
     )
@@ -455,10 +445,8 @@
         head_terms.reshape(8, share, -1), ("xh", "xl", "c"), 0, 0, tiled=True
     )
     summed = jnp.sum(exchanged.reshape(nmp, 2, share, -1), axis=0)
-    blocks = summed.reshape(2, share, 4, 8 * rows)
-    turned = lax.dynamic_slice_in_dim(jnp.concatenate([blocks, blocks], axis=2), 4 - y, 4, 2)
     output_own = (
-        turned.reshape(2, share, 4, 8, rows).transpose(1, 3, 2, 0, 4).reshape(share, width)
+        summed.reshape(2, share, ndp // 2, rows).transpose(1, 2, 0, 3).reshape(share, width)
     )
     refreshed = ((states_sum + output_own) / counted).astype(bf16)
 

time: 268 us -> 224 us (0.84)
  waiting for transfers between devices: 83.2 us -> 43.6 us
  blocking collectives: 58.3 us -> 71.6 us
  starting transfers between devices: 26.2 us -> 16.9 us
  local copies, waits for them, and re-layouts: 30 us -> 22.4 us
    all_gather x2, waiting for transfers between devices: 40.4 us -> 12.3 us  [the longest x1 12.3 us: shards(): in_z = lax.all_gather(moved[:, :SENT], 'z', axis=0, tiled=True)]
    all_to_all x0 -> x1, blocking collectives: none -> 12.8 us  [shards(): lax.all_to_all(head_terms.reshape(8, share, -1), ('xh', 'xl', 'c'), 0, 0,...]
    all_to_all x1 -> x0, waiting for transfers between devices: 8.19 us -> none  [shards(): lax.all_to_all(head_terms.reshape(8, share, -1), ('xh', 'xl', 'c'), 0, 0,...]
    unnamed x44 -> x19, local copies, waits for them, and re-layouts: 9.12 us -> 3.13 us
    all_to_all x1 -> x0, starting transfers between devices: 4.81 us -> none  [shards(): lax.all_to_all(head_terms.reshape(8, share, -1), ('xh', 'xl', 'c'), 0, 0,...]
    ppermute x15 -> x11, starting transfers between devices: 15.8 us -> 11.4 us  [shift(): return lax.ppermute(x, axis, [(i, (i + by) % size) for i in range(size)])]
    ppermute x15 -> x11, waiting for transfers between devices: 34.6 us -> 30.3 us  [shift(): return lax.ppermute(x, axis, [(i, (i + by) % size) for i in range(size)])]
  transfers between devices with their start and end apart: 21 -> 16, of which waited for: 12 -> 11; matrix products, arithmetic and copies ran while one was open for 17% -> 18% of each run, Pallas kernels for 3% -> 9%
where the time goes in v4:
time: 224 us; the launch traced here: 221 us
  blocking collectives  71.6 us (32%)
  waiting for transfers between devices  43.6 us (19%)
  Pallas kernels  24.1 us (11%)
  local copies, waits for them, and re-layouts  22.4 us (10%)
  other arithmetic  22 us (10%)
  starting transfers between devices  16.9 us (8%)
  between operations  14.4 us (6%)
  matrix products  6.28 us (3%)
    all_to_all x2, blocking collectives, spread(): lax.all_to_all(jnp.broadcast_to(x[None], (size,) + x.shape), axes, 0, 0,...  38.4 us
    ppermute x11, waiting for transfers between devices, shift(): return lax.ppermute(x, axis, [(i, (i + by) % size) for i in range(size)])  30.3 us
    all_to_all x1, blocking collectives, shards(): lax.all_to_all(part.reshape(16, batch // 16, HALF), near, 0, 0, tiled=True)  20.3 us
    pallas_call x2, Pallas kernels, project(): pl.pallas_call(project_kernel, out_shape=jax.ShapeDtypeStruct((tokens, co...  13.3 us
    all_to_all x1, blocking collectives, shards(): lax.all_to_all(head_terms.reshape(8, share, -1), ('xh', 'xl', 'c'), 0, 0,...  12.8 us
    all_gather x1, waiting for transfers between devices, shards(): in_z = lax.all_gather(moved[:, :SENT], 'z', axis=0, tiled=True)  12.3 us
    ppermute x11, starting transfers between devices, shift(): return lax.ppermute(x, axis, [(i, (i + by) % size) for i in range(size)])  11.4 us
    optimization_barrier x1, local copies, waits for them, and re-layouts, shards(): out_y, hidden_states = lax.optimization_barrier((out_y, hidden_states))  6.08 us
  transfers between devices with their start and end apart: 16, of which 11 were waited for; matrix products, arithmetic and copies ran while one was open for 18% of the time, Pallas kernels for 9%

profile of v4, /device:TPU:2, one launch (start us, length us, event | category | flops | bytes accessed | tf_op | source)
XLA Modules:
  0.0 221.1 jit_solution(12218579391080431713)
XLA Ops:
  8.3 3.4 %collective-permute-start = (bf16[56,2048]{1,0:T(8,128)(2,1)S(1)}, bf16[56,2048]{1,0:T(8,128)(2,1)S(1)}, u32[]{:S(2)}, u32[]{:S(2)}) collective-permute-start(bf16[56,2048]{1,0:T(8,128)(2,1)S(1)} %pad_maximum_fusion), channel_id=1, source_target_pairs={{0,0},{1,2},{2,4},{3,6},{4,1},{5,3},{6,5},{7,7},{8,8},{9,10},{10,1... | collective-permute-start | bytes 688136 | tf_op jit(solution)/shard_map/ppermute | solution.py:355
  19.2 3.1 %collective-permute-start.5 = (bf16[56,896]{1,0:T(8,128)(2,1)S(1)}, bf16[56,896]{1,0:T(8,128)(2,1)S(1)}, u32[]{:S(2)}, u32[]{:S(2)}) collective-permute-start(bf16[56,896]{1,0:T(8,128)(2,1)S(1)} %slice.28), channel_id=1, source_target_pairs={{0,24},{8,0},{16,8},{24,16},{1,25},{9,1},{17,9},{25,17},{2,26},{10... | collective-permute-start | bytes 301064 | tf_op jit(solution)/shard_map/ppermute | solution.py:181
  24.0 2.5 %collective-permute-done.5 = bf16[56,896]{1,0:T(8,128)(2,1)S(1)} collective-permute-done((bf16[56,896]{1,0:T(8,128)(2,1)S(1)}, bf16[56,896]{1,0:T(8,128)(2,1)S(1)}, u32[]{:S(2)}, u32[]{:S(2)}) %collective-permute-start.5) | collective-permute-done | bytes 100384 | tf_op jit(solution)/shard_map/ppermute | solution.py:181
  26.5 2.6 %collective-permute-done.6 = bf16[56,896]{1,0:T(8,128)(2,1)S(1)} collective-permute-done((bf16[56,896]{1,0:T(8,128)(2,1)S(1)}, bf16[56,896]{1,0:T(8,128)(2,1)S(1)}, u32[]{:S(2)}, u32[]{:S(2)}) %collective-permute-start.6) | collective-permute-done | bytes 100384 | tf_op jit(solution)/shard_map/ppermute | solution.py:181
  30.2 6.1 %copy.42 = bf16[512,3584]{0,1:T(8,128)(2,1)} copy(bf16[512,3584]{1,0:T(8,128)(2,1)} %param.16) | data formatting | bytes 7340032 | tf_op jit(solution)/shard_map/optimization_barrier | solution.py:365
  36.3 2.9 %fusion = f32[512]{0:T(512)S(1)} fusion(bf16[512,3584]{0,1:T(8,128)(2,1)} %copy.42), kind=kLoop, calls=%fused_computation.2 | loop fusion | flops 5504512 | bytes 3672064 | tf_op jit(solution)/shard_map/reduce_sum | solution.py:401
  39.2 3.1 %fusion.2 = bf16[512,3584]{0,1:T(8,128)(2,1)S(1)} fusion(bf16[512,3584]{0,1:T(8,128)(2,1)} %copy.42, f32[3584]{0:T(1024)S(1)} %copy-done.7, f32[512]{0:T(512)S(1)} %add_rsqrt_fusion), kind=kLoop, calls=%fused_computation.4 | loop fusion | flops 7340032 | bytes 7356416 | tf_op jit(solution)/shard_map/convert_element_type | solution.py:402
  47.4 12.3 %all-gather.3.cloned.1.call-done = bf16[448,1280]{1,0:T(8,128)(2,1)} async-done(((bf16[56,1280]{1,0:T(8,128)(2,1)}), bf16[448,1280]{1,0:T(8,128)(2,1)}) %all-gather.3.cloned.1.call-update) | async-done | bytes 1146896 | tf_op jit(solution)/shard_map/all_gather | solution.py:362
  61.9 2.8 %collective-permute-start.1 = (bf16[448,1152]{1,0:T(8,128)(2,1)}, bf16[448,1152]{1,0:T(8,128)(2,1)}, u32[]{:S(2)}, u32[]{:S(2)}) collective-permute-start(bf16[448,1152]{1,0:T(8,128)(2,1)} %slice.25.w0_ref), channel_id=1, source_target_pairs={{0,24},{8,0},{16,8},{24,16},{1,25},{9,1},{17,9},{25,17},{2,26},{10... | collective-permute-start | bytes 3096584 | tf_op jit(solution)/shard_map/ppermute | solution.py:181
  70.6 13.2 %collective-permute-done.1.w1_ref = bf16[448,1152]{1,0:T(8,128)(2,1)} collective-permute-done((bf16[448,1152]{1,0:T(8,128)(2,1)}, bf16[448,1152]{1,0:T(8,128)(2,1)}, u32[]{:S(2)}, u32[]{:S(2)}) %collective-permute-start.1) | collective-permute-done | bytes 1032224 | tf_op jit(solution)/shard_map/ppermute | solution.py:181
  84.9 3.1 %collective-permute-start.2 = (bf16[224,1152]{1,0:T(8,128)(2,1)S(1)}, bf16[224,1152]{1,0:T(8,128)(2,1)S(1)}, u32[]{:S(2)}, u32[]{:S(2)}) collective-permute-start(bf16[224,1152]{1,0:T(8,128)(2,1)S(1)} %slice.26), channel_id=1, source_target_pairs={{0,24},{8,0},{16,8},{24,16},{1,25},{9,1},{17,9},{25,17},{2,26},{10... | collective-permute-start | bytes 1548296 | tf_op jit(solution)/shard_map/ppermute | solution.py:181
  89.3 2.3 %broadcast_select_fusion = (bf16[1792,512]{1,0:T(8,128)(2,1)S(1)}, bf16[1792,512]{1,0:T(8,128)(2,1)S(1)}) fusion(bf16[1792,512]{1,0:T(8,128)(2,1)} %collective-permute-done.9, pred[]{:T(512)S(6)} %eq.60, bf16[32,1,56,512]{3,2,1,0:T(8,128)(2,1)} %constant_dynamic-slice_fusion), kind=kLoop, calls=%fused_computation.8 | loop fusion | flops 1835008 | bytes 7340033 | tf_op jit(solution)/shard_map/jit(_where)/select_n | solution.py:419
  94.5 5.0 %collective-permute-done.4.w2b_ref = bf16[224,1152]{1,0:T(8,128)(2,1)S(1)} collective-permute-done((bf16[224,1152]{1,0:T(8,128)(2,1)S(1)}, bf16[224,1152]{1,0:T(8,128)(2,1)S(1)}, u32[]{:S(2)}, u32[]{:S(2)}) %collective-permute-start.4) | collective-permute-done | bytes 516128 | tf_op jit(solution)/shard_map/ppermute | solution.py:181
  100.4 6.7 %project.3 = f32[512,1152]{1,0:T(8,128)} custom-call(s32[1]{0:T(128)} %bitcast.19.place_ref, bf16[4,448,512]{2,1,0:T(8,128)(2,1)} %bitcast.55, bf16[448,1152]{1,0:T(8,128)(2,1)} %slice.25.w0_ref, bf16[448,1152]{1,0:T(8,128)(2,1)} %collective-permute-done.1.w1_ref, bf16[224,1152]{1,0:T(8,128)(2,1)} %copy-done.3, bf16[224,1152]{1,0:T(8,128)(2,1)} %copy-done.4, ...), custom_call_target="tpu_custom_call" | custom-call | flops 2113929216 | bytes 8323072 | tf_op jit(solution)/shard_map/project/pallas_call | solution.py:65
  107.9 6.6 %project.2.raw_ref = f32[512,1152]{1,0:T(8,128)} custom-call(s32[1]{0:T(128)} %bitcast.19.place_ref, bf16[4,448,512]{2,1,0:T(8,128)(2,1)} %bitcast.54, bf16[448,1152]{1,0:T(8,128)(2,1)} %slice.25.w0_ref, bf16[448,1152]{1,0:T(8,128)(2,1)} %collective-permute-done.1.w1_ref, bf16[224,1152]{1,0:T(8,128)(2,1)} %copy-done.3, bf16[224,1152]{1,0:T(8,128)(2,1)} %copy-done.4, ...), custom_call_target="tpu_custom_call" | custom-call | flops 2113929216 | bytes 8323072 | tf_op jit(solution)/shard_map/project/pallas_call | solution.py:65
  114.6 5.7 %attend.1 = f32[32,896]{1,0:T(8,128)} custom-call(f32[512,1152]{1,0:T(8,128)} %project.2.raw_ref, f32[512,1152]{1,0:T(8,128)} %collective-permute-done.10.add_ref, f32[512,128]{1,0:T(8,128)} %bitcast.60, f32[512,1]{1,0:T(8,128)} %copy.45.live_ref, bf16[56,896]{1,0:T(8,128)(2,1)} %constant.101.clone.member_ref, f32[128,128]{1,0:T(8,128)} %constant.102.clone.cos_ref, ...), custom_call_target="tpu_custom_call" | custom-call | flops 234881024 | bytes 4718592 | tf_op jit(solution)/shard_map/attend/pallas_call | solution.py:148
  123.5 3.0 %convolution_bitcast_fusion = f32[8,8,1792]{2,1,0:T(8,128)S(1)} fusion(bf16[1792,896]{1,0:T(8,128)(2,1)} %all-gather.5.cloned.1.call-done, bf16[32,896]{1,0:T(8,128)(2,1)S(1)} %get-tuple-element.64, bf16[32,896]{1,0:T(8,128)(2,1)S(1)} %get-tuple-element.63), kind=kOutput, calls=%fused_computation.5 | convolution fusion | flops 205750272 | bytes 3784704 | tf_op jit(solution)/shard_map/dot_general | solution.py:441
  126.5 12.8 %all_to_all.20 = f32[8,8,1792]{2,1,0:T(8,128)S(1)} all-to-all(f32[8,8,1792]{2,1,0:T(8,128)S(1)} %convolution_bitcast_fusion), channel_id=1, replica_groups=mesh['z'=8,'y'=4,'xh'=2,'xl'=2,'c'=2] {'xh','xl','c'}, dimensions={0} | all-to-all | bytes 917504 | tf_op jit(solution)/shard_map/all_to_all | solution.py:444
  145.2 2.6 %collective-permute-done.12 = f32[128,1920]{1,0:T(8,128)S(1)} collective-permute-done((f32[128,1920]{1,0:T(8,128)S(1)}, f32[128,1920]{1,0:T(8,128)S(1)}, u32[]{:S(2)}, u32[]{:S(2)}) %collective-permute-start.12) | collective-permute-done | bytes 983072 | tf_op jit(solution)/shard_map/ppermute | solution.py:181
  147.9 20.3 %all_to_all.21 = f32[16,8,1920]{2,1,0:T(8,128)} all-to-all(f32[16,8,1920]{2,1,0:T(8,128)S(1)} %add_bitcast_fusion), channel_id=1, replica_groups=mesh['z'=8,'y'=4,'xh'=2,'xl'=2,'c'=2] {'y','xh','xl'}, dimensions={0} | all-to-all | bytes 1966080 | tf_op jit(solution)/shard_map/all_to_all | solution.py:467
  169.5 20.4 %all_to_all.22 = f32[8,8,1920]{2,1,0:T(8,128)S(1)} all-to-all(f32[8,8,1920]{2,1,0:T(8,128)S(1)} %broadcast_in_dim.92), channel_id=1, replica_groups=mesh['z'=8,'y'=4,'xh'=2,'xl'=2,'c'=2] {'z'}, dimensions={0} | all-to-all | bytes 983040 | tf_op jit(solution)/shard_map/all_to_all | solution.py:202
  190.1 18.0 %all_to_all.23 = f32[16,8,1920]{2,1,0:T(8,128)S(1)} all-to-all(f32[16,8,1920]{2,1,0:T(8,128)S(1)} %broadcast_in_dim.93), channel_id=1, replica_groups=mesh['z'=8,'y'=4,'xh'=2,'xl'=2,'c'=2] {'y','xh','xl'}, dimensions={0} | all-to-all | bytes 1966080 | tf_op jit(solution)/shard_map/all_to_all | solution.py:202
  208.2 2.3 %collective-permute-done.13.back_ref = f32[128,1920]{1,0:T(8,128)S(1)} collective-permute-done((f32[128,1920]{1,0:T(8,128)S(1)}, f32[128,1920]{1,0:T(8,128)S(1)}, u32[]{:S(2)}, u32[]{:S(2)}) %collective-permute-start.13) | collective-permute-done | bytes 983072 | tf_op jit(solution)/shard_map/ppermute | solution.py:181
  210.6 3.2 %final.1 = (f32[256,3584]{1,0:T(8,128)}, f32[128,3584]{1,0:T(8,128)}, f32[8,128]{1,0:T(8,128)S(1)}) custom-call(s32[1]{0:T(128)} %bitcast.core_ref, f32[128,1920]{1,0:T(8,128)S(1)} %bitcast.51, f32[128,1920]{1,0:T(8,128)S(1)} %collective-permute-done.13.back_ref, bf16[256,128]{1,0:T(8,128)(2,1)S(1)} %bitcast_add_fusion.slopes_ref, ...), custom_call_target="tpu_custom_call" | custom-call | tf_op jit(solution)/shard_map/final/pallas_call | solution.py:304
  (96 shorter events, 42.7 us)
Async XLA Ops:
  7.2 38.8 %copy-start = (bf16[256,3584]{1,0:T(8,128)(2,1)S(1)}, bf16[256,3584]{1,0:T(8,128)(2,1)}, u32[]{:S(2)}) copy-start(bf16[256,3584]{1,0:T(8,128)(2,1)} %param.23) | copy-start | bytes 5505028
  7.2 52.5 %all-gather.3.cloned.1.call-start = ((), (), s32[]{:S(2)}) async-start(), calls=%async_computation.4 | async-start | bytes 1290240 | tf_op jit(solution)/shard_map/all_gather | solution.py:362
  8.3 7.3 %collective-permute-start = (bf16[56,2048]{1,0:T(8,128)(2,1)S(1)}, bf16[56,2048]{1,0:T(8,128)(2,1)S(1)}, u32[]{:S(2)}, u32[]{:S(2)}) collective-permute-start(bf16[56,2048]{1,0:T(8,128)(2,1)S(1)} %pad_maximum_fusion), channel_id=1, source_target_pairs={{0,0},{1,2},{2,4},{3,6},{4,1},{5,3},{6,5},{7,7},{8,8},{9,10},{10,1... | collective-permute-start | bytes 688136 | tf_op jit(solution)/shard_map/ppermute | solution.py:355
  11.7 56.2 %collective-permute-start.8 = (s32[32,16]{0,1:T(8,128)}, s32[32,16]{0,1:T(8,128)S(1)}, u32[]{:S(2)}, u32[]{:S(2)}) collective-permute-start(s32[32,16]{0,1:T(8,128)} %param.17), channel_id=1, source_target_pairs={{0,6},{2,4},{4,2},{6,0},{1,7},{3,5},{5,3},{7,1},{8,14},{10,12},{12... | collective-permute-start | bytes 6152 | tf_op jit(solution)/shard_map/ppermute | solution.py:416
  16.4 107.1 %all-gather.5.cloned.1.call-start = ((), (), s32[]{:S(2)}) async-start(), calls=%async_computation.5 | async-start | bytes 3612672 | tf_op jit(solution)/shard_map/all_gather | solution.py:366
  19.2 7.3 %collective-permute-start.5 = (bf16[56,896]{1,0:T(8,128)(2,1)S(1)}, bf16[56,896]{1,0:T(8,128)(2,1)S(1)}, u32[]{:S(2)}, u32[]{:S(2)}) collective-permute-start(bf16[56,896]{1,0:T(8,128)(2,1)S(1)} %slice.28), channel_id=1, source_target_pairs={{0,24},{8,0},{16,8},{24,16},{1,25},{9,1},{17,9},{25,17},{2,26},{10... | collective-permute-start | bytes 301064 | tf_op jit(solution)/shard_map/ppermute | solution.py:181
  22.3 6.9 %collective-permute-start.6 = (bf16[56,896]{1,0:T(8,128)(2,1)S(1)}, bf16[56,896]{1,0:T(8,128)(2,1)S(1)}, u32[]{:S(2)}, u32[]{:S(2)}) collective-permute-start(bf16[56,896]{1,0:T(8,128)(2,1)S(1)} %slice.28), channel_id=1, source_target_pairs={{0,16},{8,24},{16,0},{24,8},{1,17},{9,25},{17,1},{25,9},{2,18},{10... | collective-permute-start | bytes 301064 | tf_op jit(solution)/shard_map/ppermute | solution.py:181
  22.9 7.2 %collective-permute-start.7 = (bf16[56,896]{1,0:T(8,128)(2,1)S(1)}, bf16[56,896]{1,0:T(8,128)(2,1)S(1)}, u32[]{:S(2)}, u32[]{:S(2)}) collective-permute-start(bf16[56,896]{1,0:T(8,128)(2,1)S(1)} %slice.28), channel_id=1, source_target_pairs={{0,8},{8,16},{16,24},{24,0},{1,9},{9,17},{17,25},{25,1},{2,10},{10... | collective-permute-start | bytes 301064 | tf_op jit(solution)/shard_map/ppermute | solution.py:181
  30.2 6.1 %copy-start.5 = (bf16[4,56,896]{2,1,0:T(8,128)(2,1)}, bf16[4,56,896]{2,1,0:T(8,128)(2,1)S(1)}, u32[]{:S(2)}) copy-start(bf16[4,56,896]{2,1,0:T(8,128)(2,1)S(1)} %bitcast_dynamic-update-slice_fusion) | copy-start | bytes 1204228
  36.3 3.0 %copy-start.7 = (f32[3584]{0:T(1024)S(1)}, f32[3584]{0:T(1024)}, u32[]{:S(2)}) copy-start(f32[3584]{0:T(1024)} %param.18) | copy-start | bytes 43012
  42.3 3.3 %copy-start.6 = (s32[32,16]{0,1:T(8,128)S(1)}, s32[32,16]{0,1:T(8,128)}, u32[]{:S(2)}) copy-start(s32[32,16]{0,1:T(8,128)} %param.17) | copy-start | bytes 6148
  42.4 3.7 %copy-start.2 = (bf16[128,3584]{1,0:T(8,128)(2,1)S(1)}, bf16[128,3584]{1,0:T(8,128)(2,1)}, u32[]{:S(2)}) copy-start(bf16[128,3584]{1,0:T(8,128)(2,1)} %queries_ref.3) | copy-start | bytes 2752516
  43.7 45.5 %collective-permute-start.9 = (bf16[1792,512]{1,0:T(8,128)(2,1)}, bf16[1792,512]{1,0:T(8,128)(2,1)}, u32[]{:S(2)}, u32[]{:S(2)}) collective-permute-start(bf16[1792,512]{1,0:T(8,128)(2,1)} %bitcast.12), channel_id=1, source_target_pairs={{0,6},{2,4},{4,2},{6,0},{1,7},{3,5},{5,3},{7,1},{8,14},{10,12},{12... | collective-permute-start | bytes 5505032 | tf_op jit(solution)/shard_map/ppermute | solution.py:415
  61.9 21.8 %collective-permute-start.1 = (bf16[448,1152]{1,0:T(8,128)(2,1)}, bf16[448,1152]{1,0:T(8,128)(2,1)}, u32[]{:S(2)}, u32[]{:S(2)}) collective-permute-start(bf16[448,1152]{1,0:T(8,128)(2,1)} %slice.25.w0_ref), channel_id=1, source_target_pairs={{0,24},{8,0},{16,8},{24,16},{1,25},{9,1},{17,9},{25,17},{2,26},{10... | collective-permute-start | bytes 3096584 | tf_op jit(solution)/shard_map/ppermute | solution.py:181
  64.7 23.2 %collective-permute-start.3 = (bf16[448,1152]{1,0:T(8,128)(2,1)}, bf16[448,1152]{1,0:T(8,128)(2,1)}, u32[]{:S(2)}, u32[]{:S(2)}) collective-permute-start(bf16[448,1152]{1,0:T(8,128)(2,1)} %slice.25.w0_ref), channel_id=1, source_target_pairs={{0,8},{8,16},{16,24},{24,0},{1,9},{9,17},{17,25},{25,1},{2,10},{10... | collective-permute-start | bytes 3096584 | tf_op jit(solution)/shard_map/ppermute | solution.py:181
  64.7 3.5 %copy-start.8 = (pred[128,128]{1,0:T(32,128)(4,1)S(1)}, pred[128,128]{1,0:T(32,128)(4,1)}, u32[]{:S(2)}) copy-start(pred[128,128]{1,0:T(32,128)(4,1)} %constant.100.clone) | copy-start | bytes 49156
  84.9 9.7 %collective-permute-start.2 = (bf16[224,1152]{1,0:T(8,128)(2,1)S(1)}, bf16[224,1152]{1,0:T(8,128)(2,1)S(1)}, u32[]{:S(2)}, u32[]{:S(2)}) collective-permute-start(bf16[224,1152]{1,0:T(8,128)(2,1)S(1)} %slice.26), channel_id=1, source_target_pairs={{0,24},{8,0},{16,8},{24,16},{1,25},{9,1},{17,9},{25,17},{2,26},{10... | collective-permute-start | bytes 1548296 | tf_op jit(solution)/shard_map/ppermute | solution.py:181
  89.0 10.6 %collective-permute-start.4 = (bf16[224,1152]{1,0:T(8,128)(2,1)S(1)}, bf16[224,1152]{1,0:T(8,128)(2,1)S(1)}, u32[]{:S(2)}, u32[]{:S(2)}) collective-permute-start(bf16[224,1152]{1,0:T(8,128)(2,1)S(1)} %slice.27), channel_id=1, source_target_pairs={{0,8},{8,16},{16,24},{24,0},{1,9},{9,17},{17,25},{25,1},{2,10},{10... | collective-permute-start | bytes 1548296 | tf_op jit(solution)/shard_map/ppermute | solution.py:181
  94.5 5.0 %copy-start.3 = (bf16[224,1152]{1,0:T(8,128)(2,1)}, bf16[224,1152]{1,0:T(8,128)(2,1)S(1)}, u32[]{:S(2)}) copy-start(bf16[224,1152]{1,0:T(8,128)(2,1)S(1)} %collective-permute-done.2.w2a_ref) | copy-start | bytes 1548292
  107.1 7.5 %collective-permute-start.10 = (f32[512,1152]{1,0:T(8,128)}, f32[512,1152]{1,0:T(8,128)}, u32[]{:S(2)}, u32[]{:S(2)}) collective-permute-start(f32[512,1152]{1,0:T(8,128)} %project.3), channel_id=1, source_target_pairs={{0,1},{1,0},{2,3},{3,2},{4,5},{5,4},{6,7},{7,6},{8,9},{9,8},{10,11... | collective-permute-start | bytes 7077896 | tf_op jit(solution)/shard_map/ppermute | solution.py:181
  121.2 1.4 collective-permute-start.11
  141.7 1.5 copy-start.1
  145.1 2.7 %collective-permute-start.12 = (f32[128,1920]{1,0:T(8,128)S(1)}, f32[128,1920]{1,0:T(8,128)S(1)}, u32[]{:S(2)}, u32[]{:S(2)}) collective-permute-start(f32[128,1920]{1,0:T(8,128)S(1)} %get-tuple-element.46), channel_id=1, source_target_pairs={{0,1},{1,0},{2,3},{3,2},{4,5},{5,4},{6,7},{7,6},{8,9},{9,8},{10,11... | collective-permute-start | bytes 2949128 | tf_op jit(solution)/shard_map/ppermute | solution.py:181
  208.0 2.6 %collective-permute-start.13 = (f32[128,1920]{1,0:T(8,128)S(1)}, f32[128,1920]{1,0:T(8,128)S(1)}, u32[]{:S(2)}, u32[]{:S(2)}) collective-permute-start(f32[128,1920]{1,0:T(8,128)S(1)} %bitcast.50), channel_id=1, source_target_pairs={{0,1},{1,0},{2,3},{3,2},{4,5},{5,4},{6,7},{7,6},{8,9},{9,8},{10,11... | collective-permute-start | bytes 2949128 | tf_op jit(solution)/shard_map/ppermute | solution.py:181
  (1 other events, 0.8 us)
Sparse Core Ops, SparseCore 0:
  16.5 43.1 all-gather.2
  61.4 44.2 all-gather.4

commit v5 on v4

--- a/solution.py
+++ b/solution.py
@@ -23,7 +23,6 @@
 
 
 BLOCK = 128
-SENT = 1280
 HALF = 1920
 
 
@@ -40,48 +39,104 @@
     )
 
 
-def project_kernel(place_ref, x_ref, w0_ref, w1_ref, w2a_ref, w2b_ref, w3_ref, out_ref):
+def norm_kernel(core_ref, states_ref, gain_ref, out_ref, turned_ref):
+    states = states_ref[...].astype(jnp.float32)
+    scaled = lax.rsqrt(jnp.mean(states * states, axis=1, keepdims=True) + norm_eps)
+    turned_ref[...] = (states * scaled * gain_ref[...]).T
+    rows = out_ref.shape[1] // 8
+
+    def block(z, y):
+        first = pl.multiple_of(((z * 4 + y) * 2 + core_ref[0]) * rows, 8)
+        return turned_ref[pl.ds(first, rows), :]
+
+    for y in range(4):
+        for pair in range(4):
+            out_ref[y, 2 * pair * rows : 2 * (pair + 1) * rows, :] = jnp.concatenate(
+                [block(2 * pair, y), block(2 * pair + 1, y)], axis=0
+            ).astype(jnp.bfloat16)
+
+
+def norm_half(core, states, gain):
+    tokens, width = states.shape
+    block = 128
+    return pl.pallas_call(
+        norm_kernel,
+        out_shape=jax.ShapeDtypeStruct((4, width // 8, tokens), jnp.bfloat16),
+        grid_spec=pltpu.PrefetchScalarGridSpec(
+            num_scalar_prefetch=1,
+            grid=(tokens // block,),
+            in_specs=[
+                pl.BlockSpec((block, width), lambda i, _: (i, 0)),
+                pl.BlockSpec((1, width), lambda i, _: (0, 0)),
+            ],
+            out_specs=pl.BlockSpec((4, width // 8, block), lambda i, _: (0, 0, i)),
+            scratch_shapes=[pltpu.VMEM((width, block), jnp.float32)],
+        ),
+        compiler_params=pltpu.CompilerParams(vmem_limit_bytes=32 << 20),
+        cost_estimate=pl.CostEstimate(
+            flops=4 * tokens * width, bytes_accessed=3 * tokens * width, transcendentals=tokens
+        ),
+        name="norm",
+    )(core.reshape(1).astype(jnp.int32), states, gain.reshape(1, width))
+
+
+def near_kernel(place_ref, x_ref, w0_ref, w1_ref, w3_ref, out_ref):
     def dot(x, w):
         return lax.dot_general(
             x, w, (((0,), (0,)), ((), ())), preferred_element_type=jnp.float32
         )
 
     y = place_ref[0]
-    half = w2a_ref.shape[0]
-    far = x_ref[(y + 2) % 4]
     out_ref[...] = (
         dot(x_ref[y], w0_ref[...])
         + dot(x_ref[(y + 1) % 4], w1_ref[...])
         + dot(x_ref[(y + 3) % 4], w3_ref[...])
-        + dot(far[:half], w2a_ref[...])
-        + dot(far[half:], w2b_ref[...])
-    )
-
-
-def project(y, x, pieces):
+    )
+
+
+def far_kernel(place_ref, x_ref, near_ref, w2a_ref, w2b_ref, out_ref):
+    def dot(x, w):
+        return lax.dot_general(
+            x, w, (((0,), (0,)), ((), ())), preferred_element_type=jnp.float32
+        )
+
+    half = w2a_ref.shape[0]
+    far = x_ref[0]
+    out_ref[...] = (
+        near_ref[...] + dot(far[:half], w2a_ref[...]) + dot(far[half:], w2b_ref[...])
+    ).astype(out_ref.dtype)
+
+
+def project(y, x, pieces, near=None, dtype=jnp.float32):
     _, depth, tokens = x.shape
     columns = pieces[0].shape[1]
     block = tokens // 2
+    fixed = [pl.BlockSpec(w.shape, lambda i, _: (0, 0)) for w in pieces]
+    tile = pl.BlockSpec((block, columns), lambda i, _: (i, 0))
+    if near is None:
+        kernel, extra = near_kernel, ()
+        x_spec = pl.BlockSpec((4, depth, block), lambda i, _: (0, 0, i))
+    else:
+        kernel, extra = far_kernel, (near,)
+        x_spec = pl.BlockSpec((1, depth, block), lambda i, p: ((p[0] + 2) % 4, 0, i))
+    used = sum(w.shape[0] for w in pieces)
     return pl.pallas_call(
-        project_kernel,
-        out_shape=jax.ShapeDtypeStruct((tokens, columns), jnp.float32),
+        kernel,
+        out_shape=jax.ShapeDtypeStruct((tokens, columns), dtype),
         grid_spec=pltpu.PrefetchScalarGridSpec(
             num_scalar_prefetch=1,
             grid=(tokens // block,),
-            in_specs=[
-                pl.BlockSpec((4, depth, block), lambda i, _: (0, 0, i)),
-                *[pl.BlockSpec(w.shape, lambda i, _: (0, 0)) for w in pieces],
-            ],
-            out_specs=pl.BlockSpec((block, columns), lambda i, _: (i, 0)),
+            in_specs=[x_spec, *[tile for _ in extra], *fixed],
+            out_specs=tile,
         ),
         compiler_params=pltpu.CompilerParams(vmem_limit_bytes=56 << 20),
         cost_estimate=pl.CostEstimate(
-            flops=8 * depth * tokens * columns,
-            bytes_accessed=4 * tokens * columns + 8 * depth * (tokens + columns),
+            flops=2 * used * tokens * columns,
+            bytes_accessed=6 * tokens * columns + 2 * used * (tokens + columns),
             transcendentals=0,
         ),
-        name="project",
-    )(y.reshape(1).astype(jnp.int32), x, *pieces)
+        name="near" if near is None else "far",
+    )(y.reshape(1).astype(jnp.int32), x, *extra, *pieces)
 
 
 def attend_kernel(raw_ref, add_ref, allowed_ref, live_ref, member_ref, cos_ref, sin_ref, out_ref):
@@ -99,7 +154,7 @@
 
         def column(index):
             lanes = slice(index * width, (index + 1) * width)
-            return raw_ref[rows, lanes] + add_ref[rows, lanes]
+            return raw_ref[rows, lanes] + add_ref[rows, lanes].astype(jnp.float32)
 
         allowed = jnp.concatenate([allowed_ref[rows, :]] * heads, axis=0)
         live = jnp.concatenate([live_ref[rows, :]] * heads, axis=0)
@@ -119,9 +174,10 @@
             low, values, preferred_element_type=jnp.float32
         )
         for head in range(heads):
-            out_ref[block * texts : (block + 1) * texts, head * width : (head + 1) * width] = pooled[
+            columns = slice(head * width, (head + 1) * width)
+            out_ref[block * texts : (block + 1) * texts, columns] = pooled[
                 head * texts : (head + 1) * texts
-            ]
+            ].astype(out_ref.dtype)
 
 
 def attend_tables(text_ids):
@@ -147,7 +203,7 @@
     step = 2 * BLOCK
     return pl.pallas_call(
         attend_kernel,
-        out_shape=jax.ShapeDtypeStruct((texts, heads * HEAD_WIDTH), jnp.float32),
+        out_shape=jax.ShapeDtypeStruct((texts, heads * HEAD_WIDTH), jnp.bfloat16),
         grid=(tokens // step,),
         in_specs=[
             pl.BlockSpec((step, columns), lambda i: (i, 0)),
@@ -344,29 +400,41 @@
 ):
     f32, bf16 = jnp.float32, jnp.bfloat16
     width = hidden_states.shape[1]
-    group_tokens = hidden_states.shape[0]
     texts, length = token_ids.shape
     xh, core = lax.axis_index("xh"), lax.axis_index("c")
     member = lax.axis_index(MP)
     ndp, nmp = 64, 4
     rows = q_weight.shape[0]
 
-    packed = jnp.concatenate([key_matrix, value_matrix, q_weight, out_weight], axis=1)
-    moved = lax.ppermute(
-        packed,
-        ("xh", "xl", "c"),
-        [(4 * h + 2 * l + k, 4 * l + 2 * k + h) for h in (0, 1) for l in (0, 1) for k in (0, 1)],
-    )
-    cut = packed.shape[1] - out_weight.shape[1]
+    def to_group(block, by):
+        return lax.ppermute(
+            block,
+            ("y", "xh", "xl", "c"),
+            [
+                (8 * v + 4 * h + 2 * l + k, 8 * ((v - by) % 4) + 4 * l + 2 * k + h)
+                for v in range(4)
+                for h in (0, 1)
+                for l in (0, 1)
+                for k in (0, 1)
+            ],
+        )
+
     y = lax.axis_index("y")
-    in_z = lax.all_gather(moved[:, :SENT], "z", axis=0, tiled=True)
-    out_part = moved[:, cut:]
-    out_y = in_order([out_part] + [shift(out_part, "y", 4, -d) for d in (1, 2, 3)], y)
-    out_y, hidden_states = lax.optimization_barrier((out_y, hidden_states))
+    moved = to_group(jnp.concatenate([key_matrix, value_matrix, q_weight], axis=1), 0)
+    out_y = in_order([to_group(out_weight, d) for d in range(4)], y)
+    half = norm_half(core, hidden_states, norm_gain)
+    facing = [(i, 3 - i) for i in range(4)]
+    half_other = lax.ppermute(half, RING_X, facing)
+    ids_other = lax.ppermute(token_ids, RING_X, facing)
+    moved, half = lax.optimization_barrier((moved, half))
+    own = lax.all_gather(moved, "z", axis=0, tiled=True)
+    own, out_y = lax.optimization_barrier((own, out_y))
     out_all = lax.all_gather(out_y.reshape(4 * rows, -1), "z", axis=0, tiled=True)
-    own = in_z[:, :cut]
     up, down = ring_near(own)
-    pieces = (own, up, *ring_far(up, down), down)
+    far_a, far_b = ring_far(up, down)
+    rest = (positives, label_counts, refresh_rows, queries, token_ids)
+    half_other, rest = lax.optimization_barrier((half_other, rest))
+    positives, label_counts, refresh_rows, queries, token_ids = rest
 
     balance = (1.0 - focal_beta) / -jnp.expm1(
         label_counts.astype(f32) * math.log(focal_beta)
@@ -397,9 +465,6 @@
         -1.0,
     )
 
-    states = hidden_states.astype(f32)
-    scaled = lax.rsqrt(jnp.mean(states * states, axis=1, keepdims=True) + norm_eps)
-    normed = (states * scaled * norm_gain).astype(bf16)
     live = (token_ids != 0).astype(f32)
     share = texts // nmp
     live_own = lax.dynamic_slice_in_dim(live, member * share, share, 0)
@@ -409,29 +474,23 @@
     counted = jnp.sum(live_own, axis=1, keepdims=True)
     states_sum = jnp.sum(states_own.astype(f32) * live_own[:, :, None], axis=1)
 
-    half = normed.T.reshape(ndp // 2, 2, rows, group_tokens)
-    half = lax.dynamic_index_in_dim(half, core, 1, keepdims=False).reshape(-1, group_tokens)
-    facing = [(i, 3 - i) for i in range(4)]
-    half_other = lax.ppermute(half, RING_X, facing)
-    ids_other = lax.ppermute(token_ids, RING_X, facing)
     keeps = xh == core
     give = jnp.where(keeps, half_other, half)
     keep = jnp.where(keeps, half, half_other)
     ids = jnp.where(keeps, token_ids, ids_other)
 
-    def by_y(block):
-        return block.reshape(8, 4, rows, -1).transpose(1, 0, 2, 3).reshape(4, 8 * rows, -1)
-
     allowed, live_rows = attend_tables(ids)
     sums = jnp.stack([kept_loss, jnp.sum(balance)])
     early = (kept_query, kept_slopes, sums, new_balance, new_signs, chosen, states_sum, counted)
-    early = early + (allowed, live_rows, by_y(give), by_y(keep))
-    pieces, early = lax.optimization_barrier((pieces, early))
+    near = (own, up, down)
+    give_near, keep_near = project(y, give, near), project(y, keep, near)
+    early = early + (allowed, live_rows, give_near, keep_near)
+    far, early = lax.optimization_barrier(((far_a, far_b), early))
     kept_query, kept_slopes, sums, new_balance, new_signs, chosen, states_sum, counted = early[:8]
-    allowed, live_rows, give, keep = early[8:]
-    taken = shift(project(y, give, pieces), "c", 2, 1)
-    raw = project(y, keep, pieces)
-    pooled = attend_pooled(raw, taken, allowed, live_rows, length).astype(bf16)
+    allowed, live_rows, give_near, keep_near = early[8:]
+    taken = shift(project(y, give, far, give_near, bf16), "c", 2, 1)
+    raw = project(y, keep, far, keep_near)
+    pooled = attend_pooled(raw, taken, allowed, live_rows, length)
 
     pooled_other = shift(pooled, "c", 2, 1)
     both = jnp.concatenate(
@@ -442,9 +501,9 @@
         both, out_all, (((1,), (1,)), ((), ())), preferred_element_type=f32
     )
     exchanged = lax.all_to_all(
-        head_terms.reshape(8, share, -1), ("xh", "xl", "c"), 0, 0, tiled=True
-    )
-    summed = jnp.sum(exchanged.reshape(nmp, 2, share, -1), axis=0)
+        head_terms.astype(bf16).reshape(8, share, -1), ("xh", "xl", "c"), 0, 0, tiled=True
+    )
+    summed = jnp.sum(exchanged.astype(f32).reshape(nmp, 2, share, -1), axis=0)
     output_own = (
         summed.reshape(2, share, ndp // 2, rows).transpose(1, 2, 0, 3).reshape(share, width)
     )

time: 224 us -> 230 us (1.027)
  blocking collectives: 71.6 us -> 103 us
  waiting for transfers between devices: 43.6 us -> 24.3 us
  other arithmetic: 22 us -> 12.8 us
  Pallas kernels: 24.1 us -> 33.2 us
  local copies, waits for them, and re-layouts: 22.4 us -> 13.6 us
  starting transfers between devices: 16.9 us -> 19.6 us
    all_gather x0 -> x1, blocking collectives: none -> 32.5 us  [shards(): own = lax.all_gather(moved, 'z', axis=0, tiled=True)]
    all_gather x1 -> x0, waiting for transfers between devices: 12.3 us -> none  [shards(): in_z = lax.all_gather(moved[:, :SENT], 'z', axis=0, tiled=True)]
    pallas_call x2 -> x5, Pallas kernels: 13.3 us -> 22.8 us  [the longest x4 18.7 us: project(): pl.pallas_call(kernel, out_shape=jax.ShapeDtypeStruct((tokens, columns),...]
    ppermute x1 -> x5, starting transfers between devices: 3.4 us -> 11.7 us  [to_group(): lax.ppermute(block, ('y', 'xh', 'xl', 'c'), [(8 * v + 4 * h + 2 * l + k,...]
    ppermute x11 -> x8, waiting for transfers between devices: 30.3 us -> 24.2 us  [shift(): return lax.ppermute(x, axis, [(i, (i + by) % size) for i in range(size)])]
    optimization_barrier x2, local copies, waits for them, and re-layouts: 6.94 us -> 0.95 us  [the longest x1 0.85 us: shards(): far, early = lax.optimization_barrier(((far_a, far_b), early))]
    ppermute x11 -> x8, starting transfers between devices: 11.4 us -> 5.65 us  [shift(): return lax.ppermute(x, axis, [(i, (i + by) % size) for i in range(size)])]
    convert_element_type x2 -> x0, other arithmetic: 3.99 us -> none  [the longest x1 3.09 us: shards(): normed = (states * scaled * norm_gain).astype(bf16)]
  transfers between devices with their start and end apart: 16 -> 16, of which waited for: 11 -> 4; matrix products, arithmetic and copies ran while one was open for 18% -> 9% of each run, Pallas kernels for 9% -> 12%
where the time goes in v5:
time: 230 us; the launch traced here: 228 us
  blocking collectives  103 us (45%)
  Pallas kernels  33.2 us (14%)
  waiting for transfers between devices  24.3 us (11%)
  starting transfers between devices  19.6 us (9%)
  between operations  14.4 us (6%)
  local copies, waits for them, and re-layouts  13.6 us (6%)
  other arithmetic  12.8 us (6%)
  matrix products  6.27 us (3%)
    all_to_all x2, blocking collectives, spread(): lax.all_to_all(jnp.broadcast_to(x[None], (size,) + x.shape), axes, 0, 0,...  38.1 us
    all_gather x1, blocking collectives, shards(): own = lax.all_gather(moved, 'z', axis=0, tiled=True)  32.5 us
    ppermute x8, waiting for transfers between devices, shift(): return lax.ppermute(x, axis, [(i, (i + by) % size) for i in range(size)])  24.2 us
    all_to_all x1, blocking collectives, shards(): lax.all_to_all(part.reshape(16, batch // 16, HALF), near, 0, 0, tiled=True)  21.8 us
    pallas_call x4, Pallas kernels, project(): pl.pallas_call(kernel, out_shape=jax.ShapeDtypeStruct((tokens, columns),...  18.7 us
    ppermute x5, starting transfers between devices, to_group(): lax.ppermute(block, ('y', 'xh', 'xl', 'c'), [(8 * v + 4 * h + 2 * l + k,...  11.7 us
    all_to_all x1, blocking collectives, shards(): lax.all_to_all(head_terms.astype(bf16).reshape(8, share, -1), ('xh', 'xl'...  10.9 us
    ppermute x8, starting transfers between devices, shift(): return lax.ppermute(x, axis, [(i, (i + by) % size) for i in range(size)])  5.65 us
  transfers between devices with their start and end apart: 16, of which 4 were waited for; matrix products, arithmetic and copies ran while one was open for 9% of the time, Pallas kernels for 12%

profile of v5, /device:TPU:2, one launch (start us, length us, event | category | flops | bytes accessed | tf_op | source)
XLA Modules:
  0.0 227.5 jit_solution(18159160378042954248)
XLA Ops:
  7.2 3.5 %collective-permute-start.1 = (bf16[56,896]{1,0:T(8,128)(2,1)}, bf16[56,896]{1,0:T(8,128)(2,1)S(1)}, u32[]{:S(2)}, u32[]{:S(2)}) collective-permute-start(bf16[56,896]{1,0:T(8,128)(2,1)} %param.22), channel_id=1, source_target_pairs={{0,0},{1,2},{2,4},{3,6},{4,1},{5,3},{6,5},{7,7},{8,8},{9,10},{10,1... | collective-permute-start | bytes 301064 | tf_op jit(solution)/shard_map/ppermute | solution.py:410
  10.8 2.5 %collective-permute-start.2 = (bf16[56,896]{1,0:T(8,128)(2,1)}, bf16[56,896]{1,0:T(8,128)(2,1)S(1)}, u32[]{:S(2)}, u32[]{:S(2)}) collective-permute-start(bf16[56,896]{1,0:T(8,128)(2,1)} %param.22), channel_id=1, source_target_pairs={{0,24},{1,26},{2,28},{3,30},{4,25},{5,27},{6,29},{7,31},{8,0},{9,2... | collective-permute-start | bytes 301064 | tf_op jit(solution)/shard_map/ppermute | solution.py:410
  17.9 1.9 collective-permute-start
  20.7 2.0 copy-done.2
  22.7 4.1 %norm.1 = bf16[4,448,512]{2,1,0:T(8,128)(2,1)} custom-call(s32[1]{0:T(128)} %bitcast.core_ref, bf16[512,3584]{1,0:T(8,128)(2,1)S(1)} %copy-done.2, f32[1,3584]{1,0:T(1,128)S(1)} %reshape.74.gain_ref), custom_call_target="tpu_custom_call" | custom-call | flops 7340032 | bytes 5505024 | tf_op jit(solution)/shard_map/norm/pallas_call | solution.py:62
  28.8 32.5 %all_gather.6.w0_ref = bf16[448,1152]{1,0:T(8,128)(2,1)} all-gather(bf16[56,1152]{1,0:T(8,128)(2,1)S(1)} %collective-permute-done), channel_id=1, replica_groups=mesh['z'=8,'y'=4,'xh'=2,'xl'=2,'c'=2] {'z'}, dimensions={0}, use_global_device_ids=true | all-gather | bytes 1161216 | tf_op jit(solution)/shard_map/all_gather | solution.py:430
  61.3 2.3 collective-permute-start.5
  64.1 18.2 %collective-permute-done.5.w1_ref = bf16[448,1152]{1,0:T(8,128)(2,1)} collective-permute-done((bf16[448,1152]{1,0:T(8,128)(2,1)}, bf16[448,1152]{1,0:T(8,128)(2,1)}, u32[]{:S(2)}, u32[]{:S(2)}) %collective-permute-start.5) | collective-permute-done | bytes 1032224 | tf_op jit(solution)/shard_map/ppermute | solution.py:237
  82.3 1.9 slice.12
  84.2 2.8 %collective-permute-start.6 = (bf16[224,1152]{1,0:T(8,128)(2,1)}, bf16[224,1152]{1,0:T(8,128)(2,1)S(1)}, u32[]{:S(2)}, u32[]{:S(2)}) collective-permute-start(bf16[224,1152]{1,0:T(8,128)(2,1)} %slice.12), channel_id=1, source_target_pairs={{0,24},{8,0},{16,8},{24,16},{1,25},{9,1},{17,9},{25,17},{2,26},{10... | collective-permute-start | bytes 1548296 | tf_op jit(solution)/shard_map/ppermute | solution.py:237
  95.6 4.2 %broadcast_select_fusion = (bf16[4,448,512]{2,1,0:T(8,128)(2,1)}, bf16[4,448,512]{2,1,0:T(8,128)(2,1)}) fusion(bf16[4,448,512]{2,1,0:T(8,128)(2,1)} %norm.1, bf16[4,448,512]{2,1,0:T(8,128)(2,1)} %collective-permute-done.9, pred[]{:T(512)S(6)} %eq.60), kind=kLoop, calls=%fused_computation.4 | loop fusion | flops 1835008 | bytes 7340033 | tf_op jit(solution)/shard_map/jit(_where)/select_n | solution.py:479
  99.8 5.6 %near.3.near_ref = f32[512,1152]{1,0:T(8,128)} custom-call(s32[1]{0:T(128)} %bitcast.10.place_ref, bf16[4,448,512]{2,1,0:T(8,128)(2,1)} %get-tuple-element.69.x_ref, bf16[448,1152]{1,0:T(8,128)(2,1)} %all_gather.6.w0_ref, bf16[448,1152]{1,0:T(8,128)(2,1)} %collective-permute-done.5.w1_ref, bf16[448,1152]{1,0:T(8,128)(2,1)} %collective-permute-done.7.w3_ref), custom_call_target="tpu_custom_call" | custom-call | flops 1585446912 | bytes 8011776 | tf_op jit(solution)/shard_map/near/pallas_call | solution.py:123
  105.5 5.7 %near.2.near_ref = f32[512,1152]{1,0:T(8,128)} custom-call(s32[1]{0:T(128)} %bitcast.10.place_ref, bf16[4,448,512]{2,1,0:T(8,128)(2,1)} %get-tuple-element.70.x_ref, bf16[448,1152]{1,0:T(8,128)(2,1)} %all_gather.6.w0_ref, bf16[448,1152]{1,0:T(8,128)(2,1)} %collective-permute-done.5.w1_ref, bf16[448,1152]{1,0:T(8,128)(2,1)} %collective-permute-done.7.w3_ref), custom_call_target="tpu_custom_call" | custom-call | flops 1585446912 | bytes 8011776 | tf_op jit(solution)/shard_map/near/pallas_call | solution.py:123
  114.4 3.6 %far.3 = bf16[512,1152]{1,0:T(8,128)(2,1)} custom-call(s32[1]{0:T(128)} %bitcast.10.place_ref, bf16[4,448,512]{2,1,0:T(8,128)(2,1)} %get-tuple-element.70.x_ref, f32[512,1152]{1,0:T(8,128)} %near.2.near_ref, bf16[224,1152]{1,0:T(8,128)(2,1)} %copy-done.4, bf16[224,1152]{1,0:T(8,128)(2,1)} %collective-permute-done.8.w2b_ref), custom_call_target="tpu_custom_call" | custom-call | flops 528482304 | bytes 5029888 | tf_op jit(solution)/shard_map/far/pallas_call | solution.py:123
  118.8 3.8 %far.2.raw_ref = f32[512,1152]{1,0:T(8,128)} custom-call(s32[1]{0:T(128)} %bitcast.10.place_ref, bf16[4,448,512]{2,1,0:T(8,128)(2,1)} %get-tuple-element.69.x_ref, f32[512,1152]{1,0:T(8,128)} %near.3.near_ref, bf16[224,1152]{1,0:T(8,128)(2,1)} %copy-done.4, bf16[224,1152]{1,0:T(8,128)(2,1)} %collective-permute-done.8.w2b_ref), custom_call_target="tpu_custom_call" | custom-call | flops 528482304 | bytes 5029888 | tf_op jit(solution)/shard_map/far/pallas_call | solution.py:123
  122.7 5.3 %attend.1 = bf16[32,896]{1,0:T(8,128)(2,1)} custom-call(f32[512,1152]{1,0:T(8,128)} %far.2.raw_ref, bf16[512,1152]{1,0:T(8,128)(2,1)} %collective-permute-done.11.add_ref, f32[512,128]{1,0:T(8,128)} %bitcast.42, f32[512,1]{1,0:T(8,128)} %copy.39.live_ref, bf16[56,896]{1,0:T(8,128)(2,1)} %constant.92.clone.member_ref, f32[128,128]{1,0:T(8,128)} %constant.93.clone.cos_ref, ...), custom_call_target="tpu_custom_call" | custom-call | flops 234881024 | bytes 4718592 | tf_op jit(solution)/shard_map/attend/pallas_call | solution.py:204
  130.5 3.0 %fusion = bf16[8,8,1792]{2,1,0:T(8,128)(2,1)S(1)} fusion(bf16[1792,896]{1,0:T(8,128)(2,1)} %all-gather.2.cloned.1.call-done, bf16[32,896]{1,0:T(8,128)(2,1)S(1)} %get-tuple-element.74, bf16[32,896]{1,0:T(8,128)(2,1)S(1)} %get-tuple-element.73), kind=kOutput, calls=%fused_computation.1 | convolution fusion | flops 205864960 | bytes 3555328 | tf_op jit(solution)/shard_map/dot_general | solution.py:500
  133.4 10.9 %all_to_all.20 = bf16[8,8,1792]{2,1,0:T(8,128)(2,1)S(1)} all-to-all(bf16[8,8,1792]{2,1,0:T(8,128)(2,1)S(1)} %fusion), channel_id=1, replica_groups=mesh['z'=8,'y'=4,'xh'=2,'xl'=2,'c'=2] {'xh','xl','c'}, dimensions={0} | all-to-all | bytes 458752 | tf_op jit(solution)/shard_map/all_to_all | solution.py:503
  150.3 2.6 %collective-permute-done.13 = f32[128,1920]{1,0:T(8,128)S(1)} collective-permute-done((f32[128,1920]{1,0:T(8,128)S(1)}, f32[128,1920]{1,0:T(8,128)S(1)}, u32[]{:S(2)}, u32[]{:S(2)}) %collective-permute-start.13) | collective-permute-done | bytes 983072 | tf_op jit(solution)/shard_map/ppermute | solution.py:237
  153.0 21.8 %all_to_all.21 = f32[16,8,1920]{2,1,0:T(8,128)} all-to-all(f32[16,8,1920]{2,1,0:T(8,128)S(1)} %add_bitcast_fusion), channel_id=1, replica_groups=mesh['z'=8,'y'=4,'xh'=2,'xl'=2,'c'=2] {'y','xh','xl'}, dimensions={0} | all-to-all | bytes 1966080 | tf_op jit(solution)/shard_map/all_to_all | solution.py:526
  176.1 20.3 %all_to_all.22 = f32[8,8,1920]{2,1,0:T(8,128)S(1)} all-to-all(f32[8,8,1920]{2,1,0:T(8,128)S(1)} %broadcast_in_dim.90), channel_id=1, replica_groups=mesh['z'=8,'y'=4,'xh'=2,'xl'=2,'c'=2] {'z'}, dimensions={0} | all-to-all | bytes 983040 | tf_op jit(solution)/shard_map/all_to_all | solution.py:258
  196.6 17.8 %all_to_all.23 = f32[16,8,1920]{2,1,0:T(8,128)S(1)} all-to-all(f32[16,8,1920]{2,1,0:T(8,128)S(1)} %broadcast_in_dim.91), channel_id=1, replica_groups=mesh['z'=8,'y'=4,'xh'=2,'xl'=2,'c'=2] {'y','xh','xl'}, dimensions={0} | all-to-all | bytes 1966080 | tf_op jit(solution)/shard_map/all_to_all | solution.py:258
  214.6 2.3 %collective-permute-done.14.back_ref = f32[128,1920]{1,0:T(8,128)S(1)} collective-permute-done((f32[128,1920]{1,0:T(8,128)S(1)}, f32[128,1920]{1,0:T(8,128)S(1)}, u32[]{:S(2)}, u32[]{:S(2)}) %collective-permute-start.14) | collective-permute-done | bytes 983072 | tf_op jit(solution)/shard_map/ppermute | solution.py:237
  216.9 3.2 %final.1 = (f32[256,3584]{1,0:T(8,128)}, f32[128,3584]{1,0:T(8,128)}, f32[8,128]{1,0:T(8,128)S(1)}) custom-call(s32[1]{0:T(128)} %bitcast.core_ref, f32[128,1920]{1,0:T(8,128)S(1)} %bitcast.38, f32[128,1920]{1,0:T(8,128)S(1)} %collective-permute-done.14.back_ref, bf16[256,128]{1,0:T(8,128)(2,1)S(1)} %bitcast_add_fusion.slopes_ref, ...), custom_call_target="tpu_custom_call" | custom-call | tf_op jit(solution)/shard_map/final/pallas_call | solution.py:360
  (93 shorter events, 31.1 us)
Async XLA Ops:
  7.2 83.8 %copy-start = (bf16[256,3584]{1,0:T(8,128)(2,1)S(1)}, bf16[256,3584]{1,0:T(8,128)(2,1)}, u32[]{:S(2)}) copy-start(bf16[256,3584]{1,0:T(8,128)(2,1)} %param.23) | copy-start | bytes 5505028
  7.2 123.3 %all-gather.2.cloned.1.call-start = ((), (), s32[]{:S(2)}) async-start(), calls=%async_computation.4 | async-start | bytes 3612672 | tf_op jit(solution)/shard_map/all_gather | solution.py:432
  7.2 19.6 %collective-permute-start.1 = (bf16[56,896]{1,0:T(8,128)(2,1)}, bf16[56,896]{1,0:T(8,128)(2,1)S(1)}, u32[]{:S(2)}, u32[]{:S(2)}) collective-permute-start(bf16[56,896]{1,0:T(8,128)(2,1)} %param.22), channel_id=1, source_target_pairs={{0,0},{1,2},{2,4},{3,6},{4,1},{5,3},{6,5},{7,7},{8,8},{9,10},{10,1... | collective-permute-start | bytes 301064 | tf_op jit(solution)/shard_map/ppermute | solution.py:410
  10.8 17.8 %collective-permute-start.2 = (bf16[56,896]{1,0:T(8,128)(2,1)}, bf16[56,896]{1,0:T(8,128)(2,1)S(1)}, u32[]{:S(2)}, u32[]{:S(2)}) collective-permute-start(bf16[56,896]{1,0:T(8,128)(2,1)} %param.22), channel_id=1, source_target_pairs={{0,24},{1,26},{2,28},{3,30},{4,25},{5,27},{6,29},{7,31},{8,0},{9,2... | collective-permute-start | bytes 301064 | tf_op jit(solution)/shard_map/ppermute | solution.py:410
  13.3 15.3 %collective-permute-start.3 = (bf16[56,896]{1,0:T(8,128)(2,1)}, bf16[56,896]{1,0:T(8,128)(2,1)S(1)}, u32[]{:S(2)}, u32[]{:S(2)}) collective-permute-start(bf16[56,896]{1,0:T(8,128)(2,1)} %param.22), channel_id=1, source_target_pairs={{0,16},{1,18},{2,20},{3,22},{4,17},{5,19},{6,21},{7,23},{8,24},{9,... | collective-permute-start | bytes 301064 | tf_op jit(solution)/shard_map/ppermute | solution.py:410
  15.1 13.6 %collective-permute-start.4 = (bf16[56,896]{1,0:T(8,128)(2,1)}, bf16[56,896]{1,0:T(8,128)(2,1)S(1)}, u32[]{:S(2)}, u32[]{:S(2)}) collective-permute-start(bf16[56,896]{1,0:T(8,128)(2,1)} %param.22), channel_id=1, source_target_pairs={{0,8},{1,10},{2,12},{3,14},{4,9},{5,11},{6,13},{7,15},{8,16},{9,18... | collective-permute-start | bytes 301064 | tf_op jit(solution)/shard_map/ppermute | solution.py:410
  17.9 10.8 %collective-permute-start = (bf16[56,1152]{1,0:T(8,128)(2,1)S(1)}, bf16[56,1152]{1,0:T(8,128)(2,1)S(1)}, u32[]{:S(2)}, u32[]{:S(2)}) collective-permute-start(bf16[56,1152]{1,0:T(8,128)(2,1)S(1)} %pad_maximum_fusion), channel_id=1, source_target_pairs={{0,0},{1,2},{2,4},{3,6},{4,1},{5,3},{6,5},{7,7},{8,8},{9,10},{10,1... | collective-permute-start | bytes 387080 | tf_op jit(solution)/shard_map/ppermute | solution.py:410
  26.8 36.7 %copy-start.6 = (s32[32,16]{0,1:T(8,128)S(1)}, s32[32,16]{0,1:T(8,128)}, u32[]{:S(2)}) copy-start(s32[32,16]{0,1:T(8,128)} %param.17) | copy-start | bytes 6148
  26.8 62.1 %collective-permute-start.9 = (bf16[4,448,512]{2,1,0:T(8,128)(2,1)}, bf16[4,448,512]{2,1,0:T(8,128)(2,1)}, u32[]{:S(2)}, u32[]{:S(2)}) collective-permute-start(bf16[4,448,512]{2,1,0:T(8,128)(2,1)} %norm.1), channel_id=1, source_target_pairs={{0,6},{2,4},{4,2},{6,0},{1,7},{3,5},{5,3},{7,1},{8,14},{10,12},{12... | collective-permute-start | bytes 5505032 | tf_op jit(solution)/shard_map/ppermute | solution.py:427
  28.7 34.8 %copy-start.5 = (bf16[4,56,896]{2,1,0:T(8,128)(2,1)}, bf16[4,56,896]{2,1,0:T(8,128)(2,1)S(1)}, u32[]{:S(2)}) copy-start(bf16[4,56,896]{2,1,0:T(8,128)(2,1)S(1)} %bitcast_dynamic-update-slice_fusion) | copy-start | bytes 1204228
  28.7 60.2 %copy-start.8 = (s32[128,8]{0,1:T(8,128)S(1)}, s32[128,8]{0,1:T(8,128)}, u32[]{:S(2)}) copy-start(s32[128,8]{0,1:T(8,128)} %param.27) | copy-start | bytes 12292
  28.7 60.3 %copy-start.9 = (s32[8]{0:T(128)S(1)}, s32[8]{0:T(128)}, u32[]{:S(2)}) copy-start(s32[8]{0:T(128)} %param.24) | copy-start | bytes 100
  28.7 61.5 %copy-start.10 = (s32[256]{0:T(256)S(1)}, s32[256]{0:T(256)}, u32[]{:S(2)}) copy-start(s32[256]{0:T(256)} %param.25) | copy-start | bytes 3076
  28.7 62.3 %copy-start.3 = (bf16[128,3584]{1,0:T(8,128)(2,1)S(1)}, bf16[128,3584]{1,0:T(8,128)(2,1)}, u32[]{:S(2)}) copy-start(bf16[128,3584]{1,0:T(8,128)(2,1)} %queries_ref.1) | copy-start | bytes 2752516
  61.3 21.1 %collective-permute-start.5 = (bf16[448,1152]{1,0:T(8,128)(2,1)}, bf16[448,1152]{1,0:T(8,128)(2,1)}, u32[]{:S(2)}, u32[]{:S(2)}) collective-permute-start(bf16[448,1152]{1,0:T(8,128)(2,1)} %all_gather.6.w0_ref), channel_id=1, source_target_pairs={{0,24},{8,0},{16,8},{24,16},{1,25},{9,1},{17,9},{25,17},{2,26},{10... | collective-permute-start | bytes 3096584 | tf_op jit(solution)/shard_map/ppermute | solution.py:237
  63.5 23.5 %collective-permute-start.7 = (bf16[448,1152]{1,0:T(8,128)(2,1)}, bf16[448,1152]{1,0:T(8,128)(2,1)}, u32[]{:S(2)}, u32[]{:S(2)}) collective-permute-start(bf16[448,1152]{1,0:T(8,128)(2,1)} %all_gather.6.w0_ref), channel_id=1, source_target_pairs={{0,8},{8,16},{16,24},{24,0},{1,9},{9,17},{17,25},{25,1},{2,10},{10... | collective-permute-start | bytes 3096584 | tf_op jit(solution)/shard_map/ppermute | solution.py:237
  63.6 26.3 %collective-permute-start.10 = (s32[32,16]{0,1:T(8,128)S(1)}, s32[32,16]{0,1:T(8,128)S(1)}, u32[]{:S(2)}, u32[]{:S(2)}) collective-permute-start(s32[32,16]{0,1:T(8,128)S(1)} %copy-done.6), channel_id=1, source_target_pairs={{0,6},{2,4},{4,2},{6,0},{1,7},{3,5},{5,3},{7,1},{8,14},{10,12},{12... | collective-permute-start | bytes 6152 | tf_op jit(solution)/shard_map/ppermute | solution.py:428
  84.2 29.3 %collective-permute-start.6 = (bf16[224,1152]{1,0:T(8,128)(2,1)}, bf16[224,1152]{1,0:T(8,128)(2,1)S(1)}, u32[]{:S(2)}, u32[]{:S(2)}) collective-permute-start(bf16[224,1152]{1,0:T(8,128)(2,1)} %slice.12), channel_id=1, source_target_pairs={{0,24},{8,0},{16,8},{24,16},{1,25},{9,1},{17,9},{25,17},{2,26},{10... | collective-permute-start | bytes 1548296 | tf_op jit(solution)/shard_map/ppermute | solution.py:237
  88.9 24.7 %collective-permute-start.8 = (bf16[224,1152]{1,0:T(8,128)(2,1)}, bf16[224,1152]{1,0:T(8,128)(2,1)}, u32[]{:S(2)}, u32[]{:S(2)}) collective-permute-start(bf16[224,1152]{1,0:T(8,128)(2,1)} %slice.13), channel_id=1, source_target_pairs={{0,8},{8,16},{16,24},{24,0},{1,9},{9,17},{17,25},{25,1},{2,10},{10... | collective-permute-start | bytes 1548296 | tf_op jit(solution)/shard_map/ppermute | solution.py:237
  105.5 5.7 %copy-start.7 = (pred[128,128]{1,0:T(32,128)(4,1)S(1)}, pred[128,128]{1,0:T(32,128)(4,1)}, u32[]{:S(2)}) copy-start(pred[128,128]{1,0:T(32,128)(4,1)} %constant.91.clone) | copy-start | bytes 49156
  118.0 4.7 %collective-permute-start.11 = (bf16[512,1152]{1,0:T(8,128)(2,1)}, bf16[512,1152]{1,0:T(8,128)(2,1)}, u32[]{:S(2)}, u32[]{:S(2)}) collective-permute-start(bf16[512,1152]{1,0:T(8,128)(2,1)} %far.3), channel_id=1, source_target_pairs={{0,1},{1,0},{2,3},{3,2},{4,5},{5,4},{6,7},{7,6},{8,9},{9,8},{10,11... | collective-permute-start | bytes 3538952 | tf_op jit(solution)/shard_map/ppermute | solution.py:237
  128.0 1.6 collective-permute-start.12
  150.2 2.7 %collective-permute-start.13 = (f32[128,1920]{1,0:T(8,128)S(1)}, f32[128,1920]{1,0:T(8,128)S(1)}, u32[]{:S(2)}, u32[]{:S(2)}) collective-permute-start(f32[128,1920]{1,0:T(8,128)S(1)} %get-tuple-element.56), channel_id=1, source_target_pairs={{0,1},{1,0},{2,3},{3,2},{4,5},{5,4},{6,7},{7,6},{8,9},{9,8},{10,11... | collective-permute-start | bytes 2949128 | tf_op jit(solution)/shard_map/ppermute | solution.py:237
  214.4 2.6 %collective-permute-start.14 = (f32[128,1920]{1,0:T(8,128)S(1)}, f32[128,1920]{1,0:T(8,128)S(1)}, u32[]{:S(2)}, u32[]{:S(2)}) collective-permute-start(f32[128,1920]{1,0:T(8,128)S(1)} %bitcast.37), channel_id=1, source_target_pairs={{0,1},{1,0},{2,3},{3,2},{4,5},{5,4},{6,7},{7,6},{8,9},{9,8},{10,11... | collective-permute-start | bytes 2949128 | tf_op jit(solution)/shard_map/ppermute | solution.py:237
  (3 other events, 4.4 us)
Sparse Core Ops, SparseCore 0:
  63.7 43.9 all-gather.1

commit v6 on v5

--- a/solution.py
+++ b/solution.py
@@ -24,6 +24,7 @@
 
 BLOCK = 128
 HALF = 1920
+SENT = 1280
 
 
 def rotary_tables(length):
@@ -326,16 +327,17 @@
     lanes = (2 * HALF - width) // 2
     first = core_ref[0] == 0
     step = pl.program_id(0)
-    rows = pl.ds(pl.multiple_of(step * query_ref.shape[0], 8), query_ref.shape[0])
+    rows = pl.ds(pl.multiple_of(step * query_ref.shape[0], 16), query_ref.shape[0])
 
     def side(left_ref, right_ref):
-        losses = jnp.sum(right_ref[:, rest : rest + lanes]) / lanes
-        weights = jnp.sum(right_ref[:, rest + lanes :]) / lanes
+        extra = jnp.sum(right_ref[:, rest:].astype(jnp.float32), axis=0, keepdims=True)
+        losses = jnp.sum(extra[:, :lanes]) / (lanes // 2)
+        weights = jnp.sum(extra[:, lanes:]) / (lanes // 2)
         factor = labels / weights
         scale = factor / math.sqrt(width)
         loss_ref[...] = jnp.full(loss_ref.shape, factor * losses / (batch * labels), jnp.float32)
-        query_ref[:, :HALF] = scale * left_ref[rows, :]
-        query_ref[:, HALF:] = scale * right_ref[rows, :rest]
+        query_ref[:, :HALF] = scale * left_ref[rows, :].astype(jnp.float32)
+        query_ref[:, HALF:] = scale * right_ref[rows, :rest].astype(jnp.float32)
         label_ref[...] = scale * lax.dot_general(
             slopes_ref[...],
             queries_ref[...],
@@ -420,21 +422,17 @@
         )
 
     y = lax.axis_index("y")
-    moved = to_group(jnp.concatenate([key_matrix, value_matrix, q_weight], axis=1), 0)
+    packed = jnp.concatenate([key_matrix, value_matrix, q_weight], axis=1)
+    cut = packed.shape[1]
+    moved = to_group(jnp.concatenate([packed, out_weight[:, : SENT - cut]], axis=1), 0)
+    half = norm_half(core, hidden_states, norm_gain)
+    moved, half, out_weight = lax.optimization_barrier((moved, half, out_weight))
+    in_z = lax.all_gather(moved, "z", axis=0, tiled=True)
     out_y = in_order([to_group(out_weight, d) for d in range(4)], y)
-    half = norm_half(core, hidden_states, norm_gain)
+    out_all = lax.all_gather(out_y.reshape(4 * rows, -1), "z", axis=0, tiled=True)
     facing = [(i, 3 - i) for i in range(4)]
     half_other = lax.ppermute(half, RING_X, facing)
     ids_other = lax.ppermute(token_ids, RING_X, facing)
-    moved, half = lax.optimization_barrier((moved, half))
-    own = lax.all_gather(moved, "z", axis=0, tiled=True)
-    own, out_y = lax.optimization_barrier((own, out_y))
-    out_all = lax.all_gather(out_y.reshape(4 * rows, -1), "z", axis=0, tiled=True)
-    up, down = ring_near(own)
-    far_a, far_b = ring_far(up, down)
-    rest = (positives, label_counts, refresh_rows, queries, token_ids)
-    half_other, rest = lax.optimization_barrier((half_other, rest))
-    positives, label_counts, refresh_rows, queries, token_ids = rest
 
     balance = (1.0 - focal_beta) / -jnp.expm1(
         label_counts.astype(f32) * math.log(focal_beta)
@@ -480,14 +478,19 @@
     ids = jnp.where(keeps, token_ids, ids_other)
 
     allowed, live_rows = attend_tables(ids)
+    early = (kept_slopes, kept_loss, new_balance, new_signs, chosen, allowed, live_rows)
+    in_z, early = lax.optimization_barrier((in_z, early))
+    kept_slopes, kept_loss, new_balance, new_signs, chosen, allowed, live_rows = early
     sums = jnp.stack([kept_loss, jnp.sum(balance)])
-    early = (kept_query, kept_slopes, sums, new_balance, new_signs, chosen, states_sum, counted)
+
+    own = in_z[:, :cut]
+    up, down = ring_near(own)
+    far = ring_far(up, down)
     near = (own, up, down)
     give_near, keep_near = project(y, give, near), project(y, keep, near)
-    early = early + (allowed, live_rows, give_near, keep_near)
-    far, early = lax.optimization_barrier(((far_a, far_b), early))
-    kept_query, kept_slopes, sums, new_balance, new_signs, chosen, states_sum, counted = early[:8]
-    allowed, live_rows, give_near, keep_near = early[8:]
+    early = (kept_query, sums, states_sum, counted, give_near, keep_near)
+    far, early = lax.optimization_barrier((far, early))
+    kept_query, sums, states_sum, counted, give_near, keep_near = early
     taken = shift(project(y, give, far, give_near, bf16), "c", 2, 1)
     raw = project(y, keep, far, keep_near)
     pooled = attend_pooled(raw, taken, allowed, live_rows, length)
@@ -520,13 +523,17 @@
     ).astype(bf16)
 
     batch = queries.shape[0]
-    near = ("y", "xh", "xl")
+    plane = ("y", "xh", "xl")
     part = mine + shift(theirs, "c", 2, 1)
     part = jnp.sum(
-        lax.all_to_all(part.reshape(16, batch // 16, HALF), near, 0, 0, tiled=True), axis=0
+        lax.all_to_all(part.reshape(16, batch // 16, HALF), plane, 0, 0, tiled=True), axis=0
     )
     part = jnp.sum(spread(part, "z", 8), axis=0)
-    part = spread(part, near, 16).reshape(batch, HALF)
+    lane = lax.broadcasted_iota(jnp.int32, part.shape, 1)
+    spare = (lane >= width - HALF) & (lane % 128 >= 64) & (core == 1)
+    low = part - lax.reduce_precision(part, 8, 7)
+    part = jnp.where(spare, low, part).astype(bf16)
+    part = spread(part, plane, 16).reshape(batch, HALF)
     back = shift(part, "c", 2, 1)
     label_grad, query_grad, loss = final(core, part, back, slopes, queries, owned * ndp * nmp)
     return (label_grad, query_grad, loss[0, 0])

time: 230 us -> 218 us (0.948)
  blocking collectives: 103 us -> 45.7 us
  waiting for transfers between devices: 24.3 us -> 59.8 us
  starting transfers between devices: 19.6 us -> 27.1 us
    all_gather x1 -> x0, blocking collectives: 32.5 us -> none  [shards(): own = lax.all_gather(moved, 'z', axis=0, tiled=True)]
    all_to_all x2 -> x1, blocking collectives: 38.1 us -> 13.5 us  [spread(): lax.all_to_all(jnp.broadcast_to(x[None], (size,) + x.shape), axes, 0, 0,...]
    all_gather x0 -> x1, waiting for transfers between devices: none -> 18.1 us  [shards(): in_z = lax.all_gather(moved, 'z', axis=0, tiled=True)]
    all_to_all x0 -> x1, waiting for transfers between devices: none -> 15.7 us  [spread(): lax.all_to_all(jnp.broadcast_to(x[None], (size,) + x.shape), axes, 0, 0,...]
    ppermute x5, waiting for transfers between devices: 0.01 us -> 5.2 us  [to_group(): lax.ppermute(block, ('y', 'xh', 'xl', 'c'), [(8 * v + 4 * h + 2 * l + k,...]
    all_to_all x0 -> x1, starting transfers between devices: none -> 4.69 us  [spread(): lax.all_to_all(jnp.broadcast_to(x[None], (size,) + x.shape), axes, 0, 0,...]
    ppermute x8, waiting for transfers between devices: 24.2 us -> 20.8 us  [shift(): return lax.ppermute(x, axis, [(i, (i + by) % size) for i in range(size)])]
    slice x0 -> x2, local copies, waits for them, and re-layouts: none -> 3.09 us  [the longest x1 2.25 us: shards(): own = in_z[:, :cut]]
  transfers between devices with their start and end apart: 16 -> 18, of which waited for: 4 -> 8; matrix products, arithmetic and copies ran while one was open for 9% -> 9% of each run, Pallas kernels for 12% -> 13%
where the time goes in v6:
time: 218 us; the launch traced here: 215 us
  waiting for transfers between devices  59.8 us (27%)
  blocking collectives  45.7 us (21%)
  Pallas kernels  33.3 us (15%)
  starting transfers between devices  27.1 us (12%)
  local copies, waits for them, and re-layouts  15.8 us (7%)
  between operations  14.5 us (7%)
  other arithmetic  12.7 us (6%)
  matrix products  6.24 us (3%)
    all_to_all x1, blocking collectives, shards(): lax.all_to_all(part.reshape(16, batch // 16, HALF), plane, 0, 0, tiled=True)  21.8 us
    ppermute x8, waiting for transfers between devices, shift(): return lax.ppermute(x, axis, [(i, (i + by) % size) for i in range(size)])  20.8 us
    pallas_call x4, Pallas kernels, project(): pl.pallas_call(kernel, out_shape=jax.ShapeDtypeStruct((tokens, columns),...  18.8 us
    all_gather x1, waiting for transfers between devices, shards(): in_z = lax.all_gather(moved, 'z', axis=0, tiled=True)  18.1 us
    all_to_all x1, waiting for transfers between devices, spread(): lax.all_to_all(jnp.broadcast_to(x[None], (size,) + x.shape), axes, 0, 0,...  15.7 us
    all_to_all x1, blocking collectives, spread(): lax.all_to_all(jnp.broadcast_to(x[None], (size,) + x.shape), axes, 0, 0,...  13.5 us
    ppermute x5, starting transfers between devices, to_group(): lax.ppermute(block, ('y', 'xh', 'xl', 'c'), [(8 * v + 4 * h + 2 * l + k,...  13.5 us
    all_to_all x1, blocking collectives, shards(): lax.all_to_all(head_terms.astype(bf16).reshape(8, share, -1), ('xh', 'xl'...  10.3 us
  transfers between devices with their start and end apart: 18, of which 8 were waited for; matrix products, arithmetic and copies ran while one was open for 9% of the time, Pallas kernels for 13%

profile of v6, /device:TPU:2, one launch (start us, length us, event | category | flops | bytes accessed | tf_op | source)
XLA Modules:
  0.0 215.2 jit_solution(163822151611032993)
XLA Ops:
  9.0 3.4 %collective-permute-start = (bf16[56,1280]{1,0:T(8,128)(2,1)S(1)}, bf16[56,1280]{1,0:T(8,128)(2,1)S(1)}, u32[]{:S(2)}, u32[]{:S(2)}) collective-permute-start(bf16[56,1280]{1,0:T(8,128)(2,1)S(1)} %pad_maximum_fusion), channel_id=1, source_target_pairs={{0,0},{1,2},{2,4},{3,6},{4,1},{5,3},{6,5},{7,7},{8,8},{9,10},{10,1... | collective-permute-start | bytes 430088 | tf_op jit(solution)/shard_map/ppermute | solution.py:412
  15.2 4.1 %norm.1 = bf16[4,448,512]{2,1,0:T(8,128)(2,1)} custom-call(s32[1]{0:T(128)} %bitcast.core_ref, bf16[512,3584]{1,0:T(8,128)(2,1)S(1)} %copy-done.2, f32[1,3584]{1,0:T(1,128)S(1)} %reshape.140.gain_ref), custom_call_target="tpu_custom_call" | custom-call | flops 7340032 | bytes 5505024 | tf_op jit(solution)/shard_map/norm/pallas_call | solution.py:63
  20.4 3.9 %collective-permute-start.9 = (bf16[56,896]{1,0:T(8,128)(2,1)S(1)}, bf16[56,896]{1,0:T(8,128)(2,1)S(1)}, u32[]{:S(2)}, u32[]{:S(2)}) collective-permute-start(bf16[56,896]{1,0:T(8,128)(2,1)S(1)} %copy-done.11), channel_id=1, source_target_pairs={{0,0},{1,2},{2,4},{3,6},{4,1},{5,3},{6,5},{7,7},{8,8},{9,10},{10,1... | collective-permute-start | bytes 301064 | tf_op jit(solution)/shard_map/ppermute | solution.py:412
  24.2 2.5 %collective-permute-start.10 = (bf16[56,896]{1,0:T(8,128)(2,1)S(1)}, bf16[56,896]{1,0:T(8,128)(2,1)S(1)}, u32[]{:S(2)}, u32[]{:S(2)}) collective-permute-start(bf16[56,896]{1,0:T(8,128)(2,1)S(1)} %copy-done.11), channel_id=1, source_target_pairs={{0,24},{1,26},{2,28},{3,30},{4,25},{5,27},{6,29},{7,31},{8,0},{9,2... | collective-permute-start | bytes 301064 | tf_op jit(solution)/shard_map/ppermute | solution.py:412
  30.6 2.7 %collective-permute-done.11 = bf16[56,896]{1,0:T(8,128)(2,1)S(1)} collective-permute-done((bf16[56,896]{1,0:T(8,128)(2,1)S(1)}, bf16[56,896]{1,0:T(8,128)(2,1)S(1)}, u32[]{:S(2)}, u32[]{:S(2)}) %collective-permute-start.11) | collective-permute-done | bytes 100384 | tf_op jit(solution)/shard_map/ppermute | solution.py:412
  33.3 2.5 %collective-permute-done.12 = bf16[56,896]{1,0:T(8,128)(2,1)S(1)} collective-permute-done((bf16[56,896]{1,0:T(8,128)(2,1)S(1)}, bf16[56,896]{1,0:T(8,128)(2,1)S(1)}, u32[]{:S(2)}, u32[]{:S(2)}) %collective-permute-start.12) | collective-permute-done | bytes 100384 | tf_op jit(solution)/shard_map/ppermute | solution.py:412
  42.7 18.1 %all-gather.3.cloned.1.call-done = bf16[448,1280]{1,0:T(8,128)(2,1)} async-done(((bf16[56,1280]{1,0:T(8,128)(2,1)}), bf16[448,1280]{1,0:T(8,128)(2,1)}) %all-gather.3.cloned.1.call-update) | async-done | bytes 1146896 | tf_op jit(solution)/shard_map/all_gather | solution.py:430
  63.1 2.8 %collective-permute-start.2 = (bf16[448,1152]{1,0:T(8,128)(2,1)}, bf16[448,1152]{1,0:T(8,128)(2,1)}, u32[]{:S(2)}, u32[]{:S(2)}) collective-permute-start(bf16[448,1152]{1,0:T(8,128)(2,1)} %slice.16.w0_ref), channel_id=1, source_target_pairs={{0,24},{8,0},{16,8},{24,16},{1,25},{9,1},{17,9},{25,17},{2,26},{10... | collective-permute-start | bytes 3096584 | tf_op jit(solution)/shard_map/ppermute | solution.py:238
  69.3 15.5 %collective-permute-done.2.w1_ref = bf16[448,1152]{1,0:T(8,128)(2,1)} collective-permute-done((bf16[448,1152]{1,0:T(8,128)(2,1)}, bf16[448,1152]{1,0:T(8,128)(2,1)}, u32[]{:S(2)}, u32[]{:S(2)}) %collective-permute-start.2) | collective-permute-done | bytes 1032224 | tf_op jit(solution)/shard_map/ppermute | solution.py:238
  85.9 3.1 %collective-permute-start.3 = (bf16[224,1152]{1,0:T(8,128)(2,1)S(1)}, bf16[224,1152]{1,0:T(8,128)(2,1)S(1)}, u32[]{:S(2)}, u32[]{:S(2)}) collective-permute-start(bf16[224,1152]{1,0:T(8,128)(2,1)S(1)} %slice.20), channel_id=1, source_target_pairs={{0,24},{8,0},{16,8},{24,16},{1,25},{9,1},{17,9},{25,17},{2,26},{10... | collective-permute-start | bytes 1548296 | tf_op jit(solution)/shard_map/ppermute | solution.py:238
  90.4 4.2 %broadcast_select_fusion = (bf16[4,448,512]{2,1,0:T(8,128)(2,1)}, bf16[4,448,512]{2,1,0:T(8,128)(2,1)}) fusion(bf16[4,448,512]{2,1,0:T(8,128)(2,1)} %norm.1, bf16[4,448,512]{2,1,0:T(8,128)(2,1)} %collective-permute-done.6, pred[]{:T(512)S(6)} %eq.66), kind=kLoop, calls=%fused_computation.4 | loop fusion | flops 1835008 | bytes 7340033 | tf_op jit(solution)/shard_map/jit(_where)/select_n | solution.py:477
  96.0 5.6 %near.3.near_ref = f32[512,1152]{1,0:T(8,128)} custom-call(s32[1]{0:T(128)} %bitcast.6.place_ref, bf16[4,448,512]{2,1,0:T(8,128)(2,1)} %get-tuple-element.59.x_ref, bf16[448,1152]{1,0:T(8,128)(2,1)} %slice.16.w0_ref, bf16[448,1152]{1,0:T(8,128)(2,1)} %collective-permute-done.2.w1_ref, bf16[448,1152]{1,0:T(8,128)(2,1)} %collective-permute-done.4.w3_ref), custom_call_target="tpu_custom_call" | custom-call | flops 1585446912 | bytes 8011776 | tf_op jit(solution)/shard_map/near/pallas_call | solution.py:124
  101.6 5.7 %near.2.near_ref = f32[512,1152]{1,0:T(8,128)} custom-call(s32[1]{0:T(128)} %bitcast.6.place_ref, bf16[4,448,512]{2,1,0:T(8,128)(2,1)} %get-tuple-element.60.x_ref, bf16[448,1152]{1,0:T(8,128)(2,1)} %slice.16.w0_ref, bf16[448,1152]{1,0:T(8,128)(2,1)} %collective-permute-done.2.w1_ref, bf16[448,1152]{1,0:T(8,128)(2,1)} %collective-permute-done.4.w3_ref), custom_call_target="tpu_custom_call" | custom-call | flops 1585446912 | bytes 8011776 | tf_op jit(solution)/shard_map/near/pallas_call | solution.py:124
  108.3 3.6 %far.3 = bf16[512,1152]{1,0:T(8,128)(2,1)} custom-call(s32[1]{0:T(128)} %bitcast.6.place_ref, bf16[4,448,512]{2,1,0:T(8,128)(2,1)} %get-tuple-element.60.x_ref, f32[512,1152]{1,0:T(8,128)} %near.2.near_ref, bf16[224,1152]{1,0:T(8,128)(2,1)} %copy-done.4, bf16[224,1152]{1,0:T(8,128)(2,1)} %copy-done.5), custom_call_target="tpu_custom_call" | custom-call | flops 528482304 | bytes 5029888 | tf_op jit(solution)/shard_map/far/pallas_call | solution.py:124
  112.7 3.8 %far.2.raw_ref = f32[512,1152]{1,0:T(8,128)} custom-call(s32[1]{0:T(128)} %bitcast.6.place_ref, bf16[4,448,512]{2,1,0:T(8,128)(2,1)} %get-tuple-element.59.x_ref, f32[512,1152]{1,0:T(8,128)} %near.3.near_ref, bf16[224,1152]{1,0:T(8,128)(2,1)} %copy-done.4, bf16[224,1152]{1,0:T(8,128)(2,1)} %copy-done.5), custom_call_target="tpu_custom_call" | custom-call | flops 528482304 | bytes 5029888 | tf_op jit(solution)/shard_map/far/pallas_call | solution.py:124
  116.6 5.3 %attend.1 = bf16[32,896]{1,0:T(8,128)(2,1)} custom-call(f32[512,1152]{1,0:T(8,128)} %far.2.raw_ref, bf16[512,1152]{1,0:T(8,128)(2,1)} %collective-permute-done.7.add_ref, f32[512,128]{1,0:T(8,128)} %bitcast.42, f32[512,1]{1,0:T(8,128)} %copy.39.live_ref, bf16[56,896]{1,0:T(8,128)(2,1)} %constant.110.clone.member_ref, f32[128,128]{1,0:T(8,128)} %constant.111.clone.cos_ref, ...), custom_call_target="tpu_custom_call" | custom-call | flops 234881024 | bytes 4718592 | tf_op jit(solution)/shard_map/attend/pallas_call | solution.py:205
  124.4 3.0 %fusion = bf16[8,8,1792]{2,1,0:T(8,128)(2,1)S(1)} fusion(bf16[1792,896]{1,0:T(8,128)(2,1)} %all-gather.5.cloned.1.call-done, bf16[32,896]{1,0:T(8,128)(2,1)S(1)} %get-tuple-element.64, bf16[32,896]{1,0:T(8,128)(2,1)S(1)} %get-tuple-element.63), kind=kOutput, calls=%fused_computation.1 | convolution fusion | flops 205864960 | bytes 3555328 | tf_op jit(solution)/shard_map/dot_general | solution.py:503
  127.4 10.3 %all_to_all.20 = bf16[8,8,1792]{2,1,0:T(8,128)(2,1)S(1)} all-to-all(bf16[8,8,1792]{2,1,0:T(8,128)(2,1)S(1)} %fusion), channel_id=1, replica_groups=mesh['z'=8,'y'=4,'xh'=2,'xl'=2,'c'=2] {'xh','xl','c'}, dimensions={0} | all-to-all | bytes 458752 | tf_op jit(solution)/shard_map/all_to_all | solution.py:506
  142.1 2.6 %collective-permute-done.13 = f32[128,1920]{1,0:T(8,128)S(1)} collective-permute-done((f32[128,1920]{1,0:T(8,128)S(1)}, f32[128,1920]{1,0:T(8,128)S(1)}, u32[]{:S(2)}, u32[]{:S(2)}) %collective-permute-start.13) | collective-permute-done | bytes 983072 | tf_op jit(solution)/shard_map/ppermute | solution.py:238
  144.7 21.8 %all_to_all.21 = f32[16,8,1920]{2,1,0:T(8,128)} all-to-all(f32[16,8,1920]{2,1,0:T(8,128)S(1)} %add_bitcast_fusion), channel_id=1, replica_groups=mesh['z'=8,'y'=4,'xh'=2,'xl'=2,'c'=2] {'y','xh','xl'}, dimensions={0} | all-to-all | bytes 1966080 | tf_op jit(solution)/shard_map/all_to_all | solution.py:529
  168.7 4.7 %all-to-all-start.2 = ((f32[8,8,1920]{2,1,0:T(8,128)}), f32[8,8,1920]{2,1,0:T(8,128)S(1)}, u32[]{:S(2)}, u32[]{:S(2)}) async-start(f32[8,8,1920]{2,1,0:T(8,128)} %broadcast_in_dim.90), calls=%async_computation.2 | async-start | bytes 983040 | tf_op jit(solution)/shard_map/all_to_all | solution.py:259
  173.4 15.7 %all-to-all-done.2 = f32[8,8,1920]{2,1,0:T(8,128)S(1)} async-done(((f32[8,8,1920]{2,1,0:T(8,128)}), f32[8,8,1920]{2,1,0:T(8,128)S(1)}, u32[]{:S(2)}, u32[]{:S(2)}) %all-to-all-start.2) | async-done | bytes 491552 | tf_op jit(solution)/shard_map/all_to_all | solution.py:259
  189.2 13.5 %all_to_all.22 = bf16[16,8,1920]{2,1,0:T(8,128)(2,1)S(1)} all-to-all(bf16[16,8,1920]{2,1,0:T(8,128)(2,1)S(1)} %broadcast_in_dim.91), channel_id=1, replica_groups=mesh['z'=8,'y'=4,'xh'=2,'xl'=2,'c'=2] {'y','xh','xl'}, dimensions={0} | all-to-all | bytes 983040 | tf_op jit(solution)/shard_map/all_to_all | solution.py:259
  204.6 3.2 %final.1 = (f32[256,3584]{1,0:T(8,128)}, f32[128,3584]{1,0:T(8,128)}, f32[8,128]{1,0:T(8,128)S(1)}) custom-call(s32[1]{0:T(128)} %bitcast.core_ref, bf16[128,1920]{1,0:T(8,128)(2,1)S(1)} %bitcast.38, bf16[128,1920]{1,0:T(8,128)(2,1)S(1)} %collective-permute-done.14.back_ref, bf16[256,128]{1,0:T(8,128)(2,1)S(1)} %fusion.3.slopes_ref, ...), custom_call_target="tpu_custom_call" | custom-call | tf_op jit(solution)/shard_map/final/pallas_call | solution.py:362
  (107 shorter events, 38.9 us)
Async XLA Ops:
  7.2 30.7 %copy-start = (bf16[256,3584]{1,0:T(8,128)(2,1)S(1)}, bf16[256,3584]{1,0:T(8,128)(2,1)}, u32[]{:S(2)}) copy-start(bf16[256,3584]{1,0:T(8,128)(2,1)} %param.23) | copy-start | bytes 5505028
  7.2 53.6 %all-gather.3.cloned.1.call-start = ((), (), s32[]{:S(2)}) async-start(), calls=%async_computation.4 | async-start | bytes 1290240 | tf_op jit(solution)/shard_map/all_gather | solution.py:430
  9.0 10.3 %collective-permute-start = (bf16[56,1280]{1,0:T(8,128)(2,1)S(1)}, bf16[56,1280]{1,0:T(8,128)(2,1)S(1)}, u32[]{:S(2)}, u32[]{:S(2)}) collective-permute-start(bf16[56,1280]{1,0:T(8,128)(2,1)S(1)} %pad_maximum_fusion), channel_id=1, source_target_pairs={{0,0},{1,2},{2,4},{3,6},{4,1},{5,3},{6,5},{7,7},{8,8},{9,10},{10,1... | collective-permute-start | bytes 430088 | tf_op jit(solution)/shard_map/ppermute | solution.py:412
  15.2 5.0 %copy-start.10 = (s32[128,8]{0,1:T(8,128)S(1)}, s32[128,8]{0,1:T(8,128)}, u32[]{:S(2)}) copy-start(s32[128,8]{0,1:T(8,128)} %param.27) | copy-start | bytes 12292
  15.2 5.2 %copy-start.11 = (bf16[56,896]{1,0:T(8,128)(2,1)S(1)}, bf16[56,896]{1,0:T(8,128)(2,1)}, u32[]{:S(2)}) copy-start(bf16[56,896]{1,0:T(8,128)(2,1)} %param.22) | copy-start | bytes 301060
  19.3 17.8 %copy-start.12 = (s32[8]{0:T(128)S(1)}, s32[8]{0:T(128)}, u32[]{:S(2)}) copy-start(s32[8]{0:T(128)} %param.24) | copy-start | bytes 100
  19.3 17.8 %copy-start.13 = (s32[256]{0:T(256)S(1)}, s32[256]{0:T(256)}, u32[]{:S(2)}) copy-start(s32[256]{0:T(256)} %param.25) | copy-start | bytes 3076
  19.3 18.6 %copy-start.3 = (bf16[128,3584]{1,0:T(8,128)(2,1)S(1)}, bf16[128,3584]{1,0:T(8,128)(2,1)}, u32[]{:S(2)}) copy-start(bf16[128,3584]{1,0:T(8,128)(2,1)} %queries_ref.3) | copy-start | bytes 2752516
  20.0 104.4 %all-gather.5.cloned.1.call-start = ((), (), s32[]{:S(2)}) async-start(), calls=%async_computation.5 | async-start | bytes 3612672 | tf_op jit(solution)/shard_map/all_gather | solution.py:432
  20.1 21.5 %collective-permute-start.1 = (s32[32,16]{0,1:T(8,128)S(1)}, s32[32,16]{0,1:T(8,128)S(1)}, u32[]{:S(2)}, u32[]{:S(2)}) collective-permute-start(s32[32,16]{0,1:T(8,128)S(1)} %copy-done.8), channel_id=1, source_target_pairs={{0,6},{2,4},{4,2},{6,0},{1,7},{3,5},{5,3},{7,1},{8,14},{10,12},{12... | collective-permute-start | bytes 6152 | tf_op jit(solution)/shard_map/ppermute | solution.py:435
  20.4 10.1 %collective-permute-start.9 = (bf16[56,896]{1,0:T(8,128)(2,1)S(1)}, bf16[56,896]{1,0:T(8,128)(2,1)S(1)}, u32[]{:S(2)}, u32[]{:S(2)}) collective-permute-start(bf16[56,896]{1,0:T(8,128)(2,1)S(1)} %copy-done.11), channel_id=1, source_target_pairs={{0,0},{1,2},{2,4},{3,6},{4,1},{5,3},{6,5},{7,7},{8,8},{9,10},{10,1... | collective-permute-start | bytes 301064 | tf_op jit(solution)/shard_map/ppermute | solution.py:412
  24.2 6.3 %collective-permute-start.10 = (bf16[56,896]{1,0:T(8,128)(2,1)S(1)}, bf16[56,896]{1,0:T(8,128)(2,1)S(1)}, u32[]{:S(2)}, u32[]{:S(2)}) collective-permute-start(bf16[56,896]{1,0:T(8,128)(2,1)S(1)} %copy-done.11), channel_id=1, source_target_pairs={{0,24},{1,26},{2,28},{3,30},{4,25},{5,27},{6,29},{7,31},{8,0},{9,2... | collective-permute-start | bytes 301064 | tf_op jit(solution)/shard_map/ppermute | solution.py:412
  26.8 6.5 %collective-permute-start.11 = (bf16[56,896]{1,0:T(8,128)(2,1)S(1)}, bf16[56,896]{1,0:T(8,128)(2,1)S(1)}, u32[]{:S(2)}, u32[]{:S(2)}) collective-permute-start(bf16[56,896]{1,0:T(8,128)(2,1)S(1)} %copy-done.11), channel_id=1, source_target_pairs={{0,16},{1,18},{2,20},{3,22},{4,17},{5,19},{6,21},{7,23},{8,24},{9,... | collective-permute-start | bytes 301064 | tf_op jit(solution)/shard_map/ppermute | solution.py:412
  28.1 7.7 %collective-permute-start.12 = (bf16[56,896]{1,0:T(8,128)(2,1)S(1)}, bf16[56,896]{1,0:T(8,128)(2,1)S(1)}, u32[]{:S(2)}, u32[]{:S(2)}) collective-permute-start(bf16[56,896]{1,0:T(8,128)(2,1)S(1)} %copy-done.11), channel_id=1, source_target_pairs={{0,8},{1,10},{2,12},{3,14},{4,9},{5,11},{6,13},{7,15},{8,16},{9,18... | collective-permute-start | bytes 301064 | tf_op jit(solution)/shard_map/ppermute | solution.py:412
  39.3 51.1 %collective-permute-start.6 = (bf16[4,448,512]{2,1,0:T(8,128)(2,1)}, bf16[4,448,512]{2,1,0:T(8,128)(2,1)}, u32[]{:S(2)}, u32[]{:S(2)}) collective-permute-start(bf16[4,448,512]{2,1,0:T(8,128)(2,1)} %norm.1), channel_id=1, source_target_pairs={{0,6},{2,4},{4,2},{6,0},{1,7},{3,5},{5,3},{7,1},{8,14},{10,12},{12... | collective-permute-start | bytes 5505032 | tf_op jit(solution)/shard_map/ppermute | solution.py:434
  63.1 21.7 %collective-permute-start.2 = (bf16[448,1152]{1,0:T(8,128)(2,1)}, bf16[448,1152]{1,0:T(8,128)(2,1)}, u32[]{:S(2)}, u32[]{:S(2)}) collective-permute-start(bf16[448,1152]{1,0:T(8,128)(2,1)} %slice.16.w0_ref), channel_id=1, source_target_pairs={{0,24},{8,0},{16,8},{24,16},{1,25},{9,1},{17,9},{25,17},{2,26},{10... | collective-permute-start | bytes 3096584 | tf_op jit(solution)/shard_map/ppermute | solution.py:238
  65.8 23.2 %collective-permute-start.4 = (bf16[448,1152]{1,0:T(8,128)(2,1)}, bf16[448,1152]{1,0:T(8,128)(2,1)}, u32[]{:S(2)}, u32[]{:S(2)}) collective-permute-start(bf16[448,1152]{1,0:T(8,128)(2,1)} %slice.16.w0_ref), channel_id=1, source_target_pairs={{0,8},{8,16},{16,24},{24,0},{1,9},{9,17},{17,25},{25,1},{2,10},{10... | collective-permute-start | bytes 3096584 | tf_op jit(solution)/shard_map/ppermute | solution.py:238
  85.9 21.4 %collective-permute-start.3 = (bf16[224,1152]{1,0:T(8,128)(2,1)S(1)}, bf16[224,1152]{1,0:T(8,128)(2,1)S(1)}, u32[]{:S(2)}, u32[]{:S(2)}) collective-permute-start(bf16[224,1152]{1,0:T(8,128)(2,1)S(1)} %slice.20), channel_id=1, source_target_pairs={{0,24},{8,0},{16,8},{24,16},{1,25},{9,1},{17,9},{25,17},{2,26},{10... | collective-permute-start | bytes 1548296 | tf_op jit(solution)/shard_map/ppermute | solution.py:238
  90.1 17.2 %collective-permute-start.5 = (bf16[224,1152]{1,0:T(8,128)(2,1)S(1)}, bf16[224,1152]{1,0:T(8,128)(2,1)S(1)}, u32[]{:S(2)}, u32[]{:S(2)}) collective-permute-start(bf16[224,1152]{1,0:T(8,128)(2,1)S(1)} %slice.21), channel_id=1, source_target_pairs={{0,8},{8,16},{16,24},{24,0},{1,9},{9,17},{17,25},{25,1},{2,10},{10... | collective-permute-start | bytes 1548296 | tf_op jit(solution)/shard_map/ppermute | solution.py:238
  111.8 4.7 %collective-permute-start.7 = (bf16[512,1152]{1,0:T(8,128)(2,1)}, bf16[512,1152]{1,0:T(8,128)(2,1)}, u32[]{:S(2)}, u32[]{:S(2)}) collective-permute-start(bf16[512,1152]{1,0:T(8,128)(2,1)} %far.3), channel_id=1, source_target_pairs={{0,1},{1,0},{2,3},{3,2},{4,5},{5,4},{6,7},{7,6},{8,9},{9,8},{10,11... | collective-permute-start | bytes 3538952 | tf_op jit(solution)/shard_map/ppermute | solution.py:238
  121.9 1.6 collective-permute-start.8
  142.0 2.7 %collective-permute-start.13 = (f32[128,1920]{1,0:T(8,128)S(1)}, f32[128,1920]{1,0:T(8,128)S(1)}, u32[]{:S(2)}, u32[]{:S(2)}) collective-permute-start(f32[128,1920]{1,0:T(8,128)S(1)} %get-tuple-element.46), channel_id=1, source_target_pairs={{0,1},{1,0},{2,3},{3,2},{4,5},{5,4},{6,7},{7,6},{8,9},{9,8},{10,11... | collective-permute-start | bytes 2949128 | tf_op jit(solution)/shard_map/ppermute | solution.py:238
  168.7 20.4 %all-to-all-start.2 = ((f32[8,8,1920]{2,1,0:T(8,128)}), f32[8,8,1920]{2,1,0:T(8,128)S(1)}, u32[]{:S(2)}, u32[]{:S(2)}) async-start(f32[8,8,1920]{2,1,0:T(8,128)} %broadcast_in_dim.90), calls=%async_computation.2 | async-start | bytes 983040 | tf_op jit(solution)/shard_map/all_to_all | solution.py:259
  202.7 1.9 collective-permute-start.14
  (8 other events, 15.7 us)
Sparse Core Ops, SparseCore 0:
  20.1 40.6 all-gather.2
  62.6 44.1 all-gather.4

commit v7 on v6

--- a/solution.py
+++ b/solution.py
@@ -81,53 +81,46 @@
     )(core.reshape(1).astype(jnp.int32), states, gain.reshape(1, width))
 
 
-def near_kernel(place_ref, x_ref, w0_ref, w1_ref, w3_ref, out_ref):
-    def dot(x, w):
-        return lax.dot_general(
+def project_kernel(place_ref, *refs, pieces, seeded):
+    out_ref = refs[-1]
+    total = refs[3 * pieces][...] if seeded else None
+    first = place_ref[1] != 0
+    for index in range(pieces):
+        x = jnp.where(first, refs[index][0], refs[pieces + index][0])
+        w = refs[2 * pieces + index][...]
+        term = lax.dot_general(
             x, w, (((0,), (0,)), ((), ())), preferred_element_type=jnp.float32
         )
-
-    y = place_ref[0]
-    out_ref[...] = (
-        dot(x_ref[y], w0_ref[...])
-        + dot(x_ref[(y + 1) % 4], w1_ref[...])
-        + dot(x_ref[(y + 3) % 4], w3_ref[...])
-    )
-
-
-def far_kernel(place_ref, x_ref, near_ref, w2a_ref, w2b_ref, out_ref):
-    def dot(x, w):
-        return lax.dot_general(
-            x, w, (((0,), (0,)), ((), ())), preferred_element_type=jnp.float32
+        total = term if total is None else total + term
+    out_ref[...] = total.astype(out_ref.dtype)
+
+
+def project(y, first, x, pieces, near=None, dtype=jnp.float32):
+    _, depth, tokens = x[0].shape
+    columns = pieces[0][2].shape[1]
+    block = tokens // 2
+    extra = () if near is None else (near,)
+    tile = pl.BlockSpec((block, columns), lambda i, _: (i, 0))
+
+    def x_spec(distance, part, w):
+        return pl.BlockSpec(
+            (1, w.shape[0], block), lambda i, p: ((p[0] + distance) % 4, part, i)
         )
 
-    half = w2a_ref.shape[0]
-    far = x_ref[0]
-    out_ref[...] = (
-        near_ref[...] + dot(far[:half], w2a_ref[...]) + dot(far[half:], w2b_ref[...])
-    ).astype(out_ref.dtype)
-
-
-def project(y, x, pieces, near=None, dtype=jnp.float32):
-    _, depth, tokens = x.shape
-    columns = pieces[0].shape[1]
-    block = tokens // 2
-    fixed = [pl.BlockSpec(w.shape, lambda i, _: (0, 0)) for w in pieces]
-    tile = pl.BlockSpec((block, columns), lambda i, _: (i, 0))
-    if near is None:
-        kernel, extra = near_kernel, ()
-        x_spec = pl.BlockSpec((4, depth, block), lambda i, _: (0, 0, i))
-    else:
-        kernel, extra = far_kernel, (near,)
-        x_spec = pl.BlockSpec((1, depth, block), lambda i, p: ((p[0] + 2) % 4, 0, i))
-    used = sum(w.shape[0] for w in pieces)
+    weights = [w for _, _, w in pieces]
+    used = sum(w.shape[0] for w in weights)
     return pl.pallas_call(
-        kernel,
+        functools.partial(project_kernel, pieces=len(pieces), seeded=near is not None),
         out_shape=jax.ShapeDtypeStruct((tokens, columns), dtype),
         grid_spec=pltpu.PrefetchScalarGridSpec(
             num_scalar_prefetch=1,
             grid=(tokens // block,),
-            in_specs=[x_spec, *[tile for _ in extra], *fixed],
+            in_specs=[
+                *[x_spec(*piece) for piece in pieces],
+                *[x_spec(*piece) for piece in pieces],
+                *[pl.BlockSpec(w.shape, lambda i, _: (0, 0)) for w in weights],
+                *[tile for _ in extra],
+            ],
             out_specs=tile,
         ),
         compiler_params=pltpu.CompilerParams(vmem_limit_bytes=56 << 20),
@@ -136,8 +129,14 @@
             bytes_accessed=6 * tokens * columns + 2 * used * (tokens + columns),
             transcendentals=0,
         ),
-        name="near" if near is None else "far",
-    )(y.reshape(1).astype(jnp.int32), x, *extra, *pieces)
+        name="project",
+    )(
+        jnp.stack([y, first]).astype(jnp.int32),
+        *[x[0] for _ in pieces],
+        *[x[1] for _ in pieces],
+        *weights,
+        *extra,
+    )
 
 
 def attend_kernel(raw_ref, add_ref, allowed_ref, live_ref, member_ref, cos_ref, sin_ref, out_ref):
@@ -473,8 +472,8 @@
     states_sum = jnp.sum(states_own.astype(f32) * live_own[:, :, None], axis=1)
 
     keeps = xh == core
-    give = jnp.where(keeps, half_other, half)
-    keep = jnp.where(keeps, half, half_other)
+    sides = (half, half_other)
+    keep, give = keeps.astype(jnp.int32), 1 - keeps.astype(jnp.int32)
     ids = jnp.where(keeps, token_ids, ids_other)
 
     allowed, live_rows = attend_tables(ids)
@@ -485,14 +484,19 @@
 
     own = in_z[:, :cut]
     up, down = ring_near(own)
+    give_own = project(y, give, sides, [(0, 0, own)])
+    keep_own = project(y, keep, sides, [(0, 0, own)])
+    up, down, give_own, keep_own = lax.optimization_barrier((up, down, give_own, keep_own))
     far = ring_far(up, down)
-    near = (own, up, down)
-    give_near, keep_near = project(y, give, near), project(y, keep, near)
+    near = [(1, 0, up), (3, 0, down)]
+    give_near = project(y, give, sides, near, give_own)
+    keep_near = project(y, keep, sides, near, keep_own)
     early = (kept_query, sums, states_sum, counted, give_near, keep_near)
-    far, early = lax.optimization_barrier((far, early))
+    weights, early = lax.optimization_barrier((far, early))
+    far = [(2, part, w) for part, w in enumerate(weights)]
     kept_query, sums, states_sum, counted, give_near, keep_near = early
-    taken = shift(project(y, give, far, give_near, bf16), "c", 2, 1)
-    raw = project(y, keep, far, keep_near)
+    taken = shift(project(y, give, sides, far, give_near, bf16), "c", 2, 1)
+    raw = project(y, keep, sides, far, keep_near)
     pooled = attend_pooled(raw, taken, allowed, live_rows, length)
 
     pooled_other = shift(pooled, "c", 2, 1)

time: 218 us -> 227 us (1.041)
  Pallas kernels: 33.3 us -> 44 us
  other arithmetic: 12.7 us -> 9.13 us
  local copies, waits for them, and re-layouts: 15.8 us -> 18.5 us
    ppermute x8, waiting for transfers between devices: 20.8 us -> 5.31 us  [shift(): return lax.ppermute(x, axis, [(i, (i + by) % size) for i in range(size)])]
    ppermute x1, waiting for transfers between devices: 0.01 us -> 11.7 us  [shards(): half_other = lax.ppermute(half, RING_X, facing)]
    pallas_call x4 -> x6, Pallas kernels: 18.8 us -> 29.9 us  [project(): pl.pallas_call(functools.partial(project_kernel, pieces=len(pieces), seed...]
    select_n x1 -> x0, other arithmetic: 4.24 us -> none  [shards(): keep = jnp.where(keeps, half, half_other)]
    all_to_all x1, starting transfers between devices: 4.69 us -> 8.37 us  [spread(): lax.all_to_all(jnp.broadcast_to(x[None], (size,) + x.shape), axes, 0, 0,...]
  transfers between devices with their start and end apart: 18 -> 18, of which waited for: 8 -> 9; matrix products, arithmetic and copies ran while one was open for 9% -> 8% of each run, Pallas kernels for 13% -> 17%
where the time goes in v7:
time: 227 us; the launch traced here: 224 us
  waiting for transfers between devices  58.1 us (26%)
  blocking collectives  46.2 us (20%)
  Pallas kernels  44 us (19%)
  starting transfers between devices  27.6 us (12%)
  local copies, waits for them, and re-layouts  18.5 us (8%)
  between operations  14.5 us (6%)
  other arithmetic  9.13 us (4%)
  matrix products  6.26 us (3%)
    pallas_call x6, Pallas kernels, project(): pl.pallas_call(functools.partial(project_kernel, pieces=len(pieces), seed...  29.9 us
    all_to_all x1, blocking collectives, shards(): lax.all_to_all(part.reshape(16, batch // 16, HALF), plane, 0, 0, tiled=True)  20.3 us
    all_gather x1, waiting for transfers between devices, shards(): in_z = lax.all_gather(moved, 'z', axis=0, tiled=True)  18.2 us
    all_to_all x1, waiting for transfers between devices, spread(): lax.all_to_all(jnp.broadcast_to(x[None], (size,) + x.shape), axes, 0, 0,...  15.9 us
    all_to_all x1, blocking collectives, spread(): lax.all_to_all(jnp.broadcast_to(x[None], (size,) + x.shape), axes, 0, 0,...  14.2 us
    ppermute x1, waiting for transfers between devices, shards(): half_other = lax.ppermute(half, RING_X, facing)  11.7 us
    all_to_all x1, blocking collectives, shards(): lax.all_to_all(head_terms.astype(bf16).reshape(8, share, -1), ('xh', 'xl'...  11.6 us
    ppermute x5, starting transfers between devices, to_group(): lax.ppermute(block, ('y', 'xh', 'xl', 'c'), [(8 * v + 4 * h + 2 * l + k,...  11.5 us
  transfers between devices with their start and end apart: 18, of which 9 were waited for; matrix products, arithmetic and copies ran while one was open for 8% of the time, Pallas kernels for 17%

profile of v7, /device:TPU:2, one launch (start us, length us, event | category | flops | bytes accessed | tf_op | source)
XLA Modules:
  0.0 224.1 jit_solution(1166886335649841591)
XLA Ops:
  9.0 3.4 %collective-permute-start = (bf16[56,1280]{1,0:T(8,128)(2,1)S(1)}, bf16[56,1280]{1,0:T(8,128)(2,1)S(1)}, u32[]{:S(2)}, u32[]{:S(2)}) collective-permute-start(bf16[56,1280]{1,0:T(8,128)(2,1)S(1)} %pad_maximum_fusion), channel_id=1, source_target_pairs={{0,0},{1,2},{2,4},{3,6},{4,1},{5,3},{6,5},{7,7},{8,8},{9,10},{10,1... | collective-permute-start | bytes 430088 | tf_op jit(solution)/shard_map/ppermute | solution.py:411
  15.2 3.7 %norm.1.refs_0_.refs_1_ = bf16[4,448,512]{2,1,0:T(8,128)(2,1)S(1)} custom-call(s32[1]{0:T(128)} %bitcast.core_ref, bf16[512,3584]{1,0:T(8,128)(2,1)S(1)} %copy-done.3, f32[1,3584]{1,0:T(1,128)S(1)} %reshape.134.gain_ref), custom_call_target="tpu_custom_call" | custom-call | flops 7340032 | bytes 5505024 | tf_op jit(solution)/shard_map/norm/pallas_call | solution.py:63
  22.8 4.2 %collective-permute-start.10 = (bf16[56,896]{1,0:T(8,128)(2,1)S(1)}, bf16[56,896]{1,0:T(8,128)(2,1)S(1)}, u32[]{:S(2)}, u32[]{:S(2)}) collective-permute-start(bf16[56,896]{1,0:T(8,128)(2,1)S(1)} %copy-done.11), channel_id=1, source_target_pairs={{0,24},{1,26},{2,28},{3,30},{4,25},{5,27},{6,29},{7,31},{8,0},{9,2... | collective-permute-start | bytes 301064 | tf_op jit(solution)/shard_map/ppermute | solution.py:411
  29.6 4.7 %collective-permute-done.11 = bf16[56,896]{1,0:T(8,128)(2,1)S(1)} collective-permute-done((bf16[56,896]{1,0:T(8,128)(2,1)S(1)}, bf16[56,896]{1,0:T(8,128)(2,1)S(1)}, u32[]{:S(2)}, u32[]{:S(2)}) %collective-permute-start.11) | collective-permute-done | bytes 100384 | tf_op jit(solution)/shard_map/ppermute | solution.py:411
  36.9 2.0 collective-permute-start.1
  43.4 18.2 %all-gather.3.cloned.1.call-done = bf16[448,1280]{1,0:T(8,128)(2,1)} async-done(((bf16[56,1280]{1,0:T(8,128)(2,1)}), bf16[448,1280]{1,0:T(8,128)(2,1)}) %all-gather.3.cloned.1.call-update) | async-done | bytes 1146896 | tf_op jit(solution)/shard_map/all_gather | solution.py:429
  61.6 2.3 %slice.16.refs_2_ = bf16[448,1152]{1,0:T(8,128)(2,1)} slice(bf16[448,1280]{1,0:T(8,128)(2,1)} %all-gather.3.cloned.1.call-done), slice={[0:448], [0:1152]} | slice | bytes 2064384 | tf_op jit(solution)/shard_map/slice | solution.py:485
  63.9 2.7 %collective-permute-start.2 = (bf16[448,1152]{1,0:T(8,128)(2,1)}, bf16[448,1152]{1,0:T(8,128)(2,1)}, u32[]{:S(2)}, u32[]{:S(2)}) collective-permute-start(bf16[448,1152]{1,0:T(8,128)(2,1)} %slice.16.refs_2_), channel_id=1, source_target_pairs={{0,24},{8,0},{16,8},{24,16},{1,25},{9,1},{17,9},{25,17},{2,26},{10... | collective-permute-start | bytes 3096584 | tf_op jit(solution)/shard_map/ppermute | solution.py:237
  68.9 11.7 %collective-permute-done.4.refs_1_.refs_2_.refs_3_ = bf16[4,448,512]{2,1,0:T(8,128)(2,1)} collective-permute-done((bf16[4,448,512]{2,1,0:T(8,128)(2,1)}, bf16[4,448,512]{2,1,0:T(8,128)(2,1)}, u32[]{:S(2)}, u32[]{:S(2)}) %collective-permute-start.4) | collective-permute-done | bytes 1835040 | tf_op jit(solution)/shard_map/ppermute | solution.py:433
  80.7 4.3 %project.7.refs_6_ = f32[512,1152]{1,0:T(8,128)} custom-call(s32[2]{0:T(128)} %get-tuple-element.74.place_ref, bf16[4,448,512]{2,1,0:T(8,128)(2,1)} %copy-done.1, bf16[4,448,512]{2,1,0:T(8,128)(2,1)} %collective-permute-done.4.refs_1_.refs_2_.refs_3_, bf16[448,1152]{1,0:T(8,128)(2,1)} %slice.16.refs_2_), custom_call_target="tpu_custom_call" | custom-call | flops 528482304 | bytes 5029888 | tf_op jit(solution)/shard_map/project/pallas_call | solution.py:112
  85.0 4.3 %project.6.refs_6_ = f32[512,1152]{1,0:T(8,128)} custom-call(s32[2]{0:T(128)} %get-tuple-element.73.place_ref, bf16[4,448,512]{2,1,0:T(8,128)(2,1)} %copy-done.1, bf16[4,448,512]{2,1,0:T(8,128)(2,1)} %collective-permute-done.4.refs_1_.refs_2_.refs_3_, bf16[448,1152]{1,0:T(8,128)(2,1)} %slice.16.refs_2_), custom_call_target="tpu_custom_call" | custom-call | flops 528482304 | bytes 5029888 | tf_op jit(solution)/shard_map/project/pallas_call | solution.py:112
  98.2 6.1 %project.9.refs_6_ = f32[512,1152]{1,0:T(8,128)} custom-call(s32[2]{0:T(128)} %get-tuple-element.74.place_ref, bf16[4,448,512]{2,1,0:T(8,128)(2,1)} %copy-done.1, bf16[4,448,512]{2,1,0:T(8,128)(2,1)} %copy-done.1, bf16[4,448,512]{2,1,0:T(8,128)(2,1)} %collective-permute-done.4.refs_1_.refs_2_.refs_3_, ...), custom_call_target="tpu_custom_call" | custom-call | flops 1056964608 | bytes 6520832 | tf_op jit(solution)/shard_map/project/pallas_call | solution.py:112
  104.3 6.0 %project.8.refs_6_ = f32[512,1152]{1,0:T(8,128)} custom-call(s32[2]{0:T(128)} %get-tuple-element.73.place_ref, bf16[4,448,512]{2,1,0:T(8,128)(2,1)} %copy-done.1, bf16[4,448,512]{2,1,0:T(8,128)(2,1)} %copy-done.1, bf16[4,448,512]{2,1,0:T(8,128)(2,1)} %collective-permute-done.4.refs_1_.refs_2_.refs_3_, ...), custom_call_target="tpu_custom_call" | custom-call | flops 1056964608 | bytes 6520832 | tf_op jit(solution)/shard_map/project/pallas_call | solution.py:112
  111.1 4.5 %project.11 = bf16[512,1152]{1,0:T(8,128)(2,1)} custom-call(s32[2]{0:T(128)} %get-tuple-element.73.place_ref, bf16[4,448,512]{2,1,0:T(8,128)(2,1)} %copy-done.1, bf16[4,448,512]{2,1,0:T(8,128)(2,1)} %copy-done.1, bf16[4,448,512]{2,1,0:T(8,128)(2,1)} %collective-permute-done.4.refs_1_.refs_2_.refs_3_, ...), custom_call_target="tpu_custom_call" | custom-call | flops 528482304 | bytes 5029888 | tf_op jit(solution)/shard_map/project/pallas_call | solution.py:112
  116.5 4.7 %project.10.raw_ref = f32[512,1152]{1,0:T(8,128)} custom-call(s32[2]{0:T(128)} %get-tuple-element.74.place_ref, bf16[4,448,512]{2,1,0:T(8,128)(2,1)} %copy-done.1, bf16[4,448,512]{2,1,0:T(8,128)(2,1)} %copy-done.1, bf16[4,448,512]{2,1,0:T(8,128)(2,1)} %collective-permute-done.4.refs_1_.refs_2_.refs_3_, ...), custom_call_target="tpu_custom_call" | custom-call | flops 528482304 | bytes 5029888 | tf_op jit(solution)/shard_map/project/pallas_call | solution.py:112
  121.2 5.3 %attend.1 = bf16[32,896]{1,0:T(8,128)(2,1)} custom-call(f32[512,1152]{1,0:T(8,128)} %project.10.raw_ref, bf16[512,1152]{1,0:T(8,128)(2,1)} %collective-permute-done.7.add_ref, f32[512,128]{1,0:T(8,128)} %bitcast.44, f32[512,1]{1,0:T(8,128)} %copy.39.live_ref, bf16[56,896]{1,0:T(8,128)(2,1)} %constant.110.clone.member_ref, ...), custom_call_target="tpu_custom_call" | custom-call | flops 234881024 | bytes 4718592 | tf_op jit(solution)/shard_map/attend/pallas_call | solution.py:204
  129.0 3.0 %fusion = bf16[8,8,1792]{2,1,0:T(8,128)(2,1)S(1)} fusion(bf16[1792,896]{1,0:T(8,128)(2,1)} %all-gather.5.cloned.1.call-done, bf16[32,896]{1,0:T(8,128)(2,1)S(1)} %get-tuple-element.70, bf16[32,896]{1,0:T(8,128)(2,1)S(1)} %get-tuple-element.69), kind=kOutput, calls=%fused_computation.1 | convolution fusion | flops 205864960 | bytes 3555328 | tf_op jit(solution)/shard_map/dot_general | solution.py:507
  132.0 11.6 %all_to_all.20 = bf16[8,8,1792]{2,1,0:T(8,128)(2,1)S(1)} all-to-all(bf16[8,8,1792]{2,1,0:T(8,128)(2,1)S(1)} %fusion), channel_id=1, replica_groups=mesh['z'=8,'y'=4,'xh'=2,'xl'=2,'c'=2] {'xh','xl','c'}, dimensions={0} | all-to-all | bytes 458752 | tf_op jit(solution)/shard_map/all_to_all | solution.py:510
  147.9 2.6 %collective-permute-done.13 = f32[128,1920]{1,0:T(8,128)S(1)} collective-permute-done((f32[128,1920]{1,0:T(8,128)S(1)}, f32[128,1920]{1,0:T(8,128)S(1)}, u32[]{:S(2)}, u32[]{:S(2)}) %collective-permute-start.13) | collective-permute-done | bytes 983072 | tf_op jit(solution)/shard_map/ppermute | solution.py:237
  150.6 20.3 %all_to_all.21 = f32[16,8,1920]{2,1,0:T(8,128)} all-to-all(f32[16,8,1920]{2,1,0:T(8,128)S(1)} %add_bitcast_fusion), channel_id=1, replica_groups=mesh['z'=8,'y'=4,'xh'=2,'xl'=2,'c'=2] {'y','xh','xl'}, dimensions={0} | all-to-all | bytes 1966080 | tf_op jit(solution)/shard_map/all_to_all | solution.py:533
  173.0 8.4 %all-to-all-start.2 = ((f32[8,8,1920]{2,1,0:T(8,128)}), f32[8,8,1920]{2,1,0:T(8,128)S(1)}, u32[]{:S(2)}, u32[]{:S(2)}) async-start(f32[8,8,1920]{2,1,0:T(8,128)} %broadcast_in_dim.90), calls=%async_computation.2 | async-start | bytes 983040 | tf_op jit(solution)/shard_map/all_to_all | solution.py:258
  181.4 15.9 %all-to-all-done.2 = f32[8,8,1920]{2,1,0:T(8,128)S(1)} async-done(((f32[8,8,1920]{2,1,0:T(8,128)}), f32[8,8,1920]{2,1,0:T(8,128)S(1)}, u32[]{:S(2)}, u32[]{:S(2)}) %all-to-all-start.2) | async-done | bytes 491552 | tf_op jit(solution)/shard_map/all_to_all | solution.py:258
  197.4 14.2 %all_to_all.22 = bf16[16,8,1920]{2,1,0:T(8,128)(2,1)S(1)} all-to-all(bf16[16,8,1920]{2,1,0:T(8,128)(2,1)S(1)} %broadcast_in_dim.91), channel_id=1, replica_groups=mesh['z'=8,'y'=4,'xh'=2,'xl'=2,'c'=2] {'y','xh','xl'}, dimensions={0} | all-to-all | bytes 983040 | tf_op jit(solution)/shard_map/all_to_all | solution.py:258
  213.5 3.2 %final.1 = (f32[256,3584]{1,0:T(8,128)}, f32[128,3584]{1,0:T(8,128)}, f32[8,128]{1,0:T(8,128)S(1)}) custom-call(s32[1]{0:T(128)} %bitcast.core_ref, bf16[128,1920]{1,0:T(8,128)(2,1)S(1)} %bitcast.40, bf16[128,1920]{1,0:T(8,128)(2,1)S(1)} %collective-permute-done.14.back_ref, bf16[256,128]{1,0:T(8,128)(2,1)S(1)} %fusion.3.slopes_ref, ...), custom_call_target="tpu_custom_call" | custom-call | tf_op jit(solution)/shard_map/final/pallas_call | solution.py:361
  (109 shorter events, 42.2 us)
Async XLA Ops:
  7.2 33.5 %copy-start = (bf16[256,3584]{1,0:T(8,128)(2,1)S(1)}, bf16[256,3584]{1,0:T(8,128)(2,1)}, u32[]{:S(2)}) copy-start(bf16[256,3584]{1,0:T(8,128)(2,1)} %param.23) | copy-start | bytes 5505028
  7.2 54.4 %all-gather.3.cloned.1.call-start = ((), (), s32[]{:S(2)}) async-start(), calls=%async_computation.4 | async-start | bytes 1290240 | tf_op jit(solution)/shard_map/all_gather | solution.py:429
  9.0 11.1 %collective-permute-start = (bf16[56,1280]{1,0:T(8,128)(2,1)S(1)}, bf16[56,1280]{1,0:T(8,128)(2,1)S(1)}, u32[]{:S(2)}, u32[]{:S(2)}) collective-permute-start(bf16[56,1280]{1,0:T(8,128)(2,1)S(1)} %pad_maximum_fusion), channel_id=1, source_target_pairs={{0,0},{1,2},{2,4},{3,6},{4,1},{5,3},{6,5},{7,7},{8,8},{9,10},{10,1... | collective-permute-start | bytes 430088 | tf_op jit(solution)/shard_map/ppermute | solution.py:411
  20.1 16.8 %copy-start.8 = (s32[32,16]{0,1:T(8,128)S(1)}, s32[32,16]{0,1:T(8,128)}, u32[]{:S(2)}) copy-start(s32[32,16]{0,1:T(8,128)} %param.17) | copy-start | bytes 6148
  20.1 18.8 %copy-start.10 = (s32[128,8]{0,1:T(8,128)S(1)}, s32[128,8]{0,1:T(8,128)}, u32[]{:S(2)}) copy-start(s32[128,8]{0,1:T(8,128)} %param.27) | copy-start | bytes 12292
  20.1 18.9 %copy-start.12 = (s32[8]{0:T(128)S(1)}, s32[8]{0:T(128)}, u32[]{:S(2)}) copy-start(s32[8]{0:T(128)} %param.24) | copy-start | bytes 100
  20.1 19.2 %copy-start.13 = (s32[256]{0:T(256)S(1)}, s32[256]{0:T(256)}, u32[]{:S(2)}) copy-start(s32[256]{0:T(256)} %param.25) | copy-start | bytes 3076
  20.1 20.6 %copy-start.4 = (bf16[128,3584]{1,0:T(8,128)(2,1)S(1)}, bf16[128,3584]{1,0:T(8,128)(2,1)}, u32[]{:S(2)}) copy-start(bf16[128,3584]{1,0:T(8,128)(2,1)} %queries_ref.3) | copy-start | bytes 2752516
  20.8 108.2 %all-gather.5.cloned.1.call-start = ((), (), s32[]{:S(2)}) async-start(), calls=%async_computation.5 | async-start | bytes 3612672 | tf_op jit(solution)/shard_map/all_gather | solution.py:431
  20.9 8.2 %collective-permute-start.9 = (bf16[56,896]{1,0:T(8,128)(2,1)S(1)}, bf16[56,896]{1,0:T(8,128)(2,1)S(1)}, u32[]{:S(2)}, u32[]{:S(2)}) collective-permute-start(bf16[56,896]{1,0:T(8,128)(2,1)S(1)} %copy-done.11), channel_id=1, source_target_pairs={{0,0},{1,2},{2,4},{3,6},{4,1},{5,3},{6,5},{7,7},{8,8},{9,10},{10,1... | collective-permute-start | bytes 301064 | tf_op jit(solution)/shard_map/ppermute | solution.py:411
  22.8 6.8 %collective-permute-start.10 = (bf16[56,896]{1,0:T(8,128)(2,1)S(1)}, bf16[56,896]{1,0:T(8,128)(2,1)S(1)}, u32[]{:S(2)}, u32[]{:S(2)}) collective-permute-start(bf16[56,896]{1,0:T(8,128)(2,1)S(1)} %copy-done.11), channel_id=1, source_target_pairs={{0,24},{1,26},{2,28},{3,30},{4,25},{5,27},{6,29},{7,31},{8,0},{9,2... | collective-permute-start | bytes 301064 | tf_op jit(solution)/shard_map/ppermute | solution.py:411
  27.1 7.3 %collective-permute-start.11 = (bf16[56,896]{1,0:T(8,128)(2,1)S(1)}, bf16[56,896]{1,0:T(8,128)(2,1)S(1)}, u32[]{:S(2)}, u32[]{:S(2)}) collective-permute-start(bf16[56,896]{1,0:T(8,128)(2,1)S(1)} %copy-done.11), channel_id=1, source_target_pairs={{0,16},{1,18},{2,20},{3,22},{4,17},{5,19},{6,21},{7,23},{8,24},{9,... | collective-permute-start | bytes 301064 | tf_op jit(solution)/shard_map/ppermute | solution.py:411
  28.6 7.4 %collective-permute-start.12 = (bf16[56,896]{1,0:T(8,128)(2,1)S(1)}, bf16[56,896]{1,0:T(8,128)(2,1)S(1)}, u32[]{:S(2)}, u32[]{:S(2)}) collective-permute-start(bf16[56,896]{1,0:T(8,128)(2,1)S(1)} %copy-done.11), channel_id=1, source_target_pairs={{0,8},{1,10},{2,12},{3,14},{4,9},{5,11},{6,13},{7,15},{8,16},{9,18... | collective-permute-start | bytes 301064 | tf_op jit(solution)/shard_map/ppermute | solution.py:411
  36.9 5.4 %collective-permute-start.1 = (s32[32,16]{0,1:T(8,128)S(1)}, s32[32,16]{0,1:T(8,128)S(1)}, u32[]{:S(2)}, u32[]{:S(2)}) collective-permute-start(s32[32,16]{0,1:T(8,128)S(1)} %copy-done.8), channel_id=1, source_target_pairs={{0,6},{2,4},{4,2},{6,0},{1,7},{3,5},{5,3},{7,1},{8,14},{10,12},{12... | collective-permute-start | bytes 6152 | tf_op jit(solution)/shard_map/ppermute | solution.py:434
  40.0 40.7 %collective-permute-start.4 = (bf16[4,448,512]{2,1,0:T(8,128)(2,1)}, bf16[4,448,512]{2,1,0:T(8,128)(2,1)}, u32[]{:S(2)}, u32[]{:S(2)}) collective-permute-start(bf16[4,448,512]{2,1,0:T(8,128)(2,1)} %copy-done.1), channel_id=1, source_target_pairs={{0,6},{2,4},{4,2},{6,0},{1,7},{3,5},{5,3},{7,1},{8,14},{10,12},{12... | collective-permute-start | bytes 5505032 | tf_op jit(solution)/shard_map/ppermute | solution.py:433
  63.9 25.4 %collective-permute-start.2 = (bf16[448,1152]{1,0:T(8,128)(2,1)}, bf16[448,1152]{1,0:T(8,128)(2,1)}, u32[]{:S(2)}, u32[]{:S(2)}) collective-permute-start(bf16[448,1152]{1,0:T(8,128)(2,1)} %slice.16.refs_2_), channel_id=1, source_target_pairs={{0,24},{8,0},{16,8},{24,16},{1,25},{9,1},{17,9},{25,17},{2,26},{10... | collective-permute-start | bytes 3096584 | tf_op jit(solution)/shard_map/ppermute | solution.py:237
  66.6 22.6 %collective-permute-start.3 = (bf16[448,1152]{1,0:T(8,128)(2,1)}, bf16[448,1152]{1,0:T(8,128)(2,1)}, u32[]{:S(2)}, u32[]{:S(2)}) collective-permute-start(bf16[448,1152]{1,0:T(8,128)(2,1)} %slice.16.refs_2_), channel_id=1, source_target_pairs={{0,8},{8,16},{16,24},{24,0},{1,9},{9,17},{17,25},{25,1},{2,10},{10... | collective-permute-start | bytes 3096584 | tf_op jit(solution)/shard_map/ppermute | solution.py:237
  91.1 19.1 %collective-permute-start.5 = (bf16[224,1152]{1,0:T(8,128)(2,1)}, bf16[224,1152]{1,0:T(8,128)(2,1)S(1)}, u32[]{:S(2)}, u32[]{:S(2)}) collective-permute-start(bf16[224,1152]{1,0:T(8,128)(2,1)} %slice.17), channel_id=1, source_target_pairs={{0,24},{8,0},{16,8},{24,16},{1,25},{9,1},{17,9},{25,17},{2,26},{10... | collective-permute-start | bytes 1548296 | tf_op jit(solution)/shard_map/ppermute | solution.py:237
  93.9 16.4 %collective-permute-start.6 = (bf16[224,1152]{1,0:T(8,128)(2,1)}, bf16[224,1152]{1,0:T(8,128)(2,1)}, u32[]{:S(2)}, u32[]{:S(2)}) collective-permute-start(bf16[224,1152]{1,0:T(8,128)(2,1)} %slice.18), channel_id=1, source_target_pairs={{0,8},{8,16},{16,24},{24,0},{1,9},{9,17},{17,25},{25,1},{2,10},{10... | collective-permute-start | bytes 1548296 | tf_op jit(solution)/shard_map/ppermute | solution.py:237
  115.6 5.6 %collective-permute-start.7 = (bf16[512,1152]{1,0:T(8,128)(2,1)}, bf16[512,1152]{1,0:T(8,128)(2,1)}, u32[]{:S(2)}, u32[]{:S(2)}) collective-permute-start(bf16[512,1152]{1,0:T(8,128)(2,1)} %project.11), channel_id=1, source_target_pairs={{0,1},{1,0},{2,3},{3,2},{4,5},{5,4},{6,7},{7,6},{8,9},{9,8},{10,11... | collective-permute-start | bytes 3538952 | tf_op jit(solution)/shard_map/ppermute | solution.py:237
  126.5 1.6 collective-permute-start.8
  147.8 2.7 %collective-permute-start.13 = (f32[128,1920]{1,0:T(8,128)S(1)}, f32[128,1920]{1,0:T(8,128)S(1)}, u32[]{:S(2)}, u32[]{:S(2)}) collective-permute-start(f32[128,1920]{1,0:T(8,128)S(1)} %get-tuple-element.54), channel_id=1, source_target_pairs={{0,1},{1,0},{2,3},{3,2},{4,5},{5,4},{6,7},{7,6},{8,9},{9,8},{10,11... | collective-permute-start | bytes 2949128 | tf_op jit(solution)/shard_map/ppermute | solution.py:237
  173.0 24.3 %all-to-all-start.2 = ((f32[8,8,1920]{2,1,0:T(8,128)}), f32[8,8,1920]{2,1,0:T(8,128)S(1)}, u32[]{:S(2)}, u32[]{:S(2)}) async-start(f32[8,8,1920]{2,1,0:T(8,128)} %broadcast_in_dim.90), calls=%async_computation.2 | async-start | bytes 983040 | tf_op jit(solution)/shard_map/all_to_all | solution.py:258
  211.7 1.9 collective-permute-start.14
  (8 other events, 14.7 us)
Sparse Core Ops, SparseCore 0:
  20.9 40.6 all-gather.2
  63.4 44.2 all-gather.4

commit v8 on v6

--- a/solution.py
+++ b/solution.py
@@ -108,6 +108,24 @@
     ).astype(out_ref.dtype)
 
 
+def whole_kernel(place_ref, x_ref, w0_ref, w1_ref, w3_ref, w2a_ref, w2b_ref, out_ref):
+    def dot(x, w):
+        return lax.dot_general(
+            x, w, (((0,), (0,)), ((), ())), preferred_element_type=jnp.float32
+        )
+
+    y = place_ref[0]
+    half = w2a_ref.shape[0]
+    far = x_ref[(y + 2) % 4]
+    out_ref[...] = (
+        dot(x_ref[y], w0_ref[...])
+        + dot(x_ref[(y + 1) % 4], w1_ref[...])
+        + dot(x_ref[(y + 3) % 4], w3_ref[...])
+        + dot(far[:half], w2a_ref[...])
+        + dot(far[half:], w2b_ref[...])
+    )
+
+
 def project(y, x, pieces, near=None, dtype=jnp.float32):
     _, depth, tokens = x.shape
     columns = pieces[0].shape[1]
@@ -115,7 +133,7 @@
     fixed = [pl.BlockSpec(w.shape, lambda i, _: (0, 0)) for w in pieces]
     tile = pl.BlockSpec((block, columns), lambda i, _: (i, 0))
     if near is None:
-        kernel, extra = near_kernel, ()
+        kernel, extra = near_kernel if len(pieces) == 3 else whole_kernel, ()
         x_spec = pl.BlockSpec((4, depth, block), lambda i, _: (0, 0, i))
     else:
         kernel, extra = far_kernel, (near,)
@@ -136,7 +154,7 @@
             bytes_accessed=6 * tokens * columns + 2 * used * (tokens + columns),
             transcendentals=0,
         ),
-        name="near" if near is None else "far",
+        name="far" if near is not None else "near" if len(pieces) == 3 else "whole",
     )(y.reshape(1).astype(jnp.int32), x, *extra, *pieces)
 
 
@@ -487,12 +505,14 @@
     up, down = ring_near(own)
     far = ring_far(up, down)
     near = (own, up, down)
-    give_near, keep_near = project(y, give, near), project(y, keep, near)
-    early = (kept_query, sums, states_sum, counted, give_near, keep_near)
+    give_near = project(y, give, near)
+    early = (kept_query, sums, states_sum, counted, give_near)
     far, early = lax.optimization_barrier((far, early))
-    kept_query, sums, states_sum, counted, give_near, keep_near = early
-    taken = shift(project(y, give, far, give_near, bf16), "c", 2, 1)
-    raw = project(y, keep, far, keep_near)
+    kept_query, sums, states_sum, counted, give_near = early
+    given = project(y, give, far, give_near, bf16)
+    given, keep = lax.optimization_barrier((given, keep))
+    taken = shift(given, "c", 2, 1)
+    raw = project(y, keep, (*near, *far))
     pooled = attend_pooled(raw, taken, allowed, live_rows, length)
 
     pooled_other = shift(pooled, "c", 2, 1)

time: 218 us -> 215 us (0.986)
  Pallas kernels: 33.3 us -> 30.4 us
    pallas_call x4 -> x3, Pallas kernels: 18.8 us -> 15.8 us  [project(): pl.pallas_call(kernel, out_shape=jax.ShapeDtypeStruct((tokens, columns),...]
  transfers between devices with their start and end apart: 18 -> 18, of which waited for: 8 -> 9; matrix products, arithmetic and copies ran while one was open for 9% -> 10% of each run, Pallas kernels for 13% -> 12%
where the time goes in v8:
time: 215 us; the launch traced here: 212 us
  waiting for transfers between devices  61.7 us (29%)
  blocking collectives  45.6 us (21%)
  Pallas kernels  30.4 us (14%)
  starting transfers between devices  25.1 us (12%)
  local copies, waits for them, and re-layouts  15.9 us (7%)
  between operations  14.4 us (7%)
  other arithmetic  12.9 us (6%)
  matrix products  6.31 us (3%)
    all_to_all x1, blocking collectives, shards(): lax.all_to_all(part.reshape(16, batch // 16, HALF), plane, 0, 0, tiled=True)  21.8 us
    ppermute x8, waiting for transfers between devices, shift(): return lax.ppermute(x, axis, [(i, (i + by) % size) for i in range(size)])  20.9 us
    all_gather x1, waiting for transfers between devices, shards(): in_z = lax.all_gather(moved, 'z', axis=0, tiled=True)  18.2 us
    pallas_call x3, Pallas kernels, project(): pl.pallas_call(kernel, out_shape=jax.ShapeDtypeStruct((tokens, columns),...  15.8 us
    all_to_all x1, waiting for transfers between devices, spread(): lax.all_to_all(jnp.broadcast_to(x[None], (size,) + x.shape), axes, 0, 0,...  15.7 us
    all_to_all x1, blocking collectives, spread(): lax.all_to_all(jnp.broadcast_to(x[None], (size,) + x.shape), axes, 0, 0,...  13.5 us
    ppermute x5, starting transfers between devices, to_group(): lax.ppermute(block, ('y', 'xh', 'xl', 'c'), [(8 * v + 4 * h + 2 * l + k,...  11.5 us
    all_to_all x1, blocking collectives, shards(): lax.all_to_all(head_terms.astype(bf16).reshape(8, share, -1), ('xh', 'xl'...  10.2 us
  transfers between devices with their start and end apart: 18, of which 9 were waited for; matrix products, arithmetic and copies ran while one was open for 10% of the time, Pallas kernels for 12%

profile of v8, /device:TPU:2, one launch (start us, length us, event | category | flops | bytes accessed | tf_op | source)
XLA Modules:
  0.0 212.2 jit_solution(10609312885083579354)
XLA Ops:
  9.0 3.4 %collective-permute-start = (bf16[56,1280]{1,0:T(8,128)(2,1)S(1)}, bf16[56,1280]{1,0:T(8,128)(2,1)S(1)}, u32[]{:S(2)}, u32[]{:S(2)}) collective-permute-start(bf16[56,1280]{1,0:T(8,128)(2,1)S(1)} %pad_maximum_fusion), channel_id=1, source_target_pairs={{0,0},{1,2},{2,4},{3,6},{4,1},{5,3},{6,5},{7,7},{8,8},{9,10},{10,1... | collective-permute-start | bytes 430088 | tf_op jit(solution)/shard_map/ppermute | solution.py:430
  13.2 2.0 copy-done.2
  15.2 4.1 %norm.1 = bf16[4,448,512]{2,1,0:T(8,128)(2,1)} custom-call(s32[1]{0:T(128)} %bitcast.core_ref, bf16[512,3584]{1,0:T(8,128)(2,1)S(1)} %copy-done.2, f32[1,3584]{1,0:T(1,128)S(1)} %reshape.139.gain_ref), custom_call_target="tpu_custom_call" | custom-call | flops 7340032 | bytes 5505024 | tf_op jit(solution)/shard_map/norm/pallas_call | solution.py:63
  22.1 4.2 %collective-permute-start.10 = (bf16[56,896]{1,0:T(8,128)(2,1)S(1)}, bf16[56,896]{1,0:T(8,128)(2,1)S(1)}, u32[]{:S(2)}, u32[]{:S(2)}) collective-permute-start(bf16[56,896]{1,0:T(8,128)(2,1)S(1)} %copy-done.11), channel_id=1, source_target_pairs={{0,24},{1,26},{2,28},{3,30},{4,25},{5,27},{6,29},{7,31},{8,0},{9,2... | collective-permute-start | bytes 301064 | tf_op jit(solution)/shard_map/ppermute | solution.py:430
  28.9 4.7 %collective-permute-done.11 = bf16[56,896]{1,0:T(8,128)(2,1)S(1)} collective-permute-done((bf16[56,896]{1,0:T(8,128)(2,1)S(1)}, bf16[56,896]{1,0:T(8,128)(2,1)S(1)}, u32[]{:S(2)}, u32[]{:S(2)}) %collective-permute-start.11) | collective-permute-done | bytes 100384 | tf_op jit(solution)/shard_map/ppermute | solution.py:430
  36.1 2.0 collective-permute-start.1
  42.6 18.2 %all-gather.3.cloned.1.call-done = bf16[448,1280]{1,0:T(8,128)(2,1)} async-done(((bf16[56,1280]{1,0:T(8,128)(2,1)}), bf16[448,1280]{1,0:T(8,128)(2,1)}) %all-gather.3.cloned.1.call-update) | async-done | bytes 1146896 | tf_op jit(solution)/shard_map/all_gather | solution.py:448
  60.8 2.3 %slice.16.w0_ref = bf16[448,1152]{1,0:T(8,128)(2,1)} slice(bf16[448,1280]{1,0:T(8,128)(2,1)} %all-gather.3.cloned.1.call-done), slice={[0:448], [0:1152]} | slice | bytes 2064384 | tf_op jit(solution)/shard_map/slice | solution.py:504
  63.1 2.9 %collective-permute-start.2 = (bf16[448,1152]{1,0:T(8,128)(2,1)}, bf16[448,1152]{1,0:T(8,128)(2,1)}, u32[]{:S(2)}, u32[]{:S(2)}) collective-permute-start(bf16[448,1152]{1,0:T(8,128)(2,1)} %slice.16.w0_ref), channel_id=1, source_target_pairs={{0,24},{8,0},{16,8},{24,16},{1,25},{9,1},{17,9},{25,17},{2,26},{10... | collective-permute-start | bytes 3096584 | tf_op jit(solution)/shard_map/ppermute | solution.py:256
  69.5 15.6 %collective-permute-done.2.w1_ref = bf16[448,1152]{1,0:T(8,128)(2,1)} collective-permute-done((bf16[448,1152]{1,0:T(8,128)(2,1)}, bf16[448,1152]{1,0:T(8,128)(2,1)}, u32[]{:S(2)}, u32[]{:S(2)}) %collective-permute-start.2) | collective-permute-done | bytes 1032224 | tf_op jit(solution)/shard_map/ppermute | solution.py:256
  86.2 3.1 %collective-permute-start.3 = (bf16[224,1152]{1,0:T(8,128)(2,1)S(1)}, bf16[224,1152]{1,0:T(8,128)(2,1)S(1)}, u32[]{:S(2)}, u32[]{:S(2)}) collective-permute-start(bf16[224,1152]{1,0:T(8,128)(2,1)S(1)} %slice.20), channel_id=1, source_target_pairs={{0,24},{8,0},{16,8},{24,16},{1,25},{9,1},{17,9},{25,17},{2,26},{10... | collective-permute-start | bytes 1548296 | tf_op jit(solution)/shard_map/ppermute | solution.py:256
  90.4 4.2 %broadcast_select_fusion = (bf16[4,448,512]{2,1,0:T(8,128)(2,1)}, bf16[4,448,512]{2,1,0:T(8,128)(2,1)}) fusion(bf16[4,448,512]{2,1,0:T(8,128)(2,1)} %norm.1, bf16[4,448,512]{2,1,0:T(8,128)(2,1)} %collective-permute-done.6, pred[]{:T(512)S(6)} %eq.66), kind=kLoop, calls=%fused_computation.4 | loop fusion | flops 1835008 | bytes 7340033 | tf_op jit(solution)/shard_map/jit(_where)/select_n | solution.py:495
  96.1 5.6 %near.1.near_ref = f32[512,1152]{1,0:T(8,128)} custom-call(s32[1]{0:T(128)} %bitcast.6.place_ref, bf16[4,448,512]{2,1,0:T(8,128)(2,1)} %get-tuple-element.62.x_ref, bf16[448,1152]{1,0:T(8,128)(2,1)} %slice.16.w0_ref, bf16[448,1152]{1,0:T(8,128)(2,1)} %collective-permute-done.2.w1_ref, bf16[448,1152]{1,0:T(8,128)(2,1)} %collective-permute-done.4.w3_ref), custom_call_target="tpu_custom_call" | custom-call | flops 1585446912 | bytes 8011776 | tf_op jit(solution)/shard_map/near/pallas_call | solution.py:142
  102.7 3.6 %far.1 = bf16[512,1152]{1,0:T(8,128)(2,1)} custom-call(s32[1]{0:T(128)} %bitcast.6.place_ref, bf16[4,448,512]{2,1,0:T(8,128)(2,1)} %get-tuple-element.62.x_ref, f32[512,1152]{1,0:T(8,128)} %near.1.near_ref, bf16[224,1152]{1,0:T(8,128)(2,1)} %copy-done.4, bf16[224,1152]{1,0:T(8,128)(2,1)} %copy-done.5), custom_call_target="tpu_custom_call" | custom-call | flops 528482304 | bytes 5029888 | tf_op jit(solution)/shard_map/far/pallas_call | solution.py:142
  107.2 6.6 %whole.1.raw_ref = f32[512,1152]{1,0:T(8,128)} custom-call(s32[1]{0:T(128)} %bitcast.6.place_ref, bf16[4,448,512]{2,1,0:T(8,128)(2,1)} %get-tuple-element.38.x_ref, bf16[448,1152]{1,0:T(8,128)(2,1)} %slice.16.w0_ref, bf16[448,1152]{1,0:T(8,128)(2,1)} %collective-permute-done.2.w1_ref, bf16[448,1152]{1,0:T(8,128)(2,1)} %collective-permute-done.4.w3_ref, ...), custom_call_target="tpu_custom_call" | custom-call | flops 2113929216 | bytes 9502720 | tf_op jit(solution)/shard_map/whole/pallas_call | solution.py:142
  113.8 5.3 %attend.1 = bf16[32,896]{1,0:T(8,128)(2,1)} custom-call(f32[512,1152]{1,0:T(8,128)} %whole.1.raw_ref, bf16[512,1152]{1,0:T(8,128)(2,1)} %collective-permute-done.7.add_ref, f32[512,128]{1,0:T(8,128)} %bitcast.42, f32[512,1]{1,0:T(8,128)} %copy.39.live_ref, bf16[56,896]{1,0:T(8,128)(2,1)} %constant.110.clone.member_ref, f32[128,128]{1,0:T(8,128)} %constant.111.clone.cos_ref, ...), custom_call_target="tpu_custom_call" | custom-call | flops 234881024 | bytes 4718592 | tf_op jit(solution)/shard_map/attend/pallas_call | solution.py:223
  121.6 3.0 %fusion = bf16[8,8,1792]{2,1,0:T(8,128)(2,1)S(1)} fusion(bf16[1792,896]{1,0:T(8,128)(2,1)} %all-gather.5.cloned.1.call-done, bf16[32,896]{1,0:T(8,128)(2,1)S(1)} %get-tuple-element.66, bf16[32,896]{1,0:T(8,128)(2,1)S(1)} %get-tuple-element.65), kind=kOutput, calls=%fused_computation.1 | convolution fusion | flops 205864960 | bytes 3555328 | tf_op jit(solution)/shard_map/dot_general | solution.py:523
  124.6 10.2 %all_to_all.20 = bf16[8,8,1792]{2,1,0:T(8,128)(2,1)S(1)} all-to-all(bf16[8,8,1792]{2,1,0:T(8,128)(2,1)S(1)} %fusion), channel_id=1, replica_groups=mesh['z'=8,'y'=4,'xh'=2,'xl'=2,'c'=2] {'xh','xl','c'}, dimensions={0} | all-to-all | bytes 458752 | tf_op jit(solution)/shard_map/all_to_all | solution.py:526
  139.2 2.6 %collective-permute-done.13 = f32[128,1920]{1,0:T(8,128)S(1)} collective-permute-done((f32[128,1920]{1,0:T(8,128)S(1)}, f32[128,1920]{1,0:T(8,128)S(1)}, u32[]{:S(2)}, u32[]{:S(2)}) %collective-permute-start.13) | collective-permute-done | bytes 983072 | tf_op jit(solution)/shard_map/ppermute | solution.py:256
  141.8 21.8 %all_to_all.21 = f32[16,8,1920]{2,1,0:T(8,128)} all-to-all(f32[16,8,1920]{2,1,0:T(8,128)S(1)} %add_bitcast_fusion), channel_id=1, replica_groups=mesh['z'=8,'y'=4,'xh'=2,'xl'=2,'c'=2] {'y','xh','xl'}, dimensions={0} | all-to-all | bytes 1966080 | tf_op jit(solution)/shard_map/all_to_all | solution.py:549
  165.7 4.7 %all-to-all-start.2 = ((f32[8,8,1920]{2,1,0:T(8,128)}), f32[8,8,1920]{2,1,0:T(8,128)S(1)}, u32[]{:S(2)}, u32[]{:S(2)}) async-start(f32[8,8,1920]{2,1,0:T(8,128)} %broadcast_in_dim.90), calls=%async_computation.2 | async-start | bytes 983040 | tf_op jit(solution)/shard_map/all_to_all | solution.py:277
  170.4 15.7 %all-to-all-done.2 = f32[8,8,1920]{2,1,0:T(8,128)S(1)} async-done(((f32[8,8,1920]{2,1,0:T(8,128)}), f32[8,8,1920]{2,1,0:T(8,128)S(1)}, u32[]{:S(2)}, u32[]{:S(2)}) %all-to-all-start.2) | async-done | bytes 491552 | tf_op jit(solution)/shard_map/all_to_all | solution.py:277
  186.2 13.5 %all_to_all.22 = bf16[16,8,1920]{2,1,0:T(8,128)(2,1)S(1)} all-to-all(bf16[16,8,1920]{2,1,0:T(8,128)(2,1)S(1)} %broadcast_in_dim.91), channel_id=1, replica_groups=mesh['z'=8,'y'=4,'xh'=2,'xl'=2,'c'=2] {'y','xh','xl'}, dimensions={0} | all-to-all | bytes 983040 | tf_op jit(solution)/shard_map/all_to_all | solution.py:277
  201.6 3.2 %final.1 = (f32[256,3584]{1,0:T(8,128)}, f32[128,3584]{1,0:T(8,128)}, f32[8,128]{1,0:T(8,128)S(1)}) custom-call(s32[1]{0:T(128)} %bitcast.core_ref, bf16[128,1920]{1,0:T(8,128)(2,1)S(1)} %bitcast.38, bf16[128,1920]{1,0:T(8,128)(2,1)S(1)} %collective-permute-done.14.back_ref, bf16[256,128]{1,0:T(8,128)(2,1)S(1)} %fusion.3.slopes_ref, ...), custom_call_target="tpu_custom_call" | custom-call | tf_op jit(solution)/shard_map/final/pallas_call | solution.py:380
  (106 shorter events, 35.1 us)
Async XLA Ops:
  7.2 32.4 %copy-start = (bf16[256,3584]{1,0:T(8,128)(2,1)S(1)}, bf16[256,3584]{1,0:T(8,128)(2,1)}, u32[]{:S(2)}) copy-start(bf16[256,3584]{1,0:T(8,128)(2,1)} %param.23) | copy-start | bytes 5505028
  7.2 53.6 %all-gather.3.cloned.1.call-start = ((), (), s32[]{:S(2)}) async-start(), calls=%async_computation.4 | async-start | bytes 1290240 | tf_op jit(solution)/shard_map/all_gather | solution.py:448
  9.0 10.3 %collective-permute-start = (bf16[56,1280]{1,0:T(8,128)(2,1)S(1)}, bf16[56,1280]{1,0:T(8,128)(2,1)S(1)}, u32[]{:S(2)}, u32[]{:S(2)}) collective-permute-start(bf16[56,1280]{1,0:T(8,128)(2,1)S(1)} %pad_maximum_fusion), channel_id=1, source_target_pairs={{0,0},{1,2},{2,4},{3,6},{4,1},{5,3},{6,5},{7,7},{8,8},{9,10},{10,1... | collective-permute-start | bytes 430088 | tf_op jit(solution)/shard_map/ppermute | solution.py:430
  19.3 16.8 %copy-start.8 = (s32[32,16]{0,1:T(8,128)S(1)}, s32[32,16]{0,1:T(8,128)}, u32[]{:S(2)}) copy-start(s32[32,16]{0,1:T(8,128)} %param.17) | copy-start | bytes 6148
  19.3 18.9 %copy-start.10 = (s32[128,8]{0,1:T(8,128)S(1)}, s32[128,8]{0,1:T(8,128)}, u32[]{:S(2)}) copy-start(s32[128,8]{0,1:T(8,128)} %param.27) | copy-start | bytes 12292
  19.3 19.5 %copy-start.12 = (s32[8]{0:T(128)S(1)}, s32[8]{0:T(128)}, u32[]{:S(2)}) copy-start(s32[8]{0:T(128)} %param.24) | copy-start | bytes 100
  19.3 19.5 %copy-start.13 = (s32[256]{0:T(256)S(1)}, s32[256]{0:T(256)}, u32[]{:S(2)}) copy-start(s32[256]{0:T(256)} %param.25) | copy-start | bytes 3076
  19.3 20.3 %copy-start.3 = (bf16[128,3584]{1,0:T(8,128)(2,1)S(1)}, bf16[128,3584]{1,0:T(8,128)(2,1)}, u32[]{:S(2)}) copy-start(bf16[128,3584]{1,0:T(8,128)(2,1)} %queries_ref.3) | copy-start | bytes 2752516
  20.0 101.6 %all-gather.5.cloned.1.call-start = ((), (), s32[]{:S(2)}) async-start(), calls=%async_computation.5 | async-start | bytes 3612672 | tf_op jit(solution)/shard_map/all_gather | solution.py:450
  20.1 8.2 %collective-permute-start.9 = (bf16[56,896]{1,0:T(8,128)(2,1)S(1)}, bf16[56,896]{1,0:T(8,128)(2,1)S(1)}, u32[]{:S(2)}, u32[]{:S(2)}) collective-permute-start(bf16[56,896]{1,0:T(8,128)(2,1)S(1)} %copy-done.11), channel_id=1, source_target_pairs={{0,0},{1,2},{2,4},{3,6},{4,1},{5,3},{6,5},{7,7},{8,8},{9,10},{10,1... | collective-permute-start | bytes 301064 | tf_op jit(solution)/shard_map/ppermute | solution.py:430
  22.1 6.8 %collective-permute-start.10 = (bf16[56,896]{1,0:T(8,128)(2,1)S(1)}, bf16[56,896]{1,0:T(8,128)(2,1)S(1)}, u32[]{:S(2)}, u32[]{:S(2)}) collective-permute-start(bf16[56,896]{1,0:T(8,128)(2,1)S(1)} %copy-done.11), channel_id=1, source_target_pairs={{0,24},{1,26},{2,28},{3,30},{4,25},{5,27},{6,29},{7,31},{8,0},{9,2... | collective-permute-start | bytes 301064 | tf_op jit(solution)/shard_map/ppermute | solution.py:430
  26.3 7.3 %collective-permute-start.11 = (bf16[56,896]{1,0:T(8,128)(2,1)S(1)}, bf16[56,896]{1,0:T(8,128)(2,1)S(1)}, u32[]{:S(2)}, u32[]{:S(2)}) collective-permute-start(bf16[56,896]{1,0:T(8,128)(2,1)S(1)} %copy-done.11), channel_id=1, source_target_pairs={{0,16},{1,18},{2,20},{3,22},{4,17},{5,19},{6,21},{7,23},{8,24},{9,... | collective-permute-start | bytes 301064 | tf_op jit(solution)/shard_map/ppermute | solution.py:430
  27.9 7.4 %collective-permute-start.12 = (bf16[56,896]{1,0:T(8,128)(2,1)S(1)}, bf16[56,896]{1,0:T(8,128)(2,1)S(1)}, u32[]{:S(2)}, u32[]{:S(2)}) collective-permute-start(bf16[56,896]{1,0:T(8,128)(2,1)S(1)} %copy-done.11), channel_id=1, source_target_pairs={{0,8},{1,10},{2,12},{3,14},{4,9},{5,11},{6,13},{7,15},{8,16},{9,18... | collective-permute-start | bytes 301064 | tf_op jit(solution)/shard_map/ppermute | solution.py:430
  36.1 5.4 %collective-permute-start.1 = (s32[32,16]{0,1:T(8,128)S(1)}, s32[32,16]{0,1:T(8,128)S(1)}, u32[]{:S(2)}, u32[]{:S(2)}) collective-permute-start(s32[32,16]{0,1:T(8,128)S(1)} %copy-done.8), channel_id=1, source_target_pairs={{0,6},{2,4},{4,2},{6,0},{1,7},{3,5},{5,3},{7,1},{8,14},{10,12},{12... | collective-permute-start | bytes 6152 | tf_op jit(solution)/shard_map/ppermute | solution.py:453
  41.1 49.4 %collective-permute-start.6 = (bf16[4,448,512]{2,1,0:T(8,128)(2,1)}, bf16[4,448,512]{2,1,0:T(8,128)(2,1)}, u32[]{:S(2)}, u32[]{:S(2)}) collective-permute-start(bf16[4,448,512]{2,1,0:T(8,128)(2,1)} %norm.1), channel_id=1, source_target_pairs={{0,6},{2,4},{4,2},{6,0},{1,7},{3,5},{5,3},{7,1},{8,14},{10,12},{12... | collective-permute-start | bytes 5505032 | tf_op jit(solution)/shard_map/ppermute | solution.py:452
  63.1 21.9 %collective-permute-start.2 = (bf16[448,1152]{1,0:T(8,128)(2,1)}, bf16[448,1152]{1,0:T(8,128)(2,1)}, u32[]{:S(2)}, u32[]{:S(2)}) collective-permute-start(bf16[448,1152]{1,0:T(8,128)(2,1)} %slice.16.w0_ref), channel_id=1, source_target_pairs={{0,24},{8,0},{16,8},{24,16},{1,25},{9,1},{17,9},{25,17},{2,26},{10... | collective-permute-start | bytes 3096584 | tf_op jit(solution)/shard_map/ppermute | solution.py:256
  66.0 23.2 %collective-permute-start.4 = (bf16[448,1152]{1,0:T(8,128)(2,1)}, bf16[448,1152]{1,0:T(8,128)(2,1)}, u32[]{:S(2)}, u32[]{:S(2)}) collective-permute-start(bf16[448,1152]{1,0:T(8,128)(2,1)} %slice.16.w0_ref), channel_id=1, source_target_pairs={{0,8},{8,16},{16,24},{24,0},{1,9},{9,17},{17,25},{25,1},{2,10},{10... | collective-permute-start | bytes 3096584 | tf_op jit(solution)/shard_map/ppermute | solution.py:256
  86.2 15.5 %collective-permute-start.3 = (bf16[224,1152]{1,0:T(8,128)(2,1)S(1)}, bf16[224,1152]{1,0:T(8,128)(2,1)S(1)}, u32[]{:S(2)}, u32[]{:S(2)}) collective-permute-start(bf16[224,1152]{1,0:T(8,128)(2,1)S(1)} %slice.20), channel_id=1, source_target_pairs={{0,24},{8,0},{16,8},{24,16},{1,25},{9,1},{17,9},{25,17},{2,26},{10... | collective-permute-start | bytes 1548296 | tf_op jit(solution)/shard_map/ppermute | solution.py:256
  90.3 11.4 %collective-permute-start.5 = (bf16[224,1152]{1,0:T(8,128)(2,1)S(1)}, bf16[224,1152]{1,0:T(8,128)(2,1)S(1)}, u32[]{:S(2)}, u32[]{:S(2)}) collective-permute-start(bf16[224,1152]{1,0:T(8,128)(2,1)S(1)} %slice.21), channel_id=1, source_target_pairs={{0,8},{8,16},{16,24},{24,0},{1,9},{9,17},{17,25},{25,1},{2,10},{10... | collective-permute-start | bytes 1548296 | tf_op jit(solution)/shard_map/ppermute | solution.py:256
  106.3 7.5 %collective-permute-start.7 = (bf16[512,1152]{1,0:T(8,128)(2,1)}, bf16[512,1152]{1,0:T(8,128)(2,1)}, u32[]{:S(2)}, u32[]{:S(2)}) collective-permute-start(bf16[512,1152]{1,0:T(8,128)(2,1)} %far.1), channel_id=1, source_target_pairs={{0,1},{1,0},{2,3},{3,2},{4,5},{5,4},{6,7},{7,6},{8,9},{9,8},{10,11... | collective-permute-start | bytes 3538952 | tf_op jit(solution)/shard_map/ppermute | solution.py:256
  119.1 1.6 collective-permute-start.8
  139.1 2.7 %collective-permute-start.13 = (f32[128,1920]{1,0:T(8,128)S(1)}, f32[128,1920]{1,0:T(8,128)S(1)}, u32[]{:S(2)}, u32[]{:S(2)}) collective-permute-start(f32[128,1920]{1,0:T(8,128)S(1)} %get-tuple-element.48), channel_id=1, source_target_pairs={{0,1},{1,0},{2,3},{3,2},{4,5},{5,4},{6,7},{7,6},{8,9},{9,8},{10,11... | collective-permute-start | bytes 2949128 | tf_op jit(solution)/shard_map/ppermute | solution.py:256
  165.7 20.4 %all-to-all-start.2 = ((f32[8,8,1920]{2,1,0:T(8,128)}), f32[8,8,1920]{2,1,0:T(8,128)S(1)}, u32[]{:S(2)}, u32[]{:S(2)}) async-start(f32[8,8,1920]{2,1,0:T(8,128)} %broadcast_in_dim.90), calls=%async_computation.2 | async-start | bytes 983040 | tf_op jit(solution)/shard_map/all_to_all | solution.py:277
  199.7 1.9 collective-permute-start.14
  (8 other events, 14.0 us)
Sparse Core Ops, SparseCore 0:
  20.1 40.6 all-gather.2
  62.6 44.2 all-gather.4

commit v9 on v8

--- a/solution.py
+++ b/solution.py
@@ -219,7 +219,7 @@
     owner = (np.arange(per)[:, None] == np.arange(BLOCK)[None, :] // length).astype(np.float32)
     members = jnp.asarray(np.kron(np.eye(heads), owner), jnp.bfloat16)
     cosine, sine = rotary_tables(length)
-    step = 2 * BLOCK
+    step = 4 * BLOCK
     return pl.pallas_call(
         attend_kernel,
         out_shape=jax.ShapeDtypeStruct((texts, heads * HEAD_WIDTH), jnp.bfloat16),
@@ -233,7 +233,7 @@
             pl.BlockSpec((BLOCK, HEAD_WIDTH), lambda i: (0, 0)),
             pl.BlockSpec((BLOCK, HEAD_WIDTH), lambda i: (0, 0)),
         ],
-        out_specs=pl.BlockSpec((2 * per, heads * HEAD_WIDTH), lambda i: (i, 0)),
+        out_specs=pl.BlockSpec((4 * per, heads * HEAD_WIDTH), lambda i: (i, 0)),
         compiler_params=pltpu.CompilerParams(vmem_limit_bytes=56 << 20),
         cost_estimate=pl.CostEstimate(
             flops=4 * tokens * BLOCK * heads * HEAD_WIDTH,

time: 215 us -> 216 us (level)
  no operation moved by 1% of the time
where the time goes in v9:
time: 216 us; the launch traced here: 213 us
  waiting for transfers between devices  61.7 us (29%)
  blocking collectives  45.6 us (21%)
  Pallas kernels  30.9 us (14%)
  starting transfers between devices  25 us (12%)
  local copies, waits for them, and re-layouts  15.9 us (7%)
  between operations  14.4 us (7%)
  other arithmetic  12.9 us (6%)
  matrix products  6.31 us (3%)
    all_to_all x1, blocking collectives, shards(): lax.all_to_all(part.reshape(16, batch // 16, HALF), plane, 0, 0, tiled=True)  21.8 us
    ppermute x8, waiting for transfers between devices, shift(): return lax.ppermute(x, axis, [(i, (i + by) % size) for i in range(size)])  20.9 us
    all_gather x1, waiting for transfers between devices, shards(): in_z = lax.all_gather(moved, 'z', axis=0, tiled=True)  18.2 us
    pallas_call x3, Pallas kernels, project(): pl.pallas_call(kernel, out_shape=jax.ShapeDtypeStruct((tokens, columns),...  15.8 us
    all_to_all x1, waiting for transfers between devices, spread(): lax.all_to_all(jnp.broadcast_to(x[None], (size,) + x.shape), axes, 0, 0,...  15.7 us
    all_to_all x1, blocking collectives, spread(): lax.all_to_all(jnp.broadcast_to(x[None], (size,) + x.shape), axes, 0, 0,...  13.5 us
    ppermute x5, starting transfers between devices, to_group(): lax.ppermute(block, ('y', 'xh', 'xl', 'c'), [(8 * v + 4 * h + 2 * l + k,...  11.5 us
    all_to_all x1, blocking collectives, shards(): lax.all_to_all(head_terms.astype(bf16).reshape(8, share, -1), ('xh', 'xl'...  10.2 us
  transfers between devices with their start and end apart: 18, of which 9 were waited for; matrix products, arithmetic and copies ran while one was open for 10% of the time, Pallas kernels for 12%

profile of v9, /device:TPU:2, one launch (start us, length us, event | category | flops | bytes accessed | tf_op | source)
XLA Modules:
  0.0 212.7 jit_solution(2359179292228789135)
XLA Ops:
  9.0 3.4 %collective-permute-start = (bf16[56,1280]{1,0:T(8,128)(2,1)S(1)}, bf16[56,1280]{1,0:T(8,128)(2,1)S(1)}, u32[]{:S(2)}, u32[]{:S(2)}) collective-permute-start(bf16[56,1280]{1,0:T(8,128)(2,1)S(1)} %pad_maximum_fusion), channel_id=1, source_target_pairs={{0,0},{1,2},{2,4},{3,6},{4,1},{5,3},{6,5},{7,7},{8,8},{9,10},{10,1... | collective-permute-start | bytes 430088 | tf_op jit(solution)/shard_map/ppermute | solution.py:430
  13.2 2.0 copy-done.2
  15.2 4.1 %norm.1 = bf16[4,448,512]{2,1,0:T(8,128)(2,1)} custom-call(s32[1]{0:T(128)} %bitcast.core_ref, bf16[512,3584]{1,0:T(8,128)(2,1)S(1)} %copy-done.2, f32[1,3584]{1,0:T(1,128)S(1)} %reshape.139.gain_ref), custom_call_target="tpu_custom_call" | custom-call | flops 7340032 | bytes 5505024 | tf_op jit(solution)/shard_map/norm/pallas_call | solution.py:63
  22.1 4.2 %collective-permute-start.10 = (bf16[56,896]{1,0:T(8,128)(2,1)S(1)}, bf16[56,896]{1,0:T(8,128)(2,1)S(1)}, u32[]{:S(2)}, u32[]{:S(2)}) collective-permute-start(bf16[56,896]{1,0:T(8,128)(2,1)S(1)} %copy-done.11), channel_id=1, source_target_pairs={{0,24},{1,26},{2,28},{3,30},{4,25},{5,27},{6,29},{7,31},{8,0},{9,2... | collective-permute-start | bytes 301064 | tf_op jit(solution)/shard_map/ppermute | solution.py:430
  28.9 4.7 %collective-permute-done.11 = bf16[56,896]{1,0:T(8,128)(2,1)S(1)} collective-permute-done((bf16[56,896]{1,0:T(8,128)(2,1)S(1)}, bf16[56,896]{1,0:T(8,128)(2,1)S(1)}, u32[]{:S(2)}, u32[]{:S(2)}) %collective-permute-start.11) | collective-permute-done | bytes 100384 | tf_op jit(solution)/shard_map/ppermute | solution.py:430
  36.1 2.0 collective-permute-start.1
  42.6 18.2 %all-gather.3.cloned.1.call-done = bf16[448,1280]{1,0:T(8,128)(2,1)} async-done(((bf16[56,1280]{1,0:T(8,128)(2,1)}), bf16[448,1280]{1,0:T(8,128)(2,1)}) %all-gather.3.cloned.1.call-update) | async-done | bytes 1146896 | tf_op jit(solution)/shard_map/all_gather | solution.py:448
  60.8 2.3 %slice.16.w0_ref = bf16[448,1152]{1,0:T(8,128)(2,1)} slice(bf16[448,1280]{1,0:T(8,128)(2,1)} %all-gather.3.cloned.1.call-done), slice={[0:448], [0:1152]} | slice | bytes 2064384 | tf_op jit(solution)/shard_map/slice | solution.py:504
  63.1 2.9 %collective-permute-start.2 = (bf16[448,1152]{1,0:T(8,128)(2,1)}, bf16[448,1152]{1,0:T(8,128)(2,1)}, u32[]{:S(2)}, u32[]{:S(2)}) collective-permute-start(bf16[448,1152]{1,0:T(8,128)(2,1)} %slice.16.w0_ref), channel_id=1, source_target_pairs={{0,24},{8,0},{16,8},{24,16},{1,25},{9,1},{17,9},{25,17},{2,26},{10... | collective-permute-start | bytes 3096584 | tf_op jit(solution)/shard_map/ppermute | solution.py:256
  69.5 15.6 %collective-permute-done.2.w1_ref = bf16[448,1152]{1,0:T(8,128)(2,1)} collective-permute-done((bf16[448,1152]{1,0:T(8,128)(2,1)}, bf16[448,1152]{1,0:T(8,128)(2,1)}, u32[]{:S(2)}, u32[]{:S(2)}) %collective-permute-start.2) | collective-permute-done | bytes 1032224 | tf_op jit(solution)/shard_map/ppermute | solution.py:256
  86.2 3.1 %collective-permute-start.3 = (bf16[224,1152]{1,0:T(8,128)(2,1)S(1)}, bf16[224,1152]{1,0:T(8,128)(2,1)S(1)}, u32[]{:S(2)}, u32[]{:S(2)}) collective-permute-start(bf16[224,1152]{1,0:T(8,128)(2,1)S(1)} %slice.20), channel_id=1, source_target_pairs={{0,24},{8,0},{16,8},{24,16},{1,25},{9,1},{17,9},{25,17},{2,26},{10... | collective-permute-start | bytes 1548296 | tf_op jit(solution)/shard_map/ppermute | solution.py:256
  90.4 4.2 %broadcast_select_fusion = (bf16[4,448,512]{2,1,0:T(8,128)(2,1)}, bf16[4,448,512]{2,1,0:T(8,128)(2,1)}) fusion(bf16[4,448,512]{2,1,0:T(8,128)(2,1)} %norm.1, bf16[4,448,512]{2,1,0:T(8,128)(2,1)} %collective-permute-done.6, pred[]{:T(512)S(6)} %eq.66), kind=kLoop, calls=%fused_computation.4 | loop fusion | flops 1835008 | bytes 7340033 | tf_op jit(solution)/shard_map/jit(_where)/select_n | solution.py:495
  96.1 5.6 %near.1.near_ref = f32[512,1152]{1,0:T(8,128)} custom-call(s32[1]{0:T(128)} %bitcast.6.place_ref, bf16[4,448,512]{2,1,0:T(8,128)(2,1)} %get-tuple-element.62.x_ref, bf16[448,1152]{1,0:T(8,128)(2,1)} %slice.16.w0_ref, bf16[448,1152]{1,0:T(8,128)(2,1)} %collective-permute-done.2.w1_ref, bf16[448,1152]{1,0:T(8,128)(2,1)} %collective-permute-done.4.w3_ref), custom_call_target="tpu_custom_call" | custom-call | flops 1585446912 | bytes 8011776 | tf_op jit(solution)/shard_map/near/pallas_call | solution.py:142
  102.7 3.6 %far.1 = bf16[512,1152]{1,0:T(8,128)(2,1)} custom-call(s32[1]{0:T(128)} %bitcast.6.place_ref, bf16[4,448,512]{2,1,0:T(8,128)(2,1)} %get-tuple-element.62.x_ref, f32[512,1152]{1,0:T(8,128)} %near.1.near_ref, bf16[224,1152]{1,0:T(8,128)(2,1)} %copy-done.4, bf16[224,1152]{1,0:T(8,128)(2,1)} %copy-done.5), custom_call_target="tpu_custom_call" | custom-call | flops 528482304 | bytes 5029888 | tf_op jit(solution)/shard_map/far/pallas_call | solution.py:142
  107.2 6.6 %whole.1.raw_ref = f32[512,1152]{1,0:T(8,128)} custom-call(s32[1]{0:T(128)} %bitcast.6.place_ref, bf16[4,448,512]{2,1,0:T(8,128)(2,1)} %get-tuple-element.38.x_ref, bf16[448,1152]{1,0:T(8,128)(2,1)} %slice.16.w0_ref, bf16[448,1152]{1,0:T(8,128)(2,1)} %collective-permute-done.2.w1_ref, bf16[448,1152]{1,0:T(8,128)(2,1)} %collective-permute-done.4.w3_ref, ...), custom_call_target="tpu_custom_call" | custom-call | flops 2113929216 | bytes 9502720 | tf_op jit(solution)/shard_map/whole/pallas_call | solution.py:142
  113.8 5.8 %attend.1 = bf16[32,896]{1,0:T(8,128)(2,1)} custom-call(f32[512,1152]{1,0:T(8,128)} %whole.1.raw_ref, bf16[512,1152]{1,0:T(8,128)(2,1)} %collective-permute-done.7.add_ref, f32[512,128]{1,0:T(8,128)} %bitcast.42, f32[512,1]{1,0:T(8,128)} %copy.39.live_ref, bf16[56,896]{1,0:T(8,128)(2,1)} %constant.110.clone.member_ref, f32[128,128]{1,0:T(8,128)} %constant.111.clone.cos_ref, ...), custom_call_target="tpu_custom_call" | custom-call | flops 234881024 | bytes 4718592 | tf_op jit(solution)/shard_map/attend/pallas_call | solution.py:223
  122.1 3.0 %fusion = bf16[8,8,1792]{2,1,0:T(8,128)(2,1)S(1)} fusion(bf16[1792,896]{1,0:T(8,128)(2,1)} %all-gather.5.cloned.1.call-done, bf16[32,896]{1,0:T(8,128)(2,1)S(1)} %get-tuple-element.66, bf16[32,896]{1,0:T(8,128)(2,1)S(1)} %get-tuple-element.65), kind=kOutput, calls=%fused_computation.1 | convolution fusion | flops 205864960 | bytes 3555328 | tf_op jit(solution)/shard_map/dot_general | solution.py:523
  125.1 10.2 %all_to_all.20 = bf16[8,8,1792]{2,1,0:T(8,128)(2,1)S(1)} all-to-all(bf16[8,8,1792]{2,1,0:T(8,128)(2,1)S(1)} %fusion), channel_id=1, replica_groups=mesh['z'=8,'y'=4,'xh'=2,'xl'=2,'c'=2] {'xh','xl','c'}, dimensions={0} | all-to-all | bytes 458752 | tf_op jit(solution)/shard_map/all_to_all | solution.py:526
  139.7 2.6 %collective-permute-done.13 = f32[128,1920]{1,0:T(8,128)S(1)} collective-permute-done((f32[128,1920]{1,0:T(8,128)S(1)}, f32[128,1920]{1,0:T(8,128)S(1)}, u32[]{:S(2)}, u32[]{:S(2)}) %collective-permute-start.13) | collective-permute-done | bytes 983072 | tf_op jit(solution)/shard_map/ppermute | solution.py:256
  142.3 21.8 %all_to_all.21 = f32[16,8,1920]{2,1,0:T(8,128)} all-to-all(f32[16,8,1920]{2,1,0:T(8,128)S(1)} %add_bitcast_fusion), channel_id=1, replica_groups=mesh['z'=8,'y'=4,'xh'=2,'xl'=2,'c'=2] {'y','xh','xl'}, dimensions={0} | all-to-all | bytes 1966080 | tf_op jit(solution)/shard_map/all_to_all | solution.py:549
  166.2 4.7 %all-to-all-start.2 = ((f32[8,8,1920]{2,1,0:T(8,128)}), f32[8,8,1920]{2,1,0:T(8,128)S(1)}, u32[]{:S(2)}, u32[]{:S(2)}) async-start(f32[8,8,1920]{2,1,0:T(8,128)} %broadcast_in_dim.90), calls=%async_computation.2 | async-start | bytes 983040 | tf_op jit(solution)/shard_map/all_to_all | solution.py:277
  170.9 15.7 %all-to-all-done.2 = f32[8,8,1920]{2,1,0:T(8,128)S(1)} async-done(((f32[8,8,1920]{2,1,0:T(8,128)}), f32[8,8,1920]{2,1,0:T(8,128)S(1)}, u32[]{:S(2)}, u32[]{:S(2)}) %all-to-all-start.2) | async-done | bytes 491552 | tf_op jit(solution)/shard_map/all_to_all | solution.py:277
  186.7 13.5 %all_to_all.22 = bf16[16,8,1920]{2,1,0:T(8,128)(2,1)S(1)} all-to-all(bf16[16,8,1920]{2,1,0:T(8,128)(2,1)S(1)} %broadcast_in_dim.91), channel_id=1, replica_groups=mesh['z'=8,'y'=4,'xh'=2,'xl'=2,'c'=2] {'y','xh','xl'}, dimensions={0} | all-to-all | bytes 983040 | tf_op jit(solution)/shard_map/all_to_all | solution.py:277
  202.1 3.2 %final.1 = (f32[256,3584]{1,0:T(8,128)}, f32[128,3584]{1,0:T(8,128)}, f32[8,128]{1,0:T(8,128)S(1)}) custom-call(s32[1]{0:T(128)} %bitcast.core_ref, bf16[128,1920]{1,0:T(8,128)(2,1)S(1)} %bitcast.38, bf16[128,1920]{1,0:T(8,128)(2,1)S(1)} %collective-permute-done.14.back_ref, bf16[256,128]{1,0:T(8,128)(2,1)S(1)} %fusion.3.slopes_ref, ...), custom_call_target="tpu_custom_call" | custom-call | tf_op jit(solution)/shard_map/final/pallas_call | solution.py:380
  (106 shorter events, 35.1 us)
Async XLA Ops:
  7.2 32.4 %copy-start = (bf16[256,3584]{1,0:T(8,128)(2,1)S(1)}, bf16[256,3584]{1,0:T(8,128)(2,1)}, u32[]{:S(2)}) copy-start(bf16[256,3584]{1,0:T(8,128)(2,1)} %param.23) | copy-start | bytes 5505028
  7.2 53.6 %all-gather.3.cloned.1.call-start = ((), (), s32[]{:S(2)}) async-start(), calls=%async_computation.4 | async-start | bytes 1290240 | tf_op jit(solution)/shard_map/all_gather | solution.py:448
  9.0 10.3 %collective-permute-start = (bf16[56,1280]{1,0:T(8,128)(2,1)S(1)}, bf16[56,1280]{1,0:T(8,128)(2,1)S(1)}, u32[]{:S(2)}, u32[]{:S(2)}) collective-permute-start(bf16[56,1280]{1,0:T(8,128)(2,1)S(1)} %pad_maximum_fusion), channel_id=1, source_target_pairs={{0,0},{1,2},{2,4},{3,6},{4,1},{5,3},{6,5},{7,7},{8,8},{9,10},{10,1... | collective-permute-start | bytes 430088 | tf_op jit(solution)/shard_map/ppermute | solution.py:430
  19.3 16.8 %copy-start.8 = (s32[32,16]{0,1:T(8,128)S(1)}, s32[32,16]{0,1:T(8,128)}, u32[]{:S(2)}) copy-start(s32[32,16]{0,1:T(8,128)} %param.17) | copy-start | bytes 6148
  19.3 18.9 %copy-start.10 = (s32[128,8]{0,1:T(8,128)S(1)}, s32[128,8]{0,1:T(8,128)}, u32[]{:S(2)}) copy-start(s32[128,8]{0,1:T(8,128)} %param.27) | copy-start | bytes 12292
  19.3 19.5 %copy-start.12 = (s32[8]{0:T(128)S(1)}, s32[8]{0:T(128)}, u32[]{:S(2)}) copy-start(s32[8]{0:T(128)} %param.24) | copy-start | bytes 100
  19.3 19.5 %copy-start.13 = (s32[256]{0:T(256)S(1)}, s32[256]{0:T(256)}, u32[]{:S(2)}) copy-start(s32[256]{0:T(256)} %param.25) | copy-start | bytes 3076
  19.3 20.3 %copy-start.3 = (bf16[128,3584]{1,0:T(8,128)(2,1)S(1)}, bf16[128,3584]{1,0:T(8,128)(2,1)}, u32[]{:S(2)}) copy-start(bf16[128,3584]{1,0:T(8,128)(2,1)} %queries_ref.3) | copy-start | bytes 2752516
  20.0 102.1 %all-gather.5.cloned.1.call-start = ((), (), s32[]{:S(2)}) async-start(), calls=%async_computation.5 | async-start | bytes 3612672 | tf_op jit(solution)/shard_map/all_gather | solution.py:450
  20.1 8.2 %collective-permute-start.9 = (bf16[56,896]{1,0:T(8,128)(2,1)S(1)}, bf16[56,896]{1,0:T(8,128)(2,1)S(1)}, u32[]{:S(2)}, u32[]{:S(2)}) collective-permute-start(bf16[56,896]{1,0:T(8,128)(2,1)S(1)} %copy-done.11), channel_id=1, source_target_pairs={{0,0},{1,2},{2,4},{3,6},{4,1},{5,3},{6,5},{7,7},{8,8},{9,10},{10,1... | collective-permute-start | bytes 301064 | tf_op jit(solution)/shard_map/ppermute | solution.py:430
  22.1 6.8 %collective-permute-start.10 = (bf16[56,896]{1,0:T(8,128)(2,1)S(1)}, bf16[56,896]{1,0:T(8,128)(2,1)S(1)}, u32[]{:S(2)}, u32[]{:S(2)}) collective-permute-start(bf16[56,896]{1,0:T(8,128)(2,1)S(1)} %copy-done.11), channel_id=1, source_target_pairs={{0,24},{1,26},{2,28},{3,30},{4,25},{5,27},{6,29},{7,31},{8,0},{9,2... | collective-permute-start | bytes 301064 | tf_op jit(solution)/shard_map/ppermute | solution.py:430
  26.3 7.3 %collective-permute-start.11 = (bf16[56,896]{1,0:T(8,128)(2,1)S(1)}, bf16[56,896]{1,0:T(8,128)(2,1)S(1)}, u32[]{:S(2)}, u32[]{:S(2)}) collective-permute-start(bf16[56,896]{1,0:T(8,128)(2,1)S(1)} %copy-done.11), channel_id=1, source_target_pairs={{0,16},{1,18},{2,20},{3,22},{4,17},{5,19},{6,21},{7,23},{8,24},{9,... | collective-permute-start | bytes 301064 | tf_op jit(solution)/shard_map/ppermute | solution.py:430
  27.9 7.4 %collective-permute-start.12 = (bf16[56,896]{1,0:T(8,128)(2,1)S(1)}, bf16[56,896]{1,0:T(8,128)(2,1)S(1)}, u32[]{:S(2)}, u32[]{:S(2)}) collective-permute-start(bf16[56,896]{1,0:T(8,128)(2,1)S(1)} %copy-done.11), channel_id=1, source_target_pairs={{0,8},{1,10},{2,12},{3,14},{4,9},{5,11},{6,13},{7,15},{8,16},{9,18... | collective-permute-start | bytes 301064 | tf_op jit(solution)/shard_map/ppermute | solution.py:430
  36.1 5.4 %collective-permute-start.1 = (s32[32,16]{0,1:T(8,128)S(1)}, s32[32,16]{0,1:T(8,128)S(1)}, u32[]{:S(2)}, u32[]{:S(2)}) collective-permute-start(s32[32,16]{0,1:T(8,128)S(1)} %copy-done.8), channel_id=1, source_target_pairs={{0,6},{2,4},{4,2},{6,0},{1,7},{3,5},{5,3},{7,1},{8,14},{10,12},{12... | collective-permute-start | bytes 6152 | tf_op jit(solution)/shard_map/ppermute | solution.py:453
  41.1 49.4 %collective-permute-start.6 = (bf16[4,448,512]{2,1,0:T(8,128)(2,1)}, bf16[4,448,512]{2,1,0:T(8,128)(2,1)}, u32[]{:S(2)}, u32[]{:S(2)}) collective-permute-start(bf16[4,448,512]{2,1,0:T(8,128)(2,1)} %norm.1), channel_id=1, source_target_pairs={{0,6},{2,4},{4,2},{6,0},{1,7},{3,5},{5,3},{7,1},{8,14},{10,12},{12... | collective-permute-start | bytes 5505032 | tf_op jit(solution)/shard_map/ppermute | solution.py:452
  63.1 21.9 %collective-permute-start.2 = (bf16[448,1152]{1,0:T(8,128)(2,1)}, bf16[448,1152]{1,0:T(8,128)(2,1)}, u32[]{:S(2)}, u32[]{:S(2)}) collective-permute-start(bf16[448,1152]{1,0:T(8,128)(2,1)} %slice.16.w0_ref), channel_id=1, source_target_pairs={{0,24},{8,0},{16,8},{24,16},{1,25},{9,1},{17,9},{25,17},{2,26},{10... | collective-permute-start | bytes 3096584 | tf_op jit(solution)/shard_map/ppermute | solution.py:256
  66.0 23.2 %collective-permute-start.4 = (bf16[448,1152]{1,0:T(8,128)(2,1)}, bf16[448,1152]{1,0:T(8,128)(2,1)}, u32[]{:S(2)}, u32[]{:S(2)}) collective-permute-start(bf16[448,1152]{1,0:T(8,128)(2,1)} %slice.16.w0_ref), channel_id=1, source_target_pairs={{0,8},{8,16},{16,24},{24,0},{1,9},{9,17},{17,25},{25,1},{2,10},{10... | collective-permute-start | bytes 3096584 | tf_op jit(solution)/shard_map/ppermute | solution.py:256
  86.2 15.5 %collective-permute-start.3 = (bf16[224,1152]{1,0:T(8,128)(2,1)S(1)}, bf16[224,1152]{1,0:T(8,128)(2,1)S(1)}, u32[]{:S(2)}, u32[]{:S(2)}) collective-permute-start(bf16[224,1152]{1,0:T(8,128)(2,1)S(1)} %slice.20), channel_id=1, source_target_pairs={{0,24},{8,0},{16,8},{24,16},{1,25},{9,1},{17,9},{25,17},{2,26},{10... | collective-permute-start | bytes 1548296 | tf_op jit(solution)/shard_map/ppermute | solution.py:256
  90.3 11.4 %collective-permute-start.5 = (bf16[224,1152]{1,0:T(8,128)(2,1)S(1)}, bf16[224,1152]{1,0:T(8,128)(2,1)S(1)}, u32[]{:S(2)}, u32[]{:S(2)}) collective-permute-start(bf16[224,1152]{1,0:T(8,128)(2,1)S(1)} %slice.21), channel_id=1, source_target_pairs={{0,8},{8,16},{16,24},{24,0},{1,9},{9,17},{17,25},{25,1},{2,10},{10... | collective-permute-start | bytes 1548296 | tf_op jit(solution)/shard_map/ppermute | solution.py:256
  106.3 7.5 %collective-permute-start.7 = (bf16[512,1152]{1,0:T(8,128)(2,1)}, bf16[512,1152]{1,0:T(8,128)(2,1)}, u32[]{:S(2)}, u32[]{:S(2)}) collective-permute-start(bf16[512,1152]{1,0:T(8,128)(2,1)} %far.1), channel_id=1, source_target_pairs={{0,1},{1,0},{2,3},{3,2},{4,5},{5,4},{6,7},{7,6},{8,9},{9,8},{10,11... | collective-permute-start | bytes 3538952 | tf_op jit(solution)/shard_map/ppermute | solution.py:256
  119.6 1.6 collective-permute-start.8
  139.6 2.7 %collective-permute-start.13 = (f32[128,1920]{1,0:T(8,128)S(1)}, f32[128,1920]{1,0:T(8,128)S(1)}, u32[]{:S(2)}, u32[]{:S(2)}) collective-permute-start(f32[128,1920]{1,0:T(8,128)S(1)} %get-tuple-element.48), channel_id=1, source_target_pairs={{0,1},{1,0},{2,3},{3,2},{4,5},{5,4},{6,7},{7,6},{8,9},{9,8},{10,11... | collective-permute-start | bytes 2949128 | tf_op jit(solution)/shard_map/ppermute | solution.py:256
  166.2 20.4 %all-to-all-start.2 = ((f32[8,8,1920]{2,1,0:T(8,128)}), f32[8,8,1920]{2,1,0:T(8,128)S(1)}, u32[]{:S(2)}, u32[]{:S(2)}) async-start(f32[8,8,1920]{2,1,0:T(8,128)} %broadcast_in_dim.90), calls=%async_computation.2 | async-start | bytes 983040 | tf_op jit(solution)/shard_map/all_to_all | solution.py:277
  200.2 1.9 collective-permute-start.14
  (8 other events, 14.0 us)
Sparse Core Ops, SparseCore 0:
  20.1 40.6 all-gather.2
  62.6 44.2 all-gather.4
